TPU v7x, 32 devices: a whole 2x2x4 slice. The times are simulated.
32 devices in a mesh: tm: 8 (over z, core), space: 4 (over y, x).
Axes of the slice: x: 2, y: 2, z: 4, core: 2. Of those that a mesh axis runs over, the one named last changes fastest.
Arguments:
- spectrum: float32 [2048], P('space'), may hold values from 4 to 64
- coupling: float32 [64, 2048], P('tm', 'space'), may hold values from 0 to 1, as said below
- spatial_basis: bfloat16 [2048, 2048], P(None, 'space'), may hold values from -0.125 to 0.125
- noise_keys: int32 [64], replicated, may hold values from 0 to 16777215
- noise_counters: int32 [64], replicated, may hold values from 0 to 1048575
Outputs:
- samples: float32 [2048, 4096], P('space', 'tm')
Inputs may be any that keep to these rules, and one draw needn't show every extreme that they name: `coupling`: every entry lies strictly between 0 and 1.
All inputs are finite; a program needn't handle non-finite values.
Results may differ from a plain program's by a relative error of at most 0.015.
Values may be sent and summed in bfloat16 or wider, within the bound.
No kernel may reach another device: no remote copies, remote signals or barrier semaphores. Data moves between devices by JAX's collectives and lax.ppermute only.
A program may use at most 64 MiB of HBM per device.

v0:
```python
import functools

import jax
import jax.numpy as jnp
from jax import lax
from jax.experimental import pallas as pl
from jax.experimental.pallas import tpu as pltpu
from jax.sharding import PartitionSpec as P


F32 = jnp.float32
BF16 = jnp.bfloat16
VMEM = pl.BlockSpec(memory_space=pltpu.VMEM)
ANY = pl.BlockSpec(memory_space=pl.ANY)
HBM = pl.BlockSpec(memory_space=pltpu.HBM)
LIMIT = pltpu.CompilerParams(vmem_limit_bytes=48 << 20)
SINE = (6.28318516, -41.34165503, 81.60100406, -76.54978208, 39.53670436)


def swap(x, axis, offset):
    count = lax.axis_size(axis)
    return lax.ppermute(x, axis, [(i, i ^ offset) for i in range(count)])


def send(x, axis, offset):
    count = lax.axis_size(axis)
    return lax.ppermute(x, axis, [(i, i - offset) for i in range(offset, count)])


def split3(x):
    high = x.astype(BF16).astype(F32)
    rest = x - high
    middle = rest.astype(BF16).astype(F32)
    return high, middle, rest - middle


def mix_bits(state):
    state = state ^ lax.shift_right_logical(state, jnp.int32(16))
    state = state * jnp.int32(-2048144789)
    state = state ^ lax.shift_right_logical(state, jnp.int32(13))
    state = state * jnp.int32(-1028477387)
    return state ^ lax.shift_right_logical(state, jnp.int32(16))


def gaussian(seeded):
    first = mix_bits(seeded)
    second = mix_bits(first + jnp.int32(1013904223))
    unit = (lax.shift_right_logical(first, jnp.int32(8)).astype(F32) + 0.5) * (1.0 / 16777216.0)
    square = -2.0 * jnp.log(unit)
    radius = square * lax.rsqrt(jnp.maximum(square, 1e-30))
    turn = (lax.shift_right_arithmetic(second, jnp.int32(8)).astype(F32) + 0.5) * (1.0 / 16777216.0)
    w = 0.25 - jnp.abs(turn)
    z = w * w
    sine = SINE[4]
    for c in SINE[3::-1]:
        sine = sine * z + c
    return radius * (sine * w)


def pack_kernel(tm_axis, sp_axis, coup, spec, basis, *rest):
    *outs, coup_out, spec_out, sems = rest
    me, sp = lax.axis_index(tm_axis), lax.axis_index(sp_axis)
    core = lax.rem(me, 2)
    rows = outs[0].shape[0] - 32
    small = [
        pltpu.make_async_copy(coup, coup_out, sems.at[len(outs)]),
        pltpu.make_async_copy(spec, spec_out, sems.at[len(outs) + 1]),
    ]
    large = []
    for i, out in enumerate(outs):
        start = pl.multiple_of(((sp ^ (i + 1)) * 2 + core) * rows, rows)
        large.append(
            pltpu.make_async_copy(basis.at[pl.ds(start, rows), :], out.at[pl.ds(0, rows), :], sems.at[i])
        )
    for copy in small + large:
        copy.start()
    for copy in small:
        copy.wait()
    x = coup_out[...]
    parts = split3(x)
    tail = [jnp.concatenate(parts[:2], 0).astype(BF16)]
    row = lax.broadcasted_iota(jnp.int32, x.shape, 0)
    sparts = split3(spec_out[...])
    extra = jnp.zeros_like(x)
    for j in range(3):
        extra = jnp.where(row == j, sparts[j], extra)
    tail.append(jnp.concatenate([parts[2], extra], 0).astype(BF16))
    for out in outs:
        out[pl.ds(rows, 16), :] = tail[0]
        out[pl.ds(rows + 16, 16), :] = tail[1]
    for copy in large:
        copy.wait()


def totals(ref):
    product = square = total = None
    for t in range(ref.shape[0]):
        c = ref[pl.ds(t, 1), :]
        product = c if t == 0 else product * c
        square = c * c if t == 0 else square * (c * c)
        total = square if t == 0 else total + square
    return product, total


def table_kernel(tm_axis, coup, other, out):
    first = lax.rem(lax.axis_index(tm_axis), 2) == 0
    mine, theirs = totals(coup), totals(other)
    row = lax.broadcasted_iota(jnp.int32, out.shape, 0)
    table = jnp.zeros(out.shape, F32)
    for j in range(2):
        table = jnp.where(row == j, jnp.where(first, mine[j], theirs[j]), table)
        table = jnp.where(row == j + 2, jnp.where(first, theirs[j], mine[j]), table)
    out[...] = table


def noise_kernel(tm_axis, sp_axis, blocks, extras, keys, counters, *rest):
    *outs, base = rest[extras:]
    outs = outs[: len(blocks)]
    steps, vecs, modes = outs[0].shape
    me, sp = lax.axis_index(tm_axis), lax.axis_index(sp_axis)
    diagonal = lax.broadcasted_iota(jnp.int32, (vecs, vecs), 0) == lax.broadcasted_iota(
        jnp.int32, (vecs, vecs), 1
    )

    def column(ref):
        row = jnp.broadcast_to(ref[...].astype(F32), (vecs, vecs))
        return jnp.sum(jnp.where(diagonal, row, 0.0), axis=1, keepdims=True).astype(jnp.int32)

    start = column(keys) * jnp.int32(668265261) + column(counters) * jnp.int32(374761393)
    base[...] = jnp.broadcast_to(start, base.shape)
    group = 8
    for out, (block, offset) in zip(outs, blocks):
        ids = (sp ^ offset) * modes + lax.broadcasted_iota(jnp.int32, (1, modes), 1)
        lane = ids * jnp.int32(-1640531535)
        first_step = (me ^ block) * steps

        def step(t, _):
            shifted = lane + (first_step + t) * jnp.int32(374761393)
            for v in range(vecs // group):
                seeded = jnp.tile(base[pl.ds(v * group, group), :], (1, modes // 128)) + shifted
                out[t, pl.ds(v * group, group), :] = gaussian(seeded)
            return 0

        lax.fori_loop(0, steps, step, 0)


def chain(coup, spec, d_start, f_start):
    before, after = [], []
    square, total = None, None
    d_now = d_start
    for t in range(coup.shape[0]):
        c = coup[t : t + 1, :]
        square = c * c if t == 0 else square * (c * c)
        total = square if t == 0 else total + square
        before.append(d_now)
        d_now = d_start + f_start * total
        after.append(d_now)
    ratio = jnp.concatenate(before, 0) / jnp.concatenate(after, 0)
    return jnp.sqrt(ratio / spec), ratio


def offset_kernel(tm_axis, noise_own, noise_other, coup, coup_other, spec, zown, *rest):
    zin = rest[:-10]
    o_ref, base_ref, wts, df, table, *coefs, tmp = rest[len(zin) :]
    steps, vecs, modes = noise_own.shape
    me = lax.axis_index(tm_axis)
    chip = me // 2
    first = lax.rem(me, 2) == 0
    chips = len(zin) + 1
    table[chip] = zown[...]
    for e, ref in enumerate(zin):
        table[chip ^ (e + 1)] = ref[...]
    one = jnp.ones((1, modes), F32)
    d_now, f_now = one, one
    starts = [one] * 4
    gains = [one] * 2
    weight = jnp.zeros((1, modes), F32)
    for b in range(chips):
        wts[b] = jnp.broadcast_to(weight, (8, modes))
        here = chip == b
        gain = one
        for half in range(2):
            product = table[b, pl.ds(2 * half, 1), :]
            total = table[b, pl.ds(2 * half + 1, 1), :]
            starts[2 * half] = jnp.where(here, d_now, starts[2 * half])
            starts[2 * half + 1] = jnp.where(here, f_now, starts[2 * half + 1])
            d_next = d_now + f_now * total
            part = product * d_now / d_next
            gains[half] = jnp.where(here, part, gains[half])
            gain = gain * part
            d_now, f_now = d_next, f_now * (product * product)
        weight = jnp.where(here, 1.0, weight * gain)
    row = lax.broadcasted_iota(jnp.int32, (8, modes), 0)
    mine = [jnp.where(first, starts[j], starts[2 + j]) for j in range(2)]
    theirs = [jnp.where(first, starts[2 + j], starts[j]) for j in range(2)]
    outer = jnp.where(first, gains[1], 1.0)
    df[...] = jnp.where(row == 0, mine[0], jnp.where(row == 1, mine[1], jnp.where(row == 2, outer, 0.0)))
    for j, (ref, sums) in enumerate(((coup, mine), (coup_other, theirs))):
        c = ref[...]
        a, ratio = chain(c, spec[...], *sums)
        coefs[2 * j][...] = c * a
        coefs[2 * j + 1][...] = c * ratio
    tmp[...] = jnp.broadcast_to(gains[0], tmp.shape)

    def tile(v, _):
        at = pl.ds(pl.multiple_of(v * 16, 16), 16)
        ends = []
        for j, noise in enumerate((noise_own, noise_other)):
            alpha, beta = coefs[2 * j], coefs[2 * j + 1]
            carry = jnp.zeros((16, modes), F32)
            for t in range(steps - 1, -1, -1):
                carry = alpha[pl.ds(t, 1), :] * noise[t, at, :] + beta[pl.ds(t, 1), :] * carry
            ends.append(carry)
        early = jnp.where(first, ends[0], ends[1])
        late = jnp.where(first, ends[1], ends[0])
        o_ref[at, :] = (early + tmp[pl.ds(0, 1), :] * late).astype(BF16)
        base_ref[at, :] = jnp.where(first, late, 0.0)
        return 0

    lax.fori_loop(0, vecs // 16, tile, 0)


def carry_kernel(tm_axis, extras, base, wts, df, *rest):
    others, out = rest[: -1 - extras], rest[-1]
    vecs, modes = base.shape
    chip = lax.axis_index(tm_axis) // 2
    last = wts.shape[0] - 1
    total = jnp.zeros(base.shape, F32)
    for e, ref in enumerate(others):
        total = total + wts[jnp.minimum(chip + (e + 1), last)][0:1, :] * ref[...].astype(F32)
    out[pl.ds(0, vecs), :] = (base[...] + df[pl.ds(2, 1), :] * total).astype(BF16)
    row = lax.broadcasted_iota(jnp.int32, (16, modes), 0)
    block = jnp.zeros((16, modes), F32)
    parts = split3(df[pl.ds(0, 1), :]) + split3(df[pl.ds(1, 1), :])
    for j, part in enumerate(parts):
        block = jnp.where(row == j, part, block)
    out[pl.ds(vecs, 16), :] = block.astype(BF16)


def values(noise, message, c, lam, coefs, rhs, column):
    steps, vecs, modes = noise.shape
    df = message[pl.ds(vecs, 16), :].astype(F32)
    a, ratio = chain(c, lam, df[0:1] + df[1:2] + df[2:3], df[3:4] + df[4:5] + df[5:6])
    a_ref, ratio_ref, c_ref = coefs
    a_ref[...] = a
    ratio_ref[...] = ratio
    c_ref[...] = c

    def tile(v, _):
        at = pl.ds(pl.multiple_of(v * 16, 16), 16)
        carry = message[at, :].astype(F32)
        for t in range(steps - 1, -1, -1):
            value = a_ref[pl.ds(t, 1), :] * noise[t, at, :] + ratio_ref[pl.ds(t, 1), :] * carry
            if t:
                carry = c_ref[pl.ds(t, 1), :] * value
            rhs[pl.ds(pl.multiple_of(t * vecs + v * 16, 16), 16), pl.ds(column, modes)] = value.astype(BF16)
        return 0

    lax.fori_loop(0, vecs // 16, tile, 0)


def product(lhs, rhs):
    return lax.dot_general(lhs[...], rhs[...], (((1,), (1,)), ((), ())), preferred_element_type=F32)


def own_kernel(sp_axis, coup, spec, basis, noise, message, out, lhs, rhs, *rest):
    *coefs, sem = rest
    rows = lhs.shape[0]
    start = pl.multiple_of(lax.axis_index(sp_axis) * rows, rows)
    copy = pltpu.make_async_copy(basis.at[pl.ds(start, rows), :], lhs, sem)
    copy.start()
    values(noise, message, coup[...], spec[...], coefs, rhs, 0)
    copy.wait()
    out[...] = product(lhs, rhs)


def final_kernel(tm_axis, count, partial, *rest):
    direct, rest = rest[:count], rest[count:]
    swapped, rest = rest[:count], rest[count:]
    noise, rest = rest[:count], rest[count:]
    messages, rest = rest[:count], rest[count:]
    out, lhs, rhs, tails, *coefs, sems = rest
    _, _, modes = noise[0].shape
    core = lax.rem(lax.axis_index(tm_axis), 2)
    rows = lhs.shape[0] // 2
    here = pl.ds(pl.multiple_of(core * rows, rows), rows)
    there = pl.ds(pl.multiple_of((1 - core) * rows, rows), rows)
    copies, heads = [], []
    for d in range(count):
        at = pl.ds(d * modes, modes)
        for j, (source, place) in enumerate(((direct[d], here), (swapped[d], there))):
            copies.append(
                pltpu.make_async_copy(source.at[pl.ds(0, rows), :], lhs.at[place, at], sems.at[3 * d + j])
            )
        heads.append(
            pltpu.make_async_copy(direct[d].at[pl.ds(rows, 32), :], tails.at[d], sems.at[3 * d + 2])
        )
    for copy in heads + copies:
        copy.start()
    for copy in heads:
        copy.wait()
    for d in range(count):
        upper = tails[d, pl.ds(0, 16), :].astype(F32)
        lower = tails[d, pl.ds(16, 16), :].astype(F32)
        c = upper[0:8] + upper[8:16] + lower[0:8]
        values(noise[d], messages[d], c, lower[8:9] + lower[9:10] + lower[10:11], coefs, rhs, d * modes)
    for copy in copies:
        copy.wait()
    out[...] = partial[...] + product(lhs, rhs)


def kernel_call(body, **options):
    return pl.pallas_call(body, **options)


def local(spectrum, coupling, spatial_basis, noise_keys, noise_counters):
    steps, modes = coupling.shape
    vecs = noise_keys.shape[0]
    tm, space = lax.axis_size("tm"), lax.axis_size("space")
    chips = tm // 2
    nodes_here = spatial_basis.shape[0] // space
    half = nodes_here // 2
    keys, counters = noise_keys.reshape(1, vecs), noise_counters.reshape(1, vecs)
    row_block = jax.ShapeDtypeStruct((steps, modes), F32)
    noise_block = jax.ShapeDtypeStruct((steps, vecs, modes), F32)
    coef_scratch = [pltpu.VMEM((steps, modes), F32)] * 3

    other = swap(coupling, "tm", 1)
    *messages, coup, spec = kernel_call(
        functools.partial(pack_kernel, "tm", "space"),
        out_shape=[jax.ShapeDtypeStruct((half + 32, modes), BF16)] * (space - 1)
        + [row_block, jax.ShapeDtypeStruct((1, modes), F32)],
        in_specs=[HBM] * 3,
        out_specs=[VMEM] * (space + 1),
        scratch_shapes=[pltpu.SemaphoreType.DMA((space + 1,))],
        compiler_params=LIMIT,
    )(*(pltpu.with_memory_space_constraint(x, pltpu.HBM) for x in (coupling, spectrum.reshape(1, modes), spatial_basis)))
    direct = [swap(m, "space", d + 1) for d, m in enumerate(messages)]
    table = kernel_call(
        functools.partial(table_kernel, "tm"),
        out_shape=row_block,
        in_specs=[VMEM] * 2,
        out_specs=VMEM,
        compiler_params=LIMIT,
    )(coup, other)
    zin = [swap(table, "tm", 2 * e) for e in range(1, chips)]

    def noise_of(blocks, after=(), through=()):
        count = len(blocks) * steps * vecs * modes
        extras = len(after) + len(through)
        return kernel_call(
            functools.partial(noise_kernel, "tm", "space", blocks, extras),
            out_shape=[noise_block] * len(blocks) + [jax.ShapeDtypeStruct(x.shape, x.dtype) for x in through],
            in_specs=[VMEM] * 2 + [ANY] * extras,
            out_specs=[VMEM] * len(blocks) + [ANY] * len(through),
            scratch_shapes=[pltpu.VMEM((vecs, 128), jnp.int32)],
            input_output_aliases={2 + len(after) + i: len(blocks) + i for i in range(len(through))},
            compiler_params=LIMIT,
            cost_estimate=pl.CostEstimate(flops=count * 60, transcendentals=count * 2, bytes_accessed=count * 4),
        )(keys, counters, *after, *through)

    own, paired = noise_of(((0, 0), (1, 0)))
    offset, base, weights, sums = kernel_call(
        functools.partial(offset_kernel, "tm"),
        out_shape=[
            jax.ShapeDtypeStruct((vecs, modes), BF16),
            jax.ShapeDtypeStruct((vecs, modes), F32),
            jax.ShapeDtypeStruct((chips, 8, modes), F32),
            jax.ShapeDtypeStruct((8, modes), F32),
        ],
        in_specs=[VMEM] * (6 + len(zin)),
        out_specs=[VMEM] * 4,
        scratch_shapes=[pltpu.VMEM((chips, 8, modes), F32)] + [pltpu.VMEM((steps, modes), F32)] * 5,
        compiler_params=LIMIT,
    )(own, paired, coup, other, spec, table, *zin)
    later = [send(offset, "tm", 2 * e) for e in range(1, chips)]
    middle = max(1, (space - 1) // 3)
    offsets = list(range(1, space))
    one, two, three = offsets[:middle], offsets[middle : 2 * middle], offsets[2 * middle :]
    noise = list(noise_of([(0, d) for d in one], after=(offset,)))
    if two:
        out = noise_of([(0, d) for d in two], after=(noise[-1],), through=direct)
        noise += out[: len(two)]
        direct = out[len(two) :]
    swapped = [swap(m, "tm", 1) for m in direct]
    carry = kernel_call(
        functools.partial(carry_kernel, "tm", 1),
        out_shape=jax.ShapeDtypeStruct((vecs + 16, modes), BF16),
        in_specs=[VMEM] * (3 + len(later)) + [ANY],
        out_specs=VMEM,
        compiler_params=LIMIT,
    )(base, weights, sums, *later, noise[-1])
    carries = [swap(carry, "space", d) for d in range(1, space)]
    if three:
        noise += noise_of([(0, d) for d in three], after=(carry,))
    flops = 2 * nodes_here * modes * steps * vecs
    partial = kernel_call(
        functools.partial(own_kernel, "space"),
        out_shape=jax.ShapeDtypeStruct((nodes_here, steps * vecs), F32),
        in_specs=[VMEM, VMEM, HBM, VMEM, VMEM],
        out_specs=VMEM,
        scratch_shapes=[pltpu.VMEM((nodes_here, modes), BF16), pltpu.VMEM((steps * vecs, modes), BF16)]
        + coef_scratch
        + [pltpu.SemaphoreType.DMA],
        compiler_params=LIMIT,
        cost_estimate=pl.CostEstimate(flops=flops, transcendentals=0, bytes_accessed=4 * steps * vecs * modes),
    )(coup, spec, spatial_basis, own, carry)
    return kernel_call(
        functools.partial(final_kernel, "tm", space - 1),
        out_shape=jax.ShapeDtypeStruct((nodes_here, steps * vecs), F32),
        in_specs=[VMEM] + [ANY] * (2 * (space - 1)) + [VMEM] * (2 * (space - 1)),
        out_specs=VMEM,
        scratch_shapes=[
            pltpu.VMEM((nodes_here, (space - 1) * modes), BF16),
            pltpu.VMEM((steps * vecs, (space - 1) * modes), BF16),
            pltpu.VMEM((space - 1, 32, modes), BF16),
        ]
        + coef_scratch
        + [pltpu.SemaphoreType.DMA((3 * (space - 1),))],
        compiler_params=LIMIT,
        cost_estimate=pl.CostEstimate(
            flops=flops * (space - 1), transcendentals=0, bytes_accessed=4 * steps * vecs * modes * space
        ),
    )(partial, *direct, *swapped, *noise, *carries)


def solution(mesh):
    in_specs = (P("space"), P("tm", "space"), P(None, "space"), P(), P())
    out_specs = P("space", "tm")
    return jax.shard_map(local, mesh=mesh, in_specs=in_specs, out_specs=out_specs, check_vma=False)
```

profile of v0, /device:TPU:0, one launch (start us, length us, event | category | flops | bytes accessed | tf_op | source)
XLA Modules:
  0.0 45.0 jit_solution(8582301371174627512)
XLA Ops:
  0.0 1.2 %shard_map.55 = (bf16[288,512]{1,0:T(8,128)(2,1)S(1)}, bf16[288,512]{1,0:T(8,128)(2,1)S(1)}, bf16[288,512]{1,0:T(8,128)(2,1)S(1)}, f32[8,512]{1,0:T(8,128)S(1)}, f32[1,512]{1,0:T(1,128)S(1)}) custom-call(f32[8,512]{1,0:T(8,128)} %coup.1, f32[1,512]{1,0:T(1,128)} %bitcast.11, bf16[2048,512]{1,0:T(8,128)(2,1)} %basis.3), custom_call_target="tpu_custom_call" | custom-call | tf_op jit(solution)/shard_map/pallas_call | solution.py:329
  1.2 3.0 %collective-permute-start.7 = (bf16[288,512]{1,0:T(8,128)(2,1)S(1)}, bf16[288,512]{1,0:T(8,128)(2,1)S(1)}, u32[]{:S(2)}, u32[]{:S(2)}) collective-permute-start(bf16[288,512]{1,0:T(8,128)(2,1)S(1)} %get-tuple-element.28), channel_id=1, source_target_pairs={{0,1},{1,0},{2,3},{3,2},{4,5},{5,4},{6,7},{7,6},{8,9},{9,8},{10,11... | collective-permute-start | bytes 884744 | tf_op jit(solution)/shard_map/ppermute | solution.py:22
  4.3 1.5 %collective-permute-start.8 = (bf16[288,512]{1,0:T(8,128)(2,1)S(1)}, bf16[288,512]{1,0:T(8,128)(2,1)S(1)}, u32[]{:S(2)}, u32[]{:S(2)}) collective-permute-start(bf16[288,512]{1,0:T(8,128)(2,1)S(1)} %get-tuple-element.29), channel_id=1, source_target_pairs={{0,2},{1,3},{2,0},{3,1},{4,6},{5,7},{6,4},{7,5},{8,10},{9,11},{10,... | collective-permute-start | bytes 884744 | tf_op jit(solution)/shard_map/ppermute | solution.py:22
  5.8 1.2 %collective-permute-done.other.coup_other = f32[8,512]{1,0:T(8,128)S(1)} collective-permute-done((f32[8,512]{1,0:T(8,128)S(1)}, f32[8,512]{1,0:T(8,128)S(1)}, u32[]{:S(2)}, u32[]{:S(2)}) %collective-permute-start) | collective-permute-done | bytes 16416 | tf_op jit(solution)/shard_map/ppermute | solution.py:22
  7.0 4.1 %collective-permute-start.3 = (f32[8,512]{1,0:T(8,128)S(1)}, f32[8,512]{1,0:T(8,128)S(1)}, u32[]{:S(2)}, u32[]{:S(2)}) collective-permute-start(f32[8,512]{1,0:T(8,128)S(1)} %shard_map.57.zown), channel_id=1, source_target_pairs={{0,24},{4,28},{8,16},{12,20},{16,8},{20,12},{24,0},{28,4},{1,25},{... | collective-permute-start | bytes 49160 | tf_op jit(solution)/shard_map/ppermute | solution.py:22
  11.2 1.7 %collective-permute-done.3.rest_2_ = f32[8,512]{1,0:T(8,128)S(1)} collective-permute-done((f32[8,512]{1,0:T(8,128)S(1)}, f32[8,512]{1,0:T(8,128)S(1)}, u32[]{:S(2)}, u32[]{:S(2)}) %collective-permute-start.3) | collective-permute-done | bytes 16416 | tf_op jit(solution)/shard_map/ppermute | solution.py:22
  13.0 3.4 %shard_map.56 = (f32[8,64,512]{2,1,0:T(8,128)S(1)}, f32[8,64,512]{2,1,0:T(8,128)S(1)}) custom-call(s32[1,64]{1,0:T(1,128)S(1)} %bitcast.3, s32[1,64]{1,0:T(1,128)S(1)} %bitcast.7), custom_call_target="tpu_custom_call" | custom-call | flops 31457280 | bytes 2097152 | tf_op jit(solution)/shard_map/pallas_call | solution.py:351
  16.6 0.5 %shard_map.58 = (bf16[64,512]{1,0:T(8,128)(2,1)S(1)}, f32[64,512]{1,0:T(8,128)S(1)}, f32[4,8,512]{2,1,0:T(8,128)S(1)}, f32[8,512]{1,0:T(8,128)S(1)}) custom-call(f32[8,64,512]{2,1,0:T(8,128)S(1)} %get-tuple-element.22.noise_own.noise, f32[8,64,512]{2,1,0:T(8,128)S(1)} %get-tuple-element.23.noise_other, f32[8,512]{1,0:T(8,128)S(1)} %get-tuple-element.20.coup, ...), custom_call_target="tpu_custom_call" | custom-call | tf_op jit(solution)/shard_map/pallas_call | solution.py:363
  17.2 1.3 %collective-permute-start.6 = (bf16[64,512]{1,0:T(8,128)(2,1)S(1)}, bf16[64,512]{1,0:T(8,128)(2,1)S(1)}, u32[]{:S(2)}, u32[]{:S(2)}) collective-permute-start(bf16[64,512]{1,0:T(8,128)(2,1)S(1)} %get-tuple-element.27.rest_0_), channel_id=1, source_target_pairs={{24,0},{28,4},{25,1},{29,5},{26,2},{30,6},{27,3},{31,7}} | collective-permute-start | bytes 196616 | tf_op jit(solution)/shard_map/ppermute | solution.py:27
  18.5 1.7 %shard_map.59.rest_0_.rest_6_ = f32[8,64,512]{2,1,0:T(8,128)S(1)} custom-call(s32[1,64]{1,0:T(1,128)S(1)} %bitcast.4, s32[1,64]{1,0:T(1,128)S(1)} %bitcast.8, bf16[64,512]{1,0:T(8,128)(2,1)S(1)} %get-tuple-element.27.rest_0_), custom_call_target="tpu_custom_call" | custom-call | flops 15728640 | bytes 1048576 | tf_op jit(solution)/shard_map/pallas_call | solution.py:351
  20.2 1.7 %shard_map.60 = (f32[8,64,512]{2,1,0:T(8,128)S(1)}, bf16[288,512]{1,0:T(8,128)(2,1)S(1)}, bf16[288,512]{1,0:T(8,128)(2,1)S(1)}, bf16[288,512]{1,0:T(8,128)(2,1)S(1)}) custom-call(s32[1,64]{1,0:T(1,128)S(1)} %bitcast.5, s32[1,64]{1,0:T(1,128)S(1)} %bitcast.9, ...), custom_call_target="tpu_custom_call", output_to_operand_aliasing={{1}: (3, {}), {2}: (4, {}), {3}: (5, {})} | custom-call | flops 15728640 | bytes 1048576 | tf_op jit(solution)/shard_map/pallas_call | solution.py:351
  22.1 0.5 %collective-permute-start.11 = (bf16[288,512]{1,0:T(8,128)(2,1)S(1)}, bf16[288,512]{1,0:T(8,128)(2,1)S(1)}, u32[]{:S(2)}, u32[]{:S(2)}) collective-permute-start(bf16[288,512]{1,0:T(8,128)(2,1)S(1)} %get-tuple-element.33.rest_1_), channel_id=1, source_target_pairs={{0,4},{4,0},{8,12},{12,8},{16,20},{20,16},{24,28},{28,24},{1,5},{5... | collective-permute-start | bytes 884744 | tf_op jit(solution)/shard_map/ppermute | solution.py:22
  22.6 1.3 %collective-permute-start.5 = (bf16[64,512]{1,0:T(8,128)(2,1)S(1)}, bf16[64,512]{1,0:T(8,128)(2,1)S(1)}, u32[]{:S(2)}, u32[]{:S(2)}) collective-permute-start(bf16[64,512]{1,0:T(8,128)(2,1)S(1)} %get-tuple-element.27.rest_0_), channel_id=1, source_target_pairs={{16,0},{20,4},{24,8},{28,12},{17,1},{21,5},{25,9},{29,13},{18,2},{... | collective-permute-start | bytes 196616 | tf_op jit(solution)/shard_map/ppermute | solution.py:27
  23.9 1.2 %collective-permute-done.6.rest_2_ = bf16[64,512]{1,0:T(8,128)(2,1)S(1)} collective-permute-done((bf16[64,512]{1,0:T(8,128)(2,1)S(1)}, bf16[64,512]{1,0:T(8,128)(2,1)S(1)}, u32[]{:S(2)}, u32[]{:S(2)}) %collective-permute-start.6) | collective-permute-done | bytes 65568 | tf_op jit(solution)/shard_map/ppermute | solution.py:27
  25.1 1.3 %collective-permute-start.4 = (bf16[64,512]{1,0:T(8,128)(2,1)S(1)}, bf16[64,512]{1,0:T(8,128)(2,1)S(1)}, u32[]{:S(2)}, u32[]{:S(2)}) collective-permute-start(bf16[64,512]{1,0:T(8,128)(2,1)S(1)} %get-tuple-element.27.rest_0_), channel_id=1, source_target_pairs={{8,0},{12,4},{16,8},{20,12},{24,16},{28,20},{9,1},{13,5},{17,9},{2... | collective-permute-start | bytes 196616 | tf_op jit(solution)/shard_map/ppermute | solution.py:27
  26.4 5.3 %collective-permute-done.5.rest_1_ = bf16[64,512]{1,0:T(8,128)(2,1)S(1)} collective-permute-done((bf16[64,512]{1,0:T(8,128)(2,1)S(1)}, bf16[64,512]{1,0:T(8,128)(2,1)S(1)}, u32[]{:S(2)}, u32[]{:S(2)}) %collective-permute-start.5) | collective-permute-done | bytes 65568 | tf_op jit(solution)/shard_map/ppermute | solution.py:27
  31.8 2.4 %collective-permute-start.15 = (bf16[80,512]{1,0:T(8,128)(2,1)S(1)}, bf16[80,512]{1,0:T(8,128)(2,1)S(1)}, u32[]{:S(2)}, u32[]{:S(2)}) collective-permute-start(bf16[80,512]{1,0:T(8,128)(2,1)S(1)} %shard_map.61.message.rest_0_), channel_id=1, source_target_pairs={{0,3},{1,2},{2,1},{3,0},{4,7},{5,6},{6,5},{7,4},{8,11},{9,10},{10,... | collective-permute-start | bytes 245768 | tf_op jit(solution)/shard_map/ppermute | solution.py:22
  34.2 0.5 %collective-permute-start.14 = (bf16[80,512]{1,0:T(8,128)(2,1)S(1)}, bf16[80,512]{1,0:T(8,128)(2,1)S(1)}, u32[]{:S(2)}, u32[]{:S(2)}) collective-permute-start(bf16[80,512]{1,0:T(8,128)(2,1)S(1)} %shard_map.61.message.rest_0_), channel_id=1, source_target_pairs={{0,2},{1,3},{2,0},{3,1},{4,6},{5,7},{6,4},{7,5},{8,10},{9,11},{10,... | collective-permute-start | bytes 245768 | tf_op jit(solution)/shard_map/ppermute | solution.py:22
  34.7 2.6 %collective-permute-done.15.rest_11_ = bf16[80,512]{1,0:T(8,128)(2,1)S(1)} collective-permute-done((bf16[80,512]{1,0:T(8,128)(2,1)S(1)}, bf16[80,512]{1,0:T(8,128)(2,1)S(1)}, u32[]{:S(2)}, u32[]{:S(2)}) %collective-permute-start.15) | collective-permute-done | bytes 81952 | tf_op jit(solution)/shard_map/ppermute | solution.py:22
  37.3 1.3 %collective-permute-start.13 = (bf16[80,512]{1,0:T(8,128)(2,1)S(1)}, bf16[80,512]{1,0:T(8,128)(2,1)S(1)}, u32[]{:S(2)}, u32[]{:S(2)}) collective-permute-start(bf16[80,512]{1,0:T(8,128)(2,1)S(1)} %shard_map.61.message.rest_0_), channel_id=1, source_target_pairs={{0,1},{1,0},{2,3},{3,2},{4,5},{5,4},{6,7},{7,6},{8,9},{9,8},{10,11... | collective-permute-start | bytes 245768 | tf_op jit(solution)/shard_map/ppermute | solution.py:22
  38.6 1.7 %shard_map.63.rest_8_ = f32[8,64,512]{2,1,0:T(8,128)S(1)} custom-call(s32[1,64]{1,0:T(1,128)S(1)} %bitcast.6, s32[1,64]{1,0:T(1,128)S(1)} %bitcast.10, bf16[80,512]{1,0:T(8,128)(2,1)S(1)} %shard_map.61.message.rest_0_), custom_call_target="tpu_custom_call" | custom-call | flops 15728640 | bytes 1048576 | tf_op jit(solution)/shard_map/pallas_call | solution.py:351
  40.4 0.8 %shard_map.62.partial = f32[512,512]{1,0:T(8,128)S(1)} custom-call(f32[8,512]{1,0:T(8,128)S(1)} %get-tuple-element.20.coup, f32[1,512]{1,0:T(1,128)S(1)} %get-tuple-element.21.spec, bf16[2048,512]{1,0:T(8,128)(2,1)S(1)} %copy-done, f32[8,64,512]{2,1,0:T(8,128)S(1)} %get-tuple-element.22.noise_own.noise, bf16[80,512]{1,0:T(8,128)(2,1)S(1)} %shard_map.61.message.rest_0_), custom_call_target="tpu_custom_call" | custom-call | flops 268435456 | bytes 1048576 | tf_op jit(solution)/shard_map/pallas_call | solution.py:397
  41.2 0.5 %collective-permute-done.13.rest_9_ = bf16[80,512]{1,0:T(8,128)(2,1)S(1)} collective-permute-done((bf16[80,512]{1,0:T(8,128)(2,1)S(1)}, bf16[80,512]{1,0:T(8,128)(2,1)S(1)}, u32[]{:S(2)}, u32[]{:S(2)}) %collective-permute-start.13) | collective-permute-done | bytes 81952 | tf_op jit(solution)/shard_map/ppermute | solution.py:22
  41.8 3.2 %shard_map.64 = f32[512,512]{1,0:T(8,128)} custom-call(f32[512,512]{1,0:T(8,128)S(1)} %shard_map.62.partial, bf16[288,512]{1,0:T(8,128)(2,1)S(1)} %get-tuple-element.32.rest_0_, bf16[288,512]{1,0:T(8,128)(2,1)S(1)} %get-tuple-element.33.rest_1_, bf16[288,512]{1,0:T(8,128)(2,1)S(1)} %get-tuple-element.34.rest_2_, ...), custom_call_target="tpu_custom_call" | custom-call | flops 805306368 | bytes 4194304 | tf_op jit(solution)/shard_map/pallas_call | solution.py:408
  (26 shorter events, 0.6 us)
Async XLA Ops:
  0.0 5.8 %copy-start.3 = (f32[8,512]{1,0:T(8,128)S(1)}, f32[8,512]{1,0:T(8,128)}, u32[]{:S(2)}) copy-start(f32[8,512]{1,0:T(8,128)} %coup.1) | copy-start | bytes 49156
  0.0 13.0 %copy-start.2 = (s32[64]{0:T(128)S(1)}, s32[64]{0:T(128)}, u32[]{:S(2)}) copy-start(s32[64]{0:T(128)} %param.9) | copy-start | bytes 772
  0.0 13.0 %copy-start.1 = (s32[64]{0:T(128)S(1)}, s32[64]{0:T(128)}, u32[]{:S(2)}) copy-start(s32[64]{0:T(128)} %param.8) | copy-start | bytes 772
  1.2 19.0 %collective-permute-start.7 = (bf16[288,512]{1,0:T(8,128)(2,1)S(1)}, bf16[288,512]{1,0:T(8,128)(2,1)S(1)}, u32[]{:S(2)}, u32[]{:S(2)}) collective-permute-start(bf16[288,512]{1,0:T(8,128)(2,1)S(1)} %get-tuple-element.28), channel_id=1, source_target_pairs={{0,1},{1,0},{2,3},{3,2},{4,5},{5,4},{6,7},{7,6},{8,9},{9,8},{10,11... | collective-permute-start | bytes 884744 | tf_op jit(solution)/shard_map/ppermute | solution.py:22
  4.3 16.0 %collective-permute-start.8 = (bf16[288,512]{1,0:T(8,128)(2,1)S(1)}, bf16[288,512]{1,0:T(8,128)(2,1)S(1)}, u32[]{:S(2)}, u32[]{:S(2)}) collective-permute-start(bf16[288,512]{1,0:T(8,128)(2,1)S(1)} %get-tuple-element.29), channel_id=1, source_target_pairs={{0,2},{1,3},{2,0},{3,1},{4,6},{5,7},{6,4},{7,5},{8,10},{9,11},{10,... | collective-permute-start | bytes 884744 | tf_op jit(solution)/shard_map/ppermute | solution.py:22
  5.8 14.4 %collective-permute-start.9 = (bf16[288,512]{1,0:T(8,128)(2,1)S(1)}, bf16[288,512]{1,0:T(8,128)(2,1)S(1)}, u32[]{:S(2)}, u32[]{:S(2)}) collective-permute-start(bf16[288,512]{1,0:T(8,128)(2,1)S(1)} %get-tuple-element.30), channel_id=1, source_target_pairs={{0,3},{1,2},{2,1},{3,0},{4,7},{5,6},{6,5},{7,4},{8,11},{9,10},{10,... | collective-permute-start | bytes 884744 | tf_op jit(solution)/shard_map/ppermute | solution.py:22
  5.8 1.2 %collective-permute-start = (f32[8,512]{1,0:T(8,128)S(1)}, f32[8,512]{1,0:T(8,128)S(1)}, u32[]{:S(2)}, u32[]{:S(2)}) collective-permute-start(f32[8,512]{1,0:T(8,128)S(1)} %copy-done.3), channel_id=1, source_target_pairs={{0,4},{4,0},{8,12},{12,8},{16,20},{20,16},{24,28},{28,24},{1,5},{5... | collective-permute-start | bytes 49160 | tf_op jit(solution)/shard_map/ppermute | solution.py:22
  7.0 5.8 %collective-permute-start.3 = (f32[8,512]{1,0:T(8,128)S(1)}, f32[8,512]{1,0:T(8,128)S(1)}, u32[]{:S(2)}, u32[]{:S(2)}) collective-permute-start(f32[8,512]{1,0:T(8,128)S(1)} %shard_map.57.zown), channel_id=1, source_target_pairs={{0,24},{4,28},{8,16},{12,20},{16,8},{20,12},{24,0},{28,4},{1,25},{... | collective-permute-start | bytes 49160 | tf_op jit(solution)/shard_map/ppermute | solution.py:22
  11.1 5.3 %collective-permute-start.2 = (f32[8,512]{1,0:T(8,128)S(1)}, f32[8,512]{1,0:T(8,128)S(1)}, u32[]{:S(2)}, u32[]{:S(2)}) collective-permute-start(f32[8,512]{1,0:T(8,128)S(1)} %shard_map.57.zown), channel_id=1, source_target_pairs={{0,16},{4,20},{8,24},{12,28},{16,0},{20,4},{24,8},{28,12},{1,17},{... | collective-permute-start | bytes 49160 | tf_op jit(solution)/shard_map/ppermute | solution.py:22
  12.9 3.7 %collective-permute-start.1 = (f32[8,512]{1,0:T(8,128)S(1)}, f32[8,512]{1,0:T(8,128)S(1)}, u32[]{:S(2)}, u32[]{:S(2)}) collective-permute-start(f32[8,512]{1,0:T(8,128)S(1)} %shard_map.57.zown), channel_id=1, source_target_pairs={{0,8},{4,12},{8,0},{12,4},{16,24},{20,28},{24,16},{28,20},{1,9},{5... | collective-permute-start | bytes 49160 | tf_op jit(solution)/shard_map/ppermute | solution.py:22
  17.2 8.0 %collective-permute-start.6 = (bf16[64,512]{1,0:T(8,128)(2,1)S(1)}, bf16[64,512]{1,0:T(8,128)(2,1)S(1)}, u32[]{:S(2)}, u32[]{:S(2)}) collective-permute-start(bf16[64,512]{1,0:T(8,128)(2,1)S(1)} %get-tuple-element.27.rest_0_), channel_id=1, source_target_pairs={{24,0},{28,4},{25,1},{29,5},{26,2},{30,6},{27,3},{31,7}} | collective-permute-start | bytes 196616 | tf_op jit(solution)/shard_map/ppermute | solution.py:27
  20.2 20.2 %copy-start = (bf16[2048,512]{1,0:T(8,128)(2,1)S(1)}, bf16[2048,512]{1,0:T(8,128)(2,1)}, u32[]{:S(2)}) copy-start(bf16[2048,512]{1,0:T(8,128)(2,1)} %basis.3) | copy-start | bytes 6291460
  22.0 19.8 %collective-permute-start.10 = (bf16[288,512]{1,0:T(8,128)(2,1)S(1)}, bf16[288,512]{1,0:T(8,128)(2,1)S(1)}, u32[]{:S(2)}, u32[]{:S(2)}) collective-permute-start(bf16[288,512]{1,0:T(8,128)(2,1)S(1)} %get-tuple-element.32.rest_0_), channel_id=1, source_target_pairs={{0,4},{4,0},{8,12},{12,8},{16,20},{20,16},{24,28},{28,24},{1,5},{5... | collective-permute-start | bytes 884744 | tf_op jit(solution)/shard_map/ppermute | solution.py:22
  22.1 19.7 %collective-permute-start.11 = (bf16[288,512]{1,0:T(8,128)(2,1)S(1)}, bf16[288,512]{1,0:T(8,128)(2,1)S(1)}, u32[]{:S(2)}, u32[]{:S(2)}) collective-permute-start(bf16[288,512]{1,0:T(8,128)(2,1)S(1)} %get-tuple-element.33.rest_1_), channel_id=1, source_target_pairs={{0,4},{4,0},{8,12},{12,8},{16,20},{20,16},{24,28},{28,24},{1,5},{5... | collective-permute-start | bytes 884744 | tf_op jit(solution)/shard_map/ppermute | solution.py:22
  22.6 19.2 %collective-permute-start.12 = (bf16[288,512]{1,0:T(8,128)(2,1)S(1)}, bf16[288,512]{1,0:T(8,128)(2,1)S(1)}, u32[]{:S(2)}, u32[]{:S(2)}) collective-permute-start(bf16[288,512]{1,0:T(8,128)(2,1)S(1)} %get-tuple-element.34.rest_2_), channel_id=1, source_target_pairs={{0,4},{4,0},{8,12},{12,8},{16,20},{20,16},{24,28},{28,24},{1,5},{5... | collective-permute-start | bytes 884744 | tf_op jit(solution)/shard_map/ppermute | solution.py:22
  22.6 9.1 %collective-permute-start.5 = (bf16[64,512]{1,0:T(8,128)(2,1)S(1)}, bf16[64,512]{1,0:T(8,128)(2,1)S(1)}, u32[]{:S(2)}, u32[]{:S(2)}) collective-permute-start(bf16[64,512]{1,0:T(8,128)(2,1)S(1)} %get-tuple-element.27.rest_0_), channel_id=1, source_target_pairs={{16,0},{20,4},{24,8},{28,12},{17,1},{21,5},{25,9},{29,13},{18,2},{... | collective-permute-start | bytes 196616 | tf_op jit(solution)/shard_map/ppermute | solution.py:27
  25.1 6.6 %collective-permute-start.4 = (bf16[64,512]{1,0:T(8,128)(2,1)S(1)}, bf16[64,512]{1,0:T(8,128)(2,1)S(1)}, u32[]{:S(2)}, u32[]{:S(2)}) collective-permute-start(bf16[64,512]{1,0:T(8,128)(2,1)S(1)} %get-tuple-element.27.rest_0_), channel_id=1, source_target_pairs={{8,0},{12,4},{16,8},{20,12},{24,16},{28,20},{9,1},{13,5},{17,9},{2... | collective-permute-start | bytes 196616 | tf_op jit(solution)/shard_map/ppermute | solution.py:27
  31.8 5.5 %collective-permute-start.15 = (bf16[80,512]{1,0:T(8,128)(2,1)S(1)}, bf16[80,512]{1,0:T(8,128)(2,1)S(1)}, u32[]{:S(2)}, u32[]{:S(2)}) collective-permute-start(bf16[80,512]{1,0:T(8,128)(2,1)S(1)} %shard_map.61.message.rest_0_), channel_id=1, source_target_pairs={{0,3},{1,2},{2,1},{3,0},{4,7},{5,6},{6,5},{7,4},{8,11},{9,10},{10,... | collective-permute-start | bytes 245768 | tf_op jit(solution)/shard_map/ppermute | solution.py:22
  34.2 7.0 %collective-permute-start.14 = (bf16[80,512]{1,0:T(8,128)(2,1)S(1)}, bf16[80,512]{1,0:T(8,128)(2,1)S(1)}, u32[]{:S(2)}, u32[]{:S(2)}) collective-permute-start(bf16[80,512]{1,0:T(8,128)(2,1)S(1)} %shard_map.61.message.rest_0_), channel_id=1, source_target_pairs={{0,2},{1,3},{2,0},{3,1},{4,6},{5,7},{6,4},{7,5},{8,10},{9,11},{10,... | collective-permute-start | bytes 245768 | tf_op jit(solution)/shard_map/ppermute | solution.py:22
  37.3 4.4 %collective-permute-start.13 = (bf16[80,512]{1,0:T(8,128)(2,1)S(1)}, bf16[80,512]{1,0:T(8,128)(2,1)S(1)}, u32[]{:S(2)}, u32[]{:S(2)}) collective-permute-start(bf16[80,512]{1,0:T(8,128)(2,1)S(1)} %shard_map.61.message.rest_0_), channel_id=1, source_target_pairs={{0,1},{1,0},{2,3},{3,2},{4,5},{5,4},{6,7},{7,6},{8,9},{9,8},{10,11... | collective-permute-start | bytes 245768 | tf_op jit(solution)/shard_map/ppermute | solution.py:22
where the time goes:
time: 45.2 us; the launch traced here: 45 us
  starting transfers between devices  17.5 us (39%)
  Pallas kernels  14.5 us (32%)
  waiting for transfers between devices  12.8 us (28%)
    ppermute x13, starting transfers between devices, swap(): return lax.ppermute(x, axis, [(i, i ^ offset) for i in range(count)])  13.7 us
    pallas_call x4, Pallas kernels, noise_of(): kernel_call(functools.partial(noise_kernel, 'tm', 'space', blocks, extras...  8.62 us
    ppermute x3, waiting for transfers between devices, send(): lax.ppermute(x, axis, [(i, i - offset) for i in range(offset, count)])  6.52 us
    ppermute x13, waiting for transfers between devices, swap(): return lax.ppermute(x, axis, [(i, i ^ offset) for i in range(count)])  6.25 us
    ppermute x3, starting transfers between devices, send(): lax.ppermute(x, axis, [(i, i - offset) for i in range(offset, count)])  3.85 us
    pallas_call x1, Pallas kernels, local(): kernel_call(functools.partial(final_kernel, 'tm', space - 1), out_shape=j...  3.19 us
    pallas_call x1, Pallas kernels, local(): kernel_call(functools.partial(pack_kernel, 'tm', 'space'), out_shape=[jax...  1.22 us
  transfers between devices with their start and end apart: 16, of which 7 were waited for; matrix products, arithmetic and copies ran while one was open for 0% of the time, Pallas kernels for 22%

commit v1 on v0

v1 whole, which is shorter than its diff:
```python
import functools

import jax
import jax.numpy as jnp
from jax import lax
from jax.experimental import pallas as pl
from jax.experimental.pallas import tpu as pltpu
from jax.sharding import PartitionSpec as P


F32 = jnp.float32
BF16 = jnp.bfloat16
VMEM = pl.BlockSpec(memory_space=pltpu.VMEM)
ANY = pl.BlockSpec(memory_space=pl.ANY)
HBM = pl.BlockSpec(memory_space=pltpu.HBM)
LIMIT = pltpu.CompilerParams(vmem_limit_bytes=48 << 20)
SINE = (6.28318516, -41.34165503, 81.60100406, -76.54978208, 39.53670436)


def partners(count):
    pairs = [(i, i + 1) for i in range(1, count - 2, 2)]
    return pairs, ([count - 1] if count > 1 else [])


def exchange(x, move):
    tm, space = lax.axis_size("tm"), lax.axis_size("space")
    moves = []
    for t in range(tm):
        for s in range(space):
            to = move(t, s)
            if to is not None:
                moves.append((t * space + s, to[0] * space + to[1]))
    return lax.ppermute(x, ("tm", "space"), moves)


def core_swap(x):
    return exchange(x, lambda t, s: (t ^ 1, s))


def split3(x):
    high = x.astype(BF16).astype(F32)
    rest = x - high
    middle = rest.astype(BF16).astype(F32)
    return high, middle, rest - middle


def mix_bits(state):
    state = state ^ lax.shift_right_logical(state, jnp.int32(16))
    state = state * jnp.int32(-2048144789)
    state = state ^ lax.shift_right_logical(state, jnp.int32(13))
    state = state * jnp.int32(-1028477387)
    return state ^ lax.shift_right_logical(state, jnp.int32(16))


def gaussian(seeded):
    first = mix_bits(seeded)
    second = mix_bits(first + jnp.int32(1013904223))
    unit = (lax.shift_right_logical(first, jnp.int32(8)).astype(F32) + 0.5) * (1.0 / 16777216.0)
    square = -2.0 * jnp.log(unit)
    radius = square * lax.rsqrt(jnp.maximum(square, 1e-30))
    turn = (lax.shift_right_arithmetic(second, jnp.int32(8)).astype(F32) + 0.5) * (1.0 / 16777216.0)
    w = 0.25 - jnp.abs(turn)
    z = w * w
    sine = SINE[4]
    for c in SINE[3::-1]:
        sine = sine * z + c
    return radius * (sine * w)


TAIL = 64


def pick(core, offsets):
    return offsets[0] if offsets[0] == offsets[1] else jnp.where(core == 0, offsets[0], offsets[1])


def pack_kernel(tm_axis, sp_axis, offsets, coup, spec, basis, *rest):
    *outs, coup_out, spec_out, sems = rest
    me, sp = lax.axis_index(tm_axis), lax.axis_index(sp_axis)
    core = lax.rem(me, 2)
    copies = [
        pltpu.make_async_copy(coup, coup_out, sems.at[len(outs)]),
        pltpu.make_async_copy(spec, spec_out, sems.at[len(outs) + 1]),
    ]
    for i, (out, offset) in enumerate(zip(outs, offsets)):
        rows = out.shape[0] - TAIL
        block = sp ^ pick(core, offset)
        if offset[0] == offset[1]:
            block = block * 2 + core
        start = pl.multiple_of(block * rows, rows)
        copies.append(
            pltpu.make_async_copy(basis.at[pl.ds(start, rows), :], out.at[pl.ds(0, rows), :], sems.at[i])
        )
    for copy in copies:
        copy.start()
    for copy in copies:
        copy.wait()


def totals(ref):
    product = square = total = None
    for t in range(ref.shape[0]):
        c = ref[pl.ds(t, 1), :]
        product = c if t == 0 else product * c
        square = c * c if t == 0 else square * (c * c)
        total = square if t == 0 else total + square
    return product, total


def joined(early, late):
    return early[0] * late[0], early[1] + (early[0] * early[0]) * late[1]


def table_rows(shape, rows):
    row = lax.broadcasted_iota(jnp.int32, shape, 0)
    table = jnp.zeros(shape, F32)
    for j, value in enumerate(rows):
        table = jnp.where(row == j, value, table)
    return table


def ordered(first, mine, theirs):
    early = tuple(jnp.where(first, x, y) for x, y in zip(mine, theirs))
    late = tuple(jnp.where(first, y, x) for x, y in zip(mine, theirs))
    return early, late


def table_kernel(tm_axis, count, coup, other, spec, *rest):
    out, *messages, tail, sems = rest[count:]
    first = lax.rem(lax.axis_index(tm_axis), 2) == 0
    (x,), (y,) = ordered(first, (coup[...],), (other[...],))
    parts = split3(x) + split3(y)
    parts = parts + (table_rows(x.shape, split3(spec[...])), jnp.zeros_like(x))
    for j in range(4):
        tail[pl.ds(16 * j, 16), :] = jnp.concatenate(parts[2 * j : 2 * j + 2], 0).astype(BF16)
    copies = []
    for i, message in enumerate(messages):
        rows = message.shape[0] - TAIL
        copies.append(pltpu.make_async_copy(tail, message.at[pl.ds(rows, TAIL), :], sems.at[i]))
        copies[-1].start()
    early, late = ordered(first, totals(coup), totals(other))
    out[...] = table_rows(out.shape, (*joined(early, late), *early, *late))
    for copy in copies:
        copy.wait()


def noise_kernel(tm_axis, sp_axis, blocks, extras, keys, counters, *rest):
    *outs, base = rest[extras:]
    outs = outs[: len(blocks)]
    steps, vecs, modes = outs[0].shape
    me, sp = lax.axis_index(tm_axis), lax.axis_index(sp_axis)
    diagonal = lax.broadcasted_iota(jnp.int32, (vecs, vecs), 0) == lax.broadcasted_iota(
        jnp.int32, (vecs, vecs), 1
    )

    def column(ref):
        row = jnp.broadcast_to(ref[...].astype(F32), (vecs, vecs))
        return jnp.sum(jnp.where(diagonal, row, 0.0), axis=1, keepdims=True).astype(jnp.int32)

    start = column(keys) * jnp.int32(668265261) + column(counters) * jnp.int32(374761393)
    base[...] = jnp.broadcast_to(start, base.shape)
    group = 8
    for out, (block, offset) in zip(outs, blocks):
        ids = (sp ^ pick(lax.rem(me, 2), offset)) * modes + lax.broadcasted_iota(jnp.int32, (1, modes), 1)
        lane = ids * jnp.int32(-1640531535)
        first_step = (me ^ block) * steps

        def step(t, _):
            shifted = lane + (first_step + t) * jnp.int32(374761393)
            for v in range(vecs // group):
                seeded = jnp.tile(base[pl.ds(v * group, group), :], (1, modes // 128)) + shifted
                out[t, pl.ds(v * group, group), :] = gaussian(seeded)
            return 0

        lax.fori_loop(0, steps, step, 0)


def chain(coup, spec, d_start, f_start):
    before, after = [], []
    square, total = None, None
    d_now = d_start
    for t in range(coup.shape[0]):
        c = coup[t : t + 1, :]
        square = c * c if t == 0 else square * (c * c)
        total = square if t == 0 else total + square
        before.append(d_now)
        d_now = d_start + f_start * total
        after.append(d_now)
    ratio = jnp.concatenate(before, 0) / jnp.concatenate(after, 0)
    return jnp.sqrt(ratio / spec), ratio


def after(start, total):
    return start[0] + start[1] * total[1], start[1] * (total[0] * total[0])


def select(flag, x, y):
    return tuple(jnp.where(flag, p, q) for p, q in zip(x, y))


def gain_of(start, total):
    return total[0] * start[0] / (start[0] + start[1] * total[1])


def offset_kernel(tm_axis, pairs, single, noise_own, noise_other, coup, coup_other, spec, table, *rest):
    count = 2 * (len(pairs) + len(single))
    received, rest = rest[:count], rest[count:]
    o_ref, late_ref, wts, df, tables, *coefs, tmp = rest
    steps, vecs, modes = noise_own.shape
    me = lax.axis_index(tm_axis)
    chip, core = me // 2, lax.rem(me, 2)
    first = core == 0
    one = jnp.ones((1, modes), F32)
    tables[chip] = table[...]
    for j, offsets in enumerate(pairs):
        tables[chip ^ pick(core, offsets)] = received[2 * j][...]
        tables[chip ^ pick(core, offsets[::-1])] = received[2 * j + 1][...]
    for e in single:
        tables[chip ^ e] = received[-2][...] + received[-1][...]
    now, start, weight = (one, one), (one, one), jnp.zeros((1, modes), F32)
    for b in range(tables.shape[0]):
        wts[b] = jnp.broadcast_to(weight, (8, modes))
        total = tables[b, pl.ds(0, 1), :], tables[b, pl.ds(1, 1), :]
        here = chip == b
        start = select(here, now, start)
        weight = jnp.where(here, 1.0, weight * gain_of(now, total))
        now = after(now, total)
    early = table[pl.ds(2, 1), :], table[pl.ds(3, 1), :]
    late = table[pl.ds(4, 1), :], table[pl.ds(5, 1), :]
    second = after(start, early)
    gain_early, gain_late = gain_of(start, early), gain_of(second, late)
    df[...] = table_rows((8, modes), (*start, *second, gain_late))
    own, other = ordered(first, start, second)
    for j, (ref, sums) in enumerate(((coup, own), (coup_other, other))):
        c = ref[...]
        a, ratio = chain(c, spec[...], *sums)
        coefs[2 * j][...] = c * a
        coefs[2 * j + 1][...] = c * ratio
    tmp[...] = jnp.broadcast_to(gain_early, tmp.shape)

    def tile(v, _):
        at = pl.ds(pl.multiple_of(v * 16, 16), 16)
        ends = []
        for j, noise in enumerate((noise_own, noise_other)):
            alpha, beta = coefs[2 * j], coefs[2 * j + 1]
            carry = jnp.zeros((16, modes), F32)
            for t in range(steps - 1, -1, -1):
                carry = alpha[pl.ds(t, 1), :] * noise[t, at, :] + beta[pl.ds(t, 1), :] * carry
            ends.append(carry)
        (early,), (late,) = ordered(first, ends[:1], ends[1:])
        o_ref[at, :] = (early + tmp[pl.ds(0, 1), :] * late).astype(BF16)
        late_ref[at, :] = late
        return 0

    lax.fori_loop(0, vecs // 16, tile, 0)


def combine_kernel(tm_axis, pairs, single, wts, *rest):
    *received, partial, sent = rest
    me = lax.axis_index(tm_axis)
    chip, core = me // 2, lax.rem(me, 2)
    last = wts.shape[0] - 1
    total = jnp.zeros(partial.shape, F32)
    for offsets, ref in zip(pairs + [(e, e) for e in single], received):
        at = jnp.minimum(chip + pick(core, offsets), last)
        total = total + wts[at][0:1, :] * ref[...].astype(F32)
    partial[...] = total
    sent[...] = total.astype(BF16)


def carry_kernel(tm_axis, partial, theirs, late, df, _, near, own):
    vecs, modes = partial.shape
    is_first = lax.rem(lax.axis_index(tm_axis), 2) == 0
    carry = partial[...] + theirs[...].astype(F32)
    before = (late[...] + df[pl.ds(4, 1), :] * carry).astype(BF16)
    carry = carry.astype(BF16)
    parts = ()
    for j in range(4):
        parts = parts + split3(df[pl.ds(j, 1), :])
    sums = table_rows((16, modes), parts).astype(BF16)
    near[pl.ds(0, vecs), :] = before
    near[pl.ds(vecs, vecs), :] = carry
    near[pl.ds(2 * vecs, 16), :] = sums
    own[pl.ds(0, vecs), :] = jnp.where(is_first, before, carry)
    own[pl.ds(vecs, 16), :] = sums


def values(core, noise, message, c, lam, coefs, rhs):
    steps, vecs, _ = noise.shape
    rows = message.shape[0] - 16
    df = message[pl.ds(rows, 16), :].astype(F32)
    sums = [df[3 * j : 3 * j + 1] + df[3 * j + 1 : 3 * j + 2] + df[3 * j + 2 : 3 * j + 3] for j in range(4)]
    sums = select(core == 0, sums[:2], sums[2:])
    a, ratio = chain(c, lam, *sums)
    a_ref, ratio_ref, c_ref = coefs
    a_ref[...] = a
    ratio_ref[...] = ratio
    c_ref[...] = c
    base = core * vecs if rows > vecs else 0

    def tile(v, _):
        at = pl.ds(pl.multiple_of(v * 16, 16), 16)
        carry = message[pl.ds(pl.multiple_of(base + v * 16, 16), 16), :].astype(F32)
        for t in range(steps - 1, -1, -1):
            value = a_ref[pl.ds(t, 1), :] * noise[t, at, :] + ratio_ref[pl.ds(t, 1), :] * carry
            if t:
                carry = c_ref[pl.ds(t, 1), :] * value
            rhs[pl.ds(pl.multiple_of(t * vecs + v * 16, 16), 16), :] = value.astype(BF16)
        return 0

    lax.fori_loop(0, vecs // 16, tile, 0)


def product(lhs, rhs):
    return lax.dot_general(lhs, rhs, (((1,), (1,)), ((), ())), preferred_element_type=F32)


def own_kernel(tm_axis, sp_axis, coup, spec, basis, noise, message, out, lhs, rhs, *rest):
    *coefs, sem = rest
    rows = lhs.shape[0]
    start = pl.multiple_of(lax.axis_index(sp_axis) * rows, rows)
    copy = pltpu.make_async_copy(basis.at[pl.ds(start, rows), :], lhs, sem)
    copy.start()
    values(lax.rem(lax.axis_index(tm_axis), 2), noise, message, coup[...], spec[...], coefs, rhs)
    copy.wait()
    out[...] = product(lhs[...], rhs[...])


def tail_of(core, tail):
    x = [tail[16 * j : 16 * j + 16].astype(F32) for j in range(4)]
    early = x[0][0:8] + x[0][8:16] + x[1][0:8]
    late = x[1][8:16] + x[2][0:8] + x[2][8:16]
    return jnp.where(core == 0, early, late), x[3][0:1] + x[3][1:2] + x[3][2:3]


def halves_kernel(tm_axis, partial, direct, swapped, noise, message, out, lhs, rhs, *rest):
    *coefs, sems = rest
    core = lax.rem(lax.axis_index(tm_axis), 2)
    rows = lhs.shape[0] // 2
    copies = []
    for j, source in enumerate((direct, swapped)):
        place = pl.multiple_of((core if j == 0 else 1 - core) * rows, rows)
        copies.append(
            pltpu.make_async_copy(source.at[pl.ds(0, rows), :], lhs.at[pl.ds(place, rows), :], sems.at[j])
        )
        copies[-1].start()
    c, lam = tail_of(core, direct[pl.ds(rows, TAIL), :])
    values(core, noise, message, c, lam, coefs, rhs)
    for copy in copies:
        copy.wait()
    out[...] = partial[...] + product(lhs[...], rhs[...])


def block_kernel(tm_axis, partial, basis, noise, message, out, rhs, *coefs):
    core = lax.rem(lax.axis_index(tm_axis), 2)
    rows = basis.shape[0] - TAIL
    c, lam = tail_of(core, basis[pl.ds(rows, TAIL), :])
    values(core, noise, message, c, lam, coefs, rhs)
    out[...] = partial[...] + product(basis[pl.ds(0, rows), :], rhs[...])


def last_kernel(tm_axis, partial, basis, noise, message, out, rhs, result, sems, *coefs):
    core = lax.rem(lax.axis_index(tm_axis), 2)
    rows = basis.shape[0] - TAIL
    c, lam = tail_of(core, basis[pl.ds(rows, TAIL), :])
    values(core, noise, message, c, lam, coefs, rhs)
    width = 128
    copies = []
    for i in range(result.shape[1] // width):
        at = pl.ds(i * width, width)
        result[:, at] = partial[:, at] + product(basis[pl.ds(0, rows), :], rhs[at, :])
        copies.append(pltpu.make_async_copy(result.at[:, at], out.at[:, at], sems.at[i]))
        copies[-1].start()
    for copy in copies:
        copy.wait()


def kernel_call(body, **options):
    return pl.pallas_call(body, **options)


def local(spectrum, coupling, spatial_basis, noise_keys, noise_counters):
    steps, modes = coupling.shape
    vecs = noise_keys.shape[0]
    tm, space = lax.axis_size("tm"), lax.axis_size("space")
    chips = tm // 2
    nodes_here = spatial_basis.shape[0] // space
    half = nodes_here // 2
    keys, counters = noise_keys.reshape(1, vecs), noise_counters.reshape(1, vecs)
    f32 = lambda *shape: jax.ShapeDtypeStruct(shape, F32)
    bf16 = lambda *shape: jax.ShapeDtypeStruct(shape, BF16)
    sp_pairs, sp_single = partners(space)
    z_pairs, z_single = partners(chips)
    routes = sp_pairs + [(d, d) for d in sp_single]
    fast = dict(compiler_params=LIMIT)

    other = core_swap(coupling)
    sizes = [nodes_here + TAIL] * len(sp_pairs) + [half + TAIL] * len(sp_single)
    *messages, coup, spec = kernel_call(
        functools.partial(pack_kernel, "tm", "space", routes),
        out_shape=[bf16(n, modes) for n in sizes] + [f32(steps, modes), f32(1, modes)],
        in_specs=[HBM] * 3,
        out_specs=[VMEM] * (len(sizes) + 2),
        scratch_shapes=[pltpu.SemaphoreType.DMA((len(sizes) + 2,))],
        **fast,
    )(*(pltpu.with_memory_space_constraint(x, pltpu.HBM) for x in (coupling, spectrum.reshape(1, modes), spatial_basis)))
    table, *messages = kernel_call(
        functools.partial(table_kernel, "tm", len(sizes)),
        out_shape=[f32(8, modes)] + [bf16(n, modes) for n in sizes],
        in_specs=[VMEM] * 3 + [ANY] * len(sizes),
        out_specs=[VMEM] + [ANY] * len(sizes),
        scratch_shapes=[pltpu.VMEM((TAIL, modes), BF16), pltpu.SemaphoreType.DMA((len(sizes),))],
        input_output_aliases={3 + i: 1 + i for i in range(len(sizes))},
        **fast,
    )(coup, other, spec, *messages)
    basis = [exchange(m, lambda t, s, r=r: (t, s ^ r[t % 2])) for m, r in zip(messages, routes)]

    def noise_of(blocks, after=(), through=()):
        count = len(blocks) * steps * vecs * modes
        extras = len(after) + len(through)
        return kernel_call(
            functools.partial(noise_kernel, "tm", "space", blocks, extras),
            out_shape=[f32(steps, vecs, modes)] * len(blocks)
            + [jax.ShapeDtypeStruct(x.shape, x.dtype) for x in through],
            in_specs=[VMEM] * 2 + [ANY] * extras,
            out_specs=[VMEM] * len(blocks) + [ANY] * len(through),
            scratch_shapes=[pltpu.VMEM((vecs, 128), jnp.int32)],
            input_output_aliases={2 + len(after) + i: len(blocks) + i for i in range(len(through))},
            cost_estimate=pl.CostEstimate(flops=count * 60, transcendentals=count * 2, bytes_accessed=count * 4),
            **fast,
        )(keys, counters, *after, *through)

    tables = [exchange(table, lambda t, s, r=r: (t ^ (2 * r[t % 2]), s)) for r in z_pairs]
    alone = [exchange(table, lambda t, s, e=e: (t ^ (2 * e), s) if t % 2 == 0 else None) for e in z_single]
    (own,) = noise_of([(0, (0, 0))], after=(table,))
    received = []
    for x in tables:
        received += [x, core_swap(x)]
    for x in alone:
        received += [x, exchange(x, lambda t, s: (t + 1, s) if t % 2 == 0 else None)]
    (paired,) = noise_of([(1, (0, 0))], after=(own,))

    total, late, weights, sums = kernel_call(
        functools.partial(offset_kernel, "tm", z_pairs, z_single),
        out_shape=[bf16(vecs, modes), f32(vecs, modes), f32(chips, 8, modes), f32(8, modes)],
        in_specs=[VMEM] * (6 + len(received)),
        out_specs=[VMEM] * 4,
        scratch_shapes=[pltpu.VMEM((chips, 8, modes), F32)] + [pltpu.VMEM((steps, modes), F32)] * 5,
        **fast,
    )(own, paired, coup, other, spec, table, *received)
    back = lambda t, s, e: (t - 2 * e, s) if t >= 2 * e else None
    later = [exchange(total, lambda t, s, r=r: back(t, s, r[t % 2])) for r in z_pairs]
    later += [exchange(total, lambda t, s, e=e: back(t, s, e) if t % 2 == 0 else None) for e in z_single]
    noise_single = noise_of([(0, (d, d)) for d in sp_single], after=(total,))
    partial, sent = kernel_call(
        functools.partial(combine_kernel, "tm", z_pairs, z_single),
        out_shape=[f32(vecs, modes), bf16(vecs, modes)],
        in_specs=[VMEM] * (1 + len(later)) + [ANY],
        out_specs=[VMEM] * 2,
        **fast,
    )(weights, *later, noise_single[0])
    theirs = core_swap(sent)
    out = noise_of([(0, r) for r in sp_pairs], after=(sent,), through=basis)
    noise_near, basis = out[: len(sp_pairs)], out[len(sp_pairs) :]
    basis_swapped = [core_swap(m) for m in basis]
    near, mine = kernel_call(
        functools.partial(carry_kernel, "tm"),
        out_shape=[bf16(2 * vecs + 16, modes), bf16(vecs + 16, modes)],
        in_specs=[VMEM] * 4 + [ANY],
        out_specs=[VMEM] * 2,
        **fast,
    )(partial, theirs, late, sums, noise_near[0])

    gather_near = [exchange(near, lambda t, s, r=r: (t, s ^ r[t % 2])) for r in sp_pairs]
    gather_single = [exchange(mine, lambda t, s, d=d: (t, s ^ d)) for d in sp_single]
    noise_far = noise_of([(0, r[::-1]) for r in sp_pairs], after=(mine,))

    flops = 2 * nodes_here * modes * steps * vecs
    rhs = pltpu.VMEM((steps * vecs, modes), BF16)
    lhs = pltpu.VMEM((nodes_here, modes), BF16)
    coefs = [pltpu.VMEM((steps, modes), F32)] * 3
    result = f32(nodes_here, steps * vecs)
    cost = pl.CostEstimate(flops=flops, transcendentals=0, bytes_accessed=4 * steps * vecs * modes)
    out = kernel_call(
        functools.partial(own_kernel, "tm", "space"),
        out_shape=result,
        in_specs=[VMEM, VMEM, HBM, VMEM, VMEM],
        out_specs=VMEM,
        scratch_shapes=[lhs, rhs] + coefs + [pltpu.SemaphoreType.DMA],
        cost_estimate=cost,
        **fast,
    )(coup, spec, spatial_basis, own, mine)
    count = len(sp_pairs)
    for j in range(len(sp_single)):
        out = kernel_call(
            functools.partial(halves_kernel, "tm"),
            out_shape=result,
            in_specs=[VMEM] * 5,
            out_specs=VMEM,
            scratch_shapes=[lhs, rhs] + coefs + [pltpu.SemaphoreType.DMA((2,))],
            cost_estimate=cost,
            **fast,
        )(out, basis[count + j], basis_swapped[count + j], noise_single[j], gather_single[j])
    gather_far = [core_swap(m) for m in gather_near]
    for group, (rows, noise, states) in enumerate(
        ((basis, noise_near, gather_near), (basis_swapped, noise_far, gather_far))
    ):
        for j in range(count):
            last = group == 1 and j == count - 1
            chunks = steps * vecs // 128
            out = kernel_call(
                functools.partial(last_kernel if last else block_kernel, "tm"),
                out_shape=result,
                in_specs=[VMEM] * 4,
                out_specs=HBM if last else VMEM,
                scratch_shapes=[rhs]
                + ([pltpu.VMEM(result.shape, F32), pltpu.SemaphoreType.DMA((chunks,))] if last else [])
                + coefs,
                cost_estimate=cost,
                **fast,
            )(out, rows[j], noise[j], states[j])
    return out


def solution(mesh):
    in_specs = (P("space"), P("tm", "space"), P(None, "space"), P(), P())
    out_specs = P("space", "tm")
    return jax.shard_map(local, mesh=mesh, in_specs=in_specs, out_specs=out_specs, check_vma=False)
```

time: 45.2 us -> 49 us (1.084)
  waiting for transfers between devices: 12.8 us -> 15.2 us
  starting transfers between devices: 17.5 us -> 18.2 us
  Pallas kernels: 14.5 us -> 15.1 us
    ppermute x16 -> x15, waiting for transfers between devices: 12.8 us -> 15.2 us  [exchange(): return lax.ppermute(x, ('tm', 'space'), moves)]
    ppermute x16 -> x15, starting transfers between devices: 17.5 us -> 18.2 us  [exchange(): return lax.ppermute(x, ('tm', 'space'), moves)]
    pallas_call x6 -> x9, Pallas kernels: 5.9 us -> 6.4 us  [the longest x2 2.64 us: local(): kernel_call(functools.partial(last_kernel if last else block_kernel, 'tm'...]
    pallas_call x4 -> x5, Pallas kernels: 8.62 us -> 8.72 us  [noise_of(): kernel_call(functools.partial(noise_kernel, 'tm', 'space', blocks, extras...]
  transfers between devices with their start and end apart: 16 -> 15, of which waited for: 7 -> 6; matrix products, arithmetic and copies ran while one was open for 0% -> 0% of each run, Pallas kernels for 22% -> 23%
where the time goes in v1:
time: 49 us; the launch traced here: 48.8 us
  starting transfers between devices  18.2 us (37%)
  waiting for transfers between devices  15.2 us (31%)
  Pallas kernels  15.1 us (31%)
    ppermute x15, starting transfers between devices, exchange(): return lax.ppermute(x, ('tm', 'space'), moves)  18.2 us
    ppermute x15, waiting for transfers between devices, exchange(): return lax.ppermute(x, ('tm', 'space'), moves)  15.2 us
    pallas_call x5, Pallas kernels, noise_of(): kernel_call(functools.partial(noise_kernel, 'tm', 'space', blocks, extras...  8.72 us
    pallas_call x2, Pallas kernels, local(): kernel_call(functools.partial(last_kernel if last else block_kernel, 'tm'...  2.64 us
    pallas_call x1, Pallas kernels, local(): kernel_call(functools.partial(pack_kernel, 'tm', 'space', routes), out_sh...  1.17 us
  transfers between devices with their start and end apart: 15, of which 6 were waited for; matrix products, arithmetic and copies ran while one was open for 0% of the time, Pallas kernels for 23%

profile of v1, /device:TPU:0, one launch (start us, length us, event | category | flops | bytes accessed | tf_op | source)
XLA Modules:
  0.0 48.8 jit_solution(1356162927022074050)
XLA Ops:
  0.5 1.2 %shard_map.55 = (bf16[576,512]{1,0:T(8,128)(2,1)S(1)}, bf16[320,512]{1,0:T(8,128)(2,1)S(1)}, f32[8,512]{1,0:T(8,128)S(1)}, f32[1,512]{1,0:T(1,128)S(1)}) custom-call(f32[8,512]{1,0:T(8,128)} %coup.1, f32[1,512]{1,0:T(1,128)} %bitcast.13, bf16[2048,512]{1,0:T(8,128)(2,1)} %basis.3), custom_call_target="tpu_custom_call" | custom-call | tf_op jit(solution)/shard_map/pallas_call | solution.py:399
  1.9 2.7 %collective-permute-start.8 = (bf16[576,512]{1,0:T(8,128)(2,1)S(1)}, bf16[576,512]{1,0:T(8,128)(2,1)S(1)}, u32[]{:S(2)}, u32[]{:S(2)}) collective-permute-start(bf16[576,512]{1,0:T(8,128)(2,1)S(1)} %get-tuple-element.34), channel_id=1, source_target_pairs={{0,1},{1,0},{2,3},{3,2},{4,6},{5,7},{6,4},{7,5},{8,9},{9,8},{10,11... | collective-permute-start | bytes 1769480 | tf_op jit(solution)/shard_map/ppermute | solution.py:33
  4.7 1.5 %collective-permute-start.9 = (bf16[320,512]{1,0:T(8,128)(2,1)S(1)}, bf16[320,512]{1,0:T(8,128)(2,1)S(1)}, u32[]{:S(2)}, u32[]{:S(2)}) collective-permute-start(bf16[320,512]{1,0:T(8,128)(2,1)S(1)} %get-tuple-element.35), channel_id=1, source_target_pairs={{0,3},{1,2},{2,1},{3,0},{4,7},{5,6},{6,5},{7,4},{8,11},{9,10},{10,... | collective-permute-start | bytes 983048 | tf_op jit(solution)/shard_map/ppermute | solution.py:33
  6.2 1.6 %collective-permute-start.1 = (f32[8,512]{1,0:T(8,128)S(1)}, f32[8,512]{1,0:T(8,128)S(1)}, u32[]{:S(2)}, u32[]{:S(2)}) collective-permute-start(f32[8,512]{1,0:T(8,128)S(1)} %get-tuple-element.27.rest_0_.table), channel_id=1, source_target_pairs={{0,8},{1,9},{2,10},{3,11},{4,20},{5,21},{6,22},{7,23},{8,0},{9,1},... | collective-permute-start | bytes 49160 | tf_op jit(solution)/shard_map/ppermute | solution.py:33
  7.7 4.4 %collective-permute-start.3 = (f32[8,512]{1,0:T(8,128)S(1)}, f32[8,512]{1,0:T(8,128)S(1)}, u32[]{:S(2)}, u32[]{:S(2)}) collective-permute-start(f32[8,512]{1,0:T(8,128)S(1)} %get-tuple-element.27.rest_0_.table), channel_id=1, source_target_pairs={{0,24},{1,25},{2,26},{3,27},{8,16},{9,17},{10,18},{11,19},{16,8},{... | collective-permute-start | bytes 49160 | tf_op jit(solution)/shard_map/ppermute | solution.py:33
  12.2 3.0 %collective-permute-done.3.rest_2_ = f32[8,512]{1,0:T(8,128)S(1)} collective-permute-done((f32[8,512]{1,0:T(8,128)S(1)}, f32[8,512]{1,0:T(8,128)S(1)}, u32[]{:S(2)}, u32[]{:S(2)}) %collective-permute-start.3) | collective-permute-done | bytes 16416 | tf_op jit(solution)/shard_map/ppermute | solution.py:33
  15.2 1.3 %collective-permute-start.4 = (f32[8,512]{1,0:T(8,128)S(1)}, f32[8,512]{1,0:T(8,128)S(1)}, u32[]{:S(2)}, u32[]{:S(2)}) collective-permute-start(f32[8,512]{1,0:T(8,128)S(1)} %collective-permute-done.3.rest_2_), channel_id=1, source_target_pairs={{0,4},{1,5},{2,6},{3,7},{8,12},{9,13},{10,14},{11,15},{16,20},{17,... | collective-permute-start | bytes 49160 | tf_op jit(solution)/shard_map/ppermute | solution.py:33
  16.5 1.7 %shard_map.57.rest_0_.noise_own.noise = f32[8,64,512]{2,1,0:T(8,128)S(1)} custom-call(s32[1,64]{1,0:T(1,128)S(1)} %bitcast.3, s32[1,64]{1,0:T(1,128)S(1)} %bitcast.8, f32[8,512]{1,0:T(8,128)S(1)} %get-tuple-element.27.rest_0_.table), custom_call_target="tpu_custom_call" | custom-call | flops 15728640 | bytes 1048576 | tf_op jit(solution)/shard_map/pallas_call | solution.py:421
  18.2 1.7 %shard_map.58.noise_other = f32[8,64,512]{2,1,0:T(8,128)S(1)} custom-call(s32[1,64]{1,0:T(1,128)S(1)} %bitcast.4, s32[1,64]{1,0:T(1,128)S(1)} %bitcast.9, f32[8,64,512]{2,1,0:T(8,128)S(1)} %shard_map.57.rest_0_.noise_own.noise), custom_call_target="tpu_custom_call" | custom-call | flops 15728640 | bytes 1048576 | tf_op jit(solution)/shard_map/pallas_call | solution.py:421
  20.5 1.3 %collective-permute-start.5 = (bf16[64,512]{1,0:T(8,128)(2,1)S(1)}, bf16[64,512]{1,0:T(8,128)(2,1)S(1)}, u32[]{:S(2)}, u32[]{:S(2)}) collective-permute-start(bf16[64,512]{1,0:T(8,128)(2,1)S(1)} %get-tuple-element.29.rest_0_), channel_id=1, source_target_pairs={{8,0},{9,1},{10,2},{11,3},{16,8},{17,9},{18,10},{19,11},{20,4},{21... | collective-permute-start | bytes 196616 | tf_op jit(solution)/shard_map/ppermute | solution.py:33
  21.8 1.3 %collective-permute-start.6 = (bf16[64,512]{1,0:T(8,128)(2,1)S(1)}, bf16[64,512]{1,0:T(8,128)(2,1)S(1)}, u32[]{:S(2)}, u32[]{:S(2)}) collective-permute-start(bf16[64,512]{1,0:T(8,128)(2,1)S(1)} %get-tuple-element.29.rest_0_), channel_id=1, source_target_pairs={{24,0},{25,1},{26,2},{27,3}} | collective-permute-start | bytes 196616 | tf_op jit(solution)/shard_map/ppermute | solution.py:33
  23.1 1.7 %shard_map.60.rest_2_.noise = f32[8,64,512]{2,1,0:T(8,128)S(1)} custom-call(s32[1,64]{1,0:T(1,128)S(1)} %bitcast.5, s32[1,64]{1,0:T(1,128)S(1)} %bitcast.10, bf16[64,512]{1,0:T(8,128)(2,1)S(1)} %get-tuple-element.29.rest_0_), custom_call_target="tpu_custom_call" | custom-call | flops 15728640 | bytes 1048576 | tf_op jit(solution)/shard_map/pallas_call | solution.py:421
  24.9 1.8 %collective-permute-done.5.rest_0_ = bf16[64,512]{1,0:T(8,128)(2,1)S(1)} collective-permute-done((bf16[64,512]{1,0:T(8,128)(2,1)S(1)}, bf16[64,512]{1,0:T(8,128)(2,1)S(1)}, u32[]{:S(2)}, u32[]{:S(2)}) %collective-permute-start.5) | collective-permute-done | bytes 65568 | tf_op jit(solution)/shard_map/ppermute | solution.py:33
  26.7 3.1 %collective-permute-done.6.rest_1_ = bf16[64,512]{1,0:T(8,128)(2,1)S(1)} collective-permute-done((bf16[64,512]{1,0:T(8,128)(2,1)S(1)}, bf16[64,512]{1,0:T(8,128)(2,1)S(1)}, u32[]{:S(2)}, u32[]{:S(2)}) %collective-permute-start.6) | collective-permute-done | bytes 65568 | tf_op jit(solution)/shard_map/ppermute | solution.py:33
  29.8 1.7 %shard_map.62 = (f32[8,64,512]{2,1,0:T(8,128)S(1)}, bf16[576,512]{1,0:T(8,128)(2,1)S(1)}, bf16[320,512]{1,0:T(8,128)(2,1)S(1)}) custom-call(s32[1,64]{1,0:T(1,128)S(1)} %bitcast.6, s32[1,64]{1,0:T(1,128)S(1)} %bitcast.11, bf16[64,512]{1,0:T(8,128)(2,1)S(1)} %get-tuple-element.31.rest_0_, ...), custom_call_target="tpu_custom_call", output_to_operand_aliasing={{1}: (3, {}), {2}: (4, {})} | custom-call | flops 15728640 | bytes 1048576 | tf_op jit(solution)/shard_map/pallas_call | solution.py:421
  32.2 2.0 %collective-permute-done.7.theirs = bf16[64,512]{1,0:T(8,128)(2,1)S(1)} collective-permute-done((bf16[64,512]{1,0:T(8,128)(2,1)S(1)}, bf16[64,512]{1,0:T(8,128)(2,1)S(1)}, u32[]{:S(2)}, u32[]{:S(2)}) %collective-permute-start.7) | collective-permute-done | bytes 65568 | tf_op jit(solution)/shard_map/ppermute | solution.py:33
  34.3 1.6 %collective-permute-start.12 = (bf16[144,512]{1,0:T(8,128)(2,1)S(1)}, bf16[144,512]{1,0:T(8,128)(2,1)S(1)}, u32[]{:S(2)}, u32[]{:S(2)}) collective-permute-start(bf16[144,512]{1,0:T(8,128)(2,1)S(1)} %get-tuple-element.40), channel_id=1, source_target_pairs={{0,1},{1,0},{2,3},{3,2},{4,6},{5,7},{6,4},{7,5},{8,9},{9,8},{10,11... | collective-permute-start | bytes 442376 | tf_op jit(solution)/shard_map/ppermute | solution.py:33
  35.9 3.7 %collective-permute-done.12.message = bf16[144,512]{1,0:T(8,128)(2,1)S(1)} collective-permute-done((bf16[144,512]{1,0:T(8,128)(2,1)S(1)}, bf16[144,512]{1,0:T(8,128)(2,1)S(1)}, u32[]{:S(2)}, u32[]{:S(2)}) %collective-permute-start.12) | collective-permute-done | bytes 147488 | tf_op jit(solution)/shard_map/ppermute | solution.py:33
  39.5 1.4 %collective-permute-start.11 = (bf16[80,512]{1,0:T(8,128)(2,1)S(1)}, bf16[80,512]{1,0:T(8,128)(2,1)S(1)}, u32[]{:S(2)}, u32[]{:S(2)}) collective-permute-start(bf16[80,512]{1,0:T(8,128)(2,1)S(1)} %get-tuple-element.37.message.rest_0_), channel_id=1, source_target_pairs={{0,3},{1,2},{2,1},{3,0},{4,7},{5,6},{6,5},{7,4},{8,11},{9,10},{10,... | collective-permute-start | bytes 245768 | tf_op jit(solution)/shard_map/ppermute | solution.py:33
  40.9 1.7 %shard_map.67.noise = f32[8,64,512]{2,1,0:T(8,128)S(1)} custom-call(s32[1,64]{1,0:T(1,128)S(1)} %bitcast.7, s32[1,64]{1,0:T(1,128)S(1)} %bitcast.12, bf16[80,512]{1,0:T(8,128)(2,1)S(1)} %get-tuple-element.37.message.rest_0_), custom_call_target="tpu_custom_call" | custom-call | flops 15728640 | bytes 1048576 | tf_op jit(solution)/shard_map/pallas_call | solution.py:421
  42.7 0.9 %shard_map.64.partial = f32[512,512]{1,0:T(8,128)S(1)} custom-call(f32[8,512]{1,0:T(8,128)S(1)} %get-tuple-element.23.coup, f32[1,512]{1,0:T(1,128)S(1)} %get-tuple-element.24.spec, bf16[2048,512]{1,0:T(8,128)(2,1)S(1)} %copy-done, f32[8,64,512]{2,1,0:T(8,128)S(1)} %shard_map.57.rest_0_.noise_own.noise, bf16[80,512]{1,0:T(8,128)(2,1)S(1)} %get-tuple-element.37.message.rest_0_), custom_call_target="tpu_custom_call" | custom-call | flops 268435456 | bytes 1048576 | tf_op jit(solution)/shard_map/pallas_call | solution.py:484
  43.6 1.7 %collective-permute-done.11.message = bf16[80,512]{1,0:T(8,128)(2,1)S(1)} collective-permute-done((bf16[80,512]{1,0:T(8,128)(2,1)S(1)}, bf16[80,512]{1,0:T(8,128)(2,1)S(1)}, u32[]{:S(2)}, u32[]{:S(2)}) %collective-permute-start.11) | collective-permute-done | bytes 81952 | tf_op jit(solution)/shard_map/ppermute | solution.py:33
  45.3 0.9 %shard_map.65.partial = f32[512,512]{1,0:T(8,128)S(1)} custom-call(f32[512,512]{1,0:T(8,128)S(1)} %shard_map.64.partial, bf16[320,512]{1,0:T(8,128)(2,1)S(1)} %get-tuple-element.38.direct, bf16[320,512]{1,0:T(8,128)(2,1)S(1)} %collective-permute-done.10.swapped, f32[8,64,512]{2,1,0:T(8,128)S(1)} %shard_map.60.rest_2_.noise, ...), custom_call_target="tpu_custom_call" | custom-call | flops 268435456 | bytes 1048576 | tf_op jit(solution)/shard_map/pallas_call | solution.py:495
  47.0 1.8 %shard_map.68 = f32[512,512]{1,0:T(8,128)} custom-call(f32[512,512]{1,0:T(8,128)S(1)} %shard_map.66.partial, bf16[576,512]{1,0:T(8,128)(2,1)S(1)} %collective-permute-done.13.basis, f32[8,64,512]{2,1,0:T(8,128)S(1)} %shard_map.67.noise, bf16[144,512]{1,0:T(8,128)(2,1)S(1)} %collective-permute-done.14.message), custom_call_target="tpu_custom_call" | custom-call | flops 268435456 | bytes 1048576 | tf_op jit(solution)/shard_map/pallas_call | solution.py:511
  (26 shorter events, 2.9 us)
Async XLA Ops:
  0.0 16.5 %copy-start.1 = (s32[64]{0:T(128)S(1)}, s32[64]{0:T(128)}, u32[]{:S(2)}) copy-start(s32[64]{0:T(128)} %param.8) | copy-start | bytes 772
  0.0 16.5 %copy-start.2 = (s32[64]{0:T(128)S(1)}, s32[64]{0:T(128)}, u32[]{:S(2)}) copy-start(s32[64]{0:T(128)} %param.9) | copy-start | bytes 772
  0.0 1.7 %collective-permute-start = (f32[8,512]{1,0:T(8,128)}, f32[8,512]{1,0:T(8,128)S(1)}, u32[]{:S(2)}, u32[]{:S(2)}) collective-permute-start(f32[8,512]{1,0:T(8,128)} %coup.1), channel_id=1, source_target_pairs={{0,4},{1,5},{2,6},{3,7},{4,0},{5,1},{6,2},{7,3},{8,12},{9,13},{10,... | collective-permute-start | bytes 49160 | tf_op jit(solution)/shard_map/ppermute | solution.py:33
  1.9 27.9 %collective-permute-start.8 = (bf16[576,512]{1,0:T(8,128)(2,1)S(1)}, bf16[576,512]{1,0:T(8,128)(2,1)S(1)}, u32[]{:S(2)}, u32[]{:S(2)}) collective-permute-start(bf16[576,512]{1,0:T(8,128)(2,1)S(1)} %get-tuple-element.34), channel_id=1, source_target_pairs={{0,1},{1,0},{2,3},{3,2},{4,6},{5,7},{6,4},{7,5},{8,9},{9,8},{10,11... | collective-permute-start | bytes 1769480 | tf_op jit(solution)/shard_map/ppermute | solution.py:33
  4.7 25.2 %collective-permute-start.9 = (bf16[320,512]{1,0:T(8,128)(2,1)S(1)}, bf16[320,512]{1,0:T(8,128)(2,1)S(1)}, u32[]{:S(2)}, u32[]{:S(2)}) collective-permute-start(bf16[320,512]{1,0:T(8,128)(2,1)S(1)} %get-tuple-element.35), channel_id=1, source_target_pairs={{0,3},{1,2},{2,1},{3,0},{4,7},{5,6},{6,5},{7,4},{8,11},{9,10},{10,... | collective-permute-start | bytes 983048 | tf_op jit(solution)/shard_map/ppermute | solution.py:33
  6.2 6.0 %collective-permute-start.1 = (f32[8,512]{1,0:T(8,128)S(1)}, f32[8,512]{1,0:T(8,128)S(1)}, u32[]{:S(2)}, u32[]{:S(2)}) collective-permute-start(f32[8,512]{1,0:T(8,128)S(1)} %get-tuple-element.27.rest_0_.table), channel_id=1, source_target_pairs={{0,8},{1,9},{2,10},{3,11},{4,20},{5,21},{6,22},{7,23},{8,0},{9,1},... | collective-permute-start | bytes 49160 | tf_op jit(solution)/shard_map/ppermute | solution.py:33
  7.7 7.4 %collective-permute-start.3 = (f32[8,512]{1,0:T(8,128)S(1)}, f32[8,512]{1,0:T(8,128)S(1)}, u32[]{:S(2)}, u32[]{:S(2)}) collective-permute-start(f32[8,512]{1,0:T(8,128)S(1)} %get-tuple-element.27.rest_0_.table), channel_id=1, source_target_pairs={{0,24},{1,25},{2,26},{3,27},{8,16},{9,17},{10,18},{11,19},{16,8},{... | collective-permute-start | bytes 49160 | tf_op jit(solution)/shard_map/ppermute | solution.py:33
  12.1 7.8 %collective-permute-start.2 = (f32[8,512]{1,0:T(8,128)S(1)}, f32[8,512]{1,0:T(8,128)S(1)}, u32[]{:S(2)}, u32[]{:S(2)}) collective-permute-start(f32[8,512]{1,0:T(8,128)S(1)} %collective-permute-done.1.rest_0_), channel_id=1, source_target_pairs={{0,4},{1,5},{2,6},{3,7},{4,0},{5,1},{6,2},{7,3},{8,12},{9,13},{10,... | collective-permute-start | bytes 49160 | tf_op jit(solution)/shard_map/ppermute | solution.py:33
  15.2 4.8 %collective-permute-start.4 = (f32[8,512]{1,0:T(8,128)S(1)}, f32[8,512]{1,0:T(8,128)S(1)}, u32[]{:S(2)}, u32[]{:S(2)}) collective-permute-start(f32[8,512]{1,0:T(8,128)S(1)} %collective-permute-done.3.rest_2_), channel_id=1, source_target_pairs={{0,4},{1,5},{2,6},{3,7},{8,12},{9,13},{10,14},{11,15},{16,20},{17,... | collective-permute-start | bytes 49160 | tf_op jit(solution)/shard_map/ppermute | solution.py:33
  20.5 6.2 %collective-permute-start.5 = (bf16[64,512]{1,0:T(8,128)(2,1)S(1)}, bf16[64,512]{1,0:T(8,128)(2,1)S(1)}, u32[]{:S(2)}, u32[]{:S(2)}) collective-permute-start(bf16[64,512]{1,0:T(8,128)(2,1)S(1)} %get-tuple-element.29.rest_0_), channel_id=1, source_target_pairs={{8,0},{9,1},{10,2},{11,3},{16,8},{17,9},{18,10},{19,11},{20,4},{21... | collective-permute-start | bytes 196616 | tf_op jit(solution)/shard_map/ppermute | solution.py:33
  21.8 8.0 %collective-permute-start.6 = (bf16[64,512]{1,0:T(8,128)(2,1)S(1)}, bf16[64,512]{1,0:T(8,128)(2,1)S(1)}, u32[]{:S(2)}, u32[]{:S(2)}) collective-permute-start(bf16[64,512]{1,0:T(8,128)(2,1)S(1)} %get-tuple-element.29.rest_0_), channel_id=1, source_target_pairs={{24,0},{25,1},{26,2},{27,3}} | collective-permute-start | bytes 196616 | tf_op jit(solution)/shard_map/ppermute | solution.py:33
  29.8 12.9 %copy-start = (bf16[2048,512]{1,0:T(8,128)(2,1)S(1)}, bf16[2048,512]{1,0:T(8,128)(2,1)}, u32[]{:S(2)}) copy-start(bf16[2048,512]{1,0:T(8,128)(2,1)} %basis.3) | copy-start | bytes 6291460
  31.6 15.4 %collective-permute-start.13 = (bf16[576,512]{1,0:T(8,128)(2,1)S(1)}, bf16[576,512]{1,0:T(8,128)(2,1)S(1)}, u32[]{:S(2)}, u32[]{:S(2)}) collective-permute-start(bf16[576,512]{1,0:T(8,128)(2,1)S(1)} %get-tuple-element.39.basis), channel_id=1, source_target_pairs={{0,4},{1,5},{2,6},{3,7},{4,0},{5,1},{6,2},{7,3},{8,12},{9,13},{10,... | collective-permute-start | bytes 1769480 | tf_op jit(solution)/shard_map/ppermute | solution.py:33
  31.7 13.6 %collective-permute-start.10 = (bf16[320,512]{1,0:T(8,128)(2,1)S(1)}, bf16[320,512]{1,0:T(8,128)(2,1)S(1)}, u32[]{:S(2)}, u32[]{:S(2)}) collective-permute-start(bf16[320,512]{1,0:T(8,128)(2,1)S(1)} %get-tuple-element.38.direct), channel_id=1, source_target_pairs={{0,4},{1,5},{2,6},{3,7},{4,0},{5,1},{6,2},{7,3},{8,12},{9,13},{10,... | collective-permute-start | bytes 983048 | tf_op jit(solution)/shard_map/ppermute | solution.py:33
  32.2 2.1 %collective-permute-start.7 = (bf16[64,512]{1,0:T(8,128)(2,1)S(1)}, bf16[64,512]{1,0:T(8,128)(2,1)S(1)}, u32[]{:S(2)}, u32[]{:S(2)}) collective-permute-start(bf16[64,512]{1,0:T(8,128)(2,1)S(1)} %get-tuple-element.31.rest_0_), channel_id=1, source_target_pairs={{0,4},{1,5},{2,6},{3,7},{4,0},{5,1},{6,2},{7,3},{8,12},{9,13},{10,... | collective-permute-start | bytes 196616 | tf_op jit(solution)/shard_map/ppermute | solution.py:33
  34.3 5.2 %collective-permute-start.12 = (bf16[144,512]{1,0:T(8,128)(2,1)S(1)}, bf16[144,512]{1,0:T(8,128)(2,1)S(1)}, u32[]{:S(2)}, u32[]{:S(2)}) collective-permute-start(bf16[144,512]{1,0:T(8,128)(2,1)S(1)} %get-tuple-element.40), channel_id=1, source_target_pairs={{0,1},{1,0},{2,3},{3,2},{4,6},{5,7},{6,4},{7,5},{8,9},{9,8},{10,11... | collective-permute-start | bytes 442376 | tf_op jit(solution)/shard_map/ppermute | solution.py:33
  39.5 7.5 %collective-permute-start.14 = (bf16[144,512]{1,0:T(8,128)(2,1)S(1)}, bf16[144,512]{1,0:T(8,128)(2,1)S(1)}, u32[]{:S(2)}, u32[]{:S(2)}) collective-permute-start(bf16[144,512]{1,0:T(8,128)(2,1)S(1)} %collective-permute-done.12.message), channel_id=1, source_target_pairs={{0,4},{1,5},{2,6},{3,7},{4,0},{5,1},{6,2},{7,3},{8,12},{9,13},{10,... | collective-permute-start | bytes 442376 | tf_op jit(solution)/shard_map/ppermute | solution.py:33
  39.5 5.8 %collective-permute-start.11 = (bf16[80,512]{1,0:T(8,128)(2,1)S(1)}, bf16[80,512]{1,0:T(8,128)(2,1)S(1)}, u32[]{:S(2)}, u32[]{:S(2)}) collective-permute-start(bf16[80,512]{1,0:T(8,128)(2,1)S(1)} %get-tuple-element.37.message.rest_0_), channel_id=1, source_target_pairs={{0,3},{1,2},{2,1},{3,0},{4,7},{5,6},{6,5},{7,4},{8,11},{9,10},{10,... | collective-permute-start | bytes 245768 | tf_op jit(solution)/shard_map/ppermute | solution.py:33

commit v2 on v1

v2 whole, which is shorter than its diff:
```python
import functools

import jax
import jax.numpy as jnp
from jax import lax
from jax.experimental import pallas as pl
from jax.experimental.pallas import tpu as pltpu
from jax.sharding import PartitionSpec as P


F32 = jnp.float32
BF16 = jnp.bfloat16
VMEM = pl.BlockSpec(memory_space=pltpu.VMEM)
ANY = pl.BlockSpec(memory_space=pl.ANY)
HBM = pl.BlockSpec(memory_space=pltpu.HBM)
LIMIT = pltpu.CompilerParams(vmem_limit_bytes=48 << 20)
SINE = (6.28318516, -41.34165503, 81.60100406, -76.54978208, 39.53670436)


def swap(x, axis, offset):
    count = lax.axis_size(axis)
    return lax.ppermute(x, axis, [(i, i ^ offset) for i in range(count)])


def split3(x):
    high = x.astype(BF16).astype(F32)
    rest = x - high
    middle = rest.astype(BF16).astype(F32)
    return high, middle, rest - middle


def mix_bits(state):
    state = state ^ lax.shift_right_logical(state, jnp.int32(16))
    state = state * jnp.int32(-2048144789)
    state = state ^ lax.shift_right_logical(state, jnp.int32(13))
    state = state * jnp.int32(-1028477387)
    return state ^ lax.shift_right_logical(state, jnp.int32(16))


def gaussian(seeded):
    first = mix_bits(seeded)
    second = mix_bits(first + jnp.int32(1013904223))
    unit = (lax.shift_right_logical(first, jnp.int32(8)).astype(F32) + 0.5) * (1.0 / 16777216.0)
    square = -2.0 * jnp.log(unit)
    radius = square * lax.rsqrt(jnp.maximum(square, 1e-30))
    turn = (lax.shift_right_arithmetic(second, jnp.int32(8)).astype(F32) + 0.5) * (1.0 / 16777216.0)
    w = 0.25 - jnp.abs(turn)
    z = w * w
    sine = SINE[4]
    for c in SINE[3::-1]:
        sine = sine * z + c
    return radius * (sine * w)


TAIL = 32


def pack_kernel(tm_axis, sp_axis, coup, spec, basis, *rest):
    *outs, coup_out, spec_out, sems = rest
    me, sp = lax.axis_index(tm_axis), lax.axis_index(sp_axis)
    core = lax.rem(me, 2)
    rows = outs[0].shape[0] - TAIL
    small = [
        pltpu.make_async_copy(coup, coup_out, sems.at[len(outs)]),
        pltpu.make_async_copy(spec, spec_out, sems.at[len(outs) + 1]),
    ]
    large = []
    for i, out in enumerate(outs):
        start = pl.multiple_of(((sp ^ (i + 1)) * 2 + core) * rows, rows)
        large.append(
            pltpu.make_async_copy(basis.at[pl.ds(start, rows), :], out.at[pl.ds(0, rows), :], sems.at[i])
        )
    for copy in small + large:
        copy.start()
    for copy in small:
        copy.wait()
    x = coup_out[...]
    parts = split3(x)
    upper = jnp.concatenate(parts[:2], 0).astype(BF16)
    lower = jnp.concatenate([parts[2], table_rows(x.shape, split3(spec_out[...]))], 0).astype(BF16)
    for out in outs:
        out[pl.ds(rows, 16), :] = upper
        out[pl.ds(rows + 16, 16), :] = lower
    for copy in large:
        copy.wait()


def totals(ref):
    product = square = total = None
    for t in range(ref.shape[0]):
        c = ref[pl.ds(t, 1), :]
        product = c if t == 0 else product * c
        square = c * c if t == 0 else square * (c * c)
        total = square if t == 0 else total + square
    return product, total


def joined(early, late):
    return early[0] * late[0], early[1] + (early[0] * early[0]) * late[1]


def table_rows(shape, rows):
    row = lax.broadcasted_iota(jnp.int32, shape, 0)
    table = jnp.zeros(shape, F32)
    for j, value in enumerate(rows):
        table = jnp.where(row == j, value, table)
    return table


def ordered(first, mine, theirs):
    early = tuple(jnp.where(first, x, y) for x, y in zip(mine, theirs))
    late = tuple(jnp.where(first, y, x) for x, y in zip(mine, theirs))
    return early, late


def table_kernel(tm_axis, coup, other, out):
    first = lax.rem(lax.axis_index(tm_axis), 2) == 0
    early, late = ordered(first, totals(coup), totals(other))
    out[...] = table_rows(out.shape, (*joined(early, late), *early, *late))


def noise_kernel(tm_axis, sp_axis, blocks, extras, keys, counters, *rest):
    *outs, base = rest[extras:]
    outs = outs[: len(blocks)]
    steps, vecs, modes = outs[0].shape
    me, sp = lax.axis_index(tm_axis), lax.axis_index(sp_axis)
    diagonal = lax.broadcasted_iota(jnp.int32, (vecs, vecs), 0) == lax.broadcasted_iota(
        jnp.int32, (vecs, vecs), 1
    )

    def column(ref):
        row = jnp.broadcast_to(ref[...].astype(F32), (vecs, vecs))
        return jnp.sum(jnp.where(diagonal, row, 0.0), axis=1, keepdims=True).astype(jnp.int32)

    start = column(keys) * jnp.int32(668265261) + column(counters) * jnp.int32(374761393)
    base[...] = jnp.broadcast_to(start, base.shape)
    group = 8
    for out, (block, offset) in zip(outs, blocks):
        ids = (sp ^ offset) * modes + lax.broadcasted_iota(jnp.int32, (1, modes), 1)
        lane = ids * jnp.int32(-1640531535)
        first_step = (me ^ block) * steps

        def step(t, _):
            shifted = lane + (first_step + t) * jnp.int32(374761393)
            for v in range(vecs // group):
                seeded = jnp.tile(base[pl.ds(v * group, group), :], (1, modes // 128)) + shifted
                out[t, pl.ds(v * group, group), :] = gaussian(seeded)
            return 0

        lax.fori_loop(0, steps, step, 0)


def chain(coup, spec, d_start, f_start):
    before, after = [], []
    square, total = None, None
    d_now = d_start
    for t in range(coup.shape[0]):
        c = coup[t : t + 1, :]
        square = c * c if t == 0 else square * (c * c)
        total = square if t == 0 else total + square
        before.append(d_now)
        d_now = d_start + f_start * total
        after.append(d_now)
    ratio = jnp.concatenate(before, 0) / jnp.concatenate(after, 0)
    return jnp.sqrt(ratio / spec), ratio


def after(start, total):
    return start[0] + start[1] * total[1], start[1] * (total[0] * total[0])


def select(flag, x, y):
    return tuple(jnp.where(flag, p, q) for p, q in zip(x, y))


def gain_of(start, total):
    return total[0] * start[0] / (start[0] + start[1] * total[1])


def offset_kernel(tm_axis, noise_own, noise_other, coup, coup_other, spec, table, *rest):
    received, rest = rest[:-10], rest[-10:]
    o_ref, late_ref, wts, df, tables, *coefs, tmp = rest
    steps, vecs, modes = noise_own.shape
    me = lax.axis_index(tm_axis)
    chip = me // 2
    first = lax.rem(me, 2) == 0
    one = jnp.ones((1, modes), F32)
    tables[chip] = table[...]
    for e, ref in enumerate(received):
        tables[chip ^ (e + 1)] = ref[...]
    now, start, weight = (one, one), (one, one), jnp.zeros((1, modes), F32)
    for b in range(tables.shape[0]):
        wts[b] = jnp.broadcast_to(weight, (8, modes))
        total = tables[b, pl.ds(0, 1), :], tables[b, pl.ds(1, 1), :]
        here = chip == b
        start = select(here, now, start)
        weight = jnp.where(here, 1.0, weight * gain_of(now, total))
        now = after(now, total)
    early = table[pl.ds(2, 1), :], table[pl.ds(3, 1), :]
    late = table[pl.ds(4, 1), :], table[pl.ds(5, 1), :]
    second = after(start, early)
    gain_early, gain_late = gain_of(start, early), gain_of(second, late)
    df[...] = table_rows((8, modes), (*start, *second, gain_late))
    own, other = ordered(first, start, second)
    for j, (ref, sums) in enumerate(((coup, own), (coup_other, other))):
        c = ref[...]
        a, ratio = chain(c, spec[...], *sums)
        coefs[2 * j][...] = c * a
        coefs[2 * j + 1][...] = c * ratio
    tmp[...] = jnp.broadcast_to(gain_early, tmp.shape)

    def tile(v, _):
        at = pl.ds(pl.multiple_of(v * 16, 16), 16)
        ends = []
        for j, noise in enumerate((noise_own, noise_other)):
            alpha, beta = coefs[2 * j], coefs[2 * j + 1]
            carry = jnp.zeros((16, modes), F32)
            for t in range(steps - 1, -1, -1):
                carry = alpha[pl.ds(t, 1), :] * noise[t, at, :] + beta[pl.ds(t, 1), :] * carry
            ends.append(carry)
        (early,), (late,) = ordered(first, ends[:1], ends[1:])
        o_ref[at, :] = (early + tmp[pl.ds(0, 1), :] * late).astype(BF16)
        late_ref[at, :] = late
        return 0

    lax.fori_loop(0, vecs // 16, tile, 0)


def carry_kernel(tm_axis, late, wts, df, *rest):
    *received, _, out = rest
    vecs, modes = late.shape
    me = lax.axis_index(tm_axis)
    first = lax.rem(me, 2) == 0
    carry = jnp.zeros(late.shape, F32)
    for e, ref in enumerate(received):
        carry = carry + wts[(me // 2) ^ (e + 1)][0:1, :] * ref[...].astype(F32)
    out[pl.ds(0, vecs), :] = jnp.where(first, late[...] + df[pl.ds(4, 1), :] * carry, carry).astype(BF16)
    own = select(first, (df[pl.ds(0, 1), :], df[pl.ds(1, 1), :]), (df[pl.ds(2, 1), :], df[pl.ds(3, 1), :]))
    out[pl.ds(vecs, 16), :] = table_rows((16, modes), split3(own[0]) + split3(own[1])).astype(BF16)


def values(noise, message, c, lam, coefs, rhs):
    steps, vecs, _ = noise.shape
    df = message[pl.ds(vecs, 16), :].astype(F32)
    a, ratio = chain(c, lam, df[0:1] + df[1:2] + df[2:3], df[3:4] + df[4:5] + df[5:6])
    a_ref, ratio_ref, c_ref = coefs
    a_ref[...] = a
    ratio_ref[...] = ratio
    c_ref[...] = c

    def tile(v, _):
        at = pl.ds(pl.multiple_of(v * 16, 16), 16)
        carry = message[at, :].astype(F32)
        for t in range(steps - 1, -1, -1):
            value = a_ref[pl.ds(t, 1), :] * noise[t, at, :] + ratio_ref[pl.ds(t, 1), :] * carry
            if t:
                carry = c_ref[pl.ds(t, 1), :] * value
            rhs[pl.ds(pl.multiple_of(t * vecs + v * 16, 16), 16), :] = value.astype(BF16)
        return 0

    lax.fori_loop(0, vecs // 16, tile, 0)


def product(lhs, rhs):
    return lax.dot_general(lhs, rhs, (((1,), (1,)), ((), ())), preferred_element_type=F32)


def own_kernel(sp_axis, coup, spec, basis, noise, message, out, lhs, rhs, *rest):
    *coefs, sem = rest
    rows = lhs.shape[0]
    start = pl.multiple_of(lax.axis_index(sp_axis) * rows, rows)
    copy = pltpu.make_async_copy(basis.at[pl.ds(start, rows), :], lhs, sem)
    copy.start()
    values(noise, message, coup[...], spec[...], coefs, rhs)
    copy.wait()
    out[...] = product(lhs[...], rhs[...])


def block_kernel(tm_axis, last, partial, direct, swapped, noise, message, out, lhs, rhs, sems, *rest):
    coefs = rest[:3]
    core = lax.rem(lax.axis_index(tm_axis), 2)
    rows = lhs.shape[0] // 2
    copies = []
    for j, source in enumerate((direct, swapped)):
        place = pl.multiple_of((core if j == 0 else 1 - core) * rows, rows)
        copies.append(
            pltpu.make_async_copy(source.at[pl.ds(0, rows), :], lhs.at[pl.ds(place, rows), :], sems.at[j])
        )
        copies[-1].start()
    upper = direct[pl.ds(rows, 16), :].astype(F32)
    lower = direct[pl.ds(rows + 16, 16), :].astype(F32)
    c = upper[0:8] + upper[8:16] + lower[0:8]
    values(noise, message, c, lower[8:9] + lower[9:10] + lower[10:11], coefs, rhs)
    for copy in copies:
        copy.wait()
    if not last:
        out[...] = partial[...] + product(lhs[...], rhs[...])
        return
    result = rest[3]
    copies = []
    width = result.shape[2]
    for i in range(result.shape[0]):
        at = pl.ds(i * width, width)
        result[i] = partial[:, at] + product(lhs[...], rhs[at, :])
        copies.append(pltpu.make_async_copy(result.at[i], out.at[:, at], sems.at[2 + i]))
        copies[-1].start()
    for copy in copies:
        copy.wait()


def kernel_call(body, **options):
    return pl.pallas_call(body, **options)


def local(spectrum, coupling, spatial_basis, noise_keys, noise_counters):
    steps, modes = coupling.shape
    vecs = noise_keys.shape[0]
    tm, space = lax.axis_size("tm"), lax.axis_size("space")
    chips = tm // 2
    nodes_here = spatial_basis.shape[0] // space
    half = nodes_here // 2
    keys, counters = noise_keys.reshape(1, vecs), noise_counters.reshape(1, vecs)
    f32 = lambda *shape: jax.ShapeDtypeStruct(shape, F32)
    bf16 = lambda *shape: jax.ShapeDtypeStruct(shape, BF16)
    fast = dict(compiler_params=LIMIT)
    in_hbm = [
        pltpu.with_memory_space_constraint(x, pltpu.HBM)
        for x in (coupling, spectrum.reshape(1, modes), spatial_basis)
    ]

    other = swap(coupling, "tm", 1)
    *messages, coup, spec = kernel_call(
        functools.partial(pack_kernel, "tm", "space"),
        out_shape=[bf16(half + TAIL, modes)] * (space - 1) + [f32(steps, modes), f32(1, modes)],
        in_specs=[HBM] * 3,
        out_specs=[VMEM] * (space + 1),
        scratch_shapes=[pltpu.SemaphoreType.DMA((space + 1,))],
        **fast,
    )(*in_hbm)
    table = kernel_call(
        functools.partial(table_kernel, "tm"),
        out_shape=f32(8, modes),
        in_specs=[VMEM] * 2,
        out_specs=VMEM,
        **fast,
    )(coup, other)
    tables = [swap(table, "tm", 2 * e) for e in range(1, chips)]
    direct = [swap(m, "space", d + 1) for d, m in enumerate(messages)]

    def noise_of(blocks, after):
        count = len(blocks) * steps * vecs * modes
        return kernel_call(
            functools.partial(noise_kernel, "tm", "space", blocks, len(after)),
            out_shape=[f32(steps, vecs, modes)] * len(blocks),
            in_specs=[VMEM] * 2 + [ANY] * len(after),
            out_specs=[VMEM] * len(blocks),
            scratch_shapes=[pltpu.VMEM((vecs, 128), jnp.int32)],
            cost_estimate=pl.CostEstimate(flops=count * 60, transcendentals=count * 2, bytes_accessed=count * 4),
            **fast,
        )(keys, counters, *after)

    own, paired = noise_of(((0, 0), (1, 0)), (table,))
    total, late, weights, sums = kernel_call(
        functools.partial(offset_kernel, "tm"),
        out_shape=[bf16(vecs, modes), f32(vecs, modes), f32(chips, 8, modes), f32(8, modes)],
        in_specs=[VMEM] * (6 + len(tables)),
        out_specs=[VMEM] * 4,
        scratch_shapes=[pltpu.VMEM((chips, 8, modes), F32)] + [pltpu.VMEM((steps, modes), F32)] * 5,
        **fast,
    )(own, paired, coup, other, spec, table, *tables)
    later = [swap(total, "tm", 2 * e) for e in range(1, chips)]
    third = max(1, (space - 1) // 3)
    parts = [range(1, 1 + third), range(1 + third, 1 + 2 * third), range(1 + 2 * third, space)]
    noise = list(noise_of([(0, d) for d in parts[0]], (total,)))
    noise += noise_of([(0, d) for d in parts[1]], (noise[-1],))
    carry = kernel_call(
        functools.partial(carry_kernel, "tm"),
        out_shape=bf16(vecs + 16, modes),
        in_specs=[VMEM] * (3 + len(later)) + [ANY],
        out_specs=VMEM,
        **fast,
    )(late, weights, sums, *later, noise[-1])
    carries = [swap(carry, "space", d) for d in range(1, space)]
    swapped = [swap(m, "tm", 1) for m in direct]
    noise += noise_of([(0, d) for d in parts[2]], (carry,))

    flops = 2 * nodes_here * modes * steps * vecs
    lhs, rhs = pltpu.VMEM((nodes_here, modes), BF16), pltpu.VMEM((steps * vecs, modes), BF16)
    coefs = [pltpu.VMEM((steps, modes), F32)] * 3
    result = f32(nodes_here, steps * vecs)
    cost = pl.CostEstimate(flops=flops, transcendentals=0, bytes_accessed=4 * steps * vecs * modes)
    out = kernel_call(
        functools.partial(own_kernel, "space"),
        out_shape=result,
        in_specs=[VMEM, VMEM, HBM, VMEM, VMEM],
        out_specs=VMEM,
        scratch_shapes=[lhs, rhs] + coefs + [pltpu.SemaphoreType.DMA],
        cost_estimate=cost,
        **fast,
    )(coup, spec, spatial_basis, own, carry)
    width = 128
    chunks = steps * vecs // width
    for d in range(space - 2, -1, -1):
        last = d == 0
        out = kernel_call(
            functools.partial(block_kernel, "tm", last),
            out_shape=result,
            in_specs=[VMEM] * 5,
            out_specs=HBM if last else VMEM,
            scratch_shapes=[lhs, rhs, pltpu.SemaphoreType.DMA((2 + chunks if last else 2,))]
            + coefs
            + ([pltpu.VMEM((chunks, nodes_here, width), F32)] if last else []),
            cost_estimate=cost,
            **fast,
        )(out, direct[d], swapped[d], noise[d], carries[d])
    return out


def solution(mesh):
    in_specs = (P("space"), P("tm", "space"), P(None, "space"), P(), P())
    out_specs = P("space", "tm")
    return jax.shard_map(local, mesh=mesh, in_specs=in_specs, out_specs=out_specs, check_vma=False)
```

time: 49 us -> 52.5 us (1.071)
  waiting for transfers between devices: 15.2 us -> 19.2 us
    ppermute x15 -> x16, waiting for transfers between devices: 15.2 us -> 19.2 us  [swap(): return lax.ppermute(x, axis, [(i, i ^ offset) for i in range(count)])]
    ppermute x15 -> x16, starting transfers between devices: 18.2 us -> 18 us  [swap(): return lax.ppermute(x, axis, [(i, i ^ offset) for i in range(count)])]
    pallas_call x14 -> x12, Pallas kernels: 15.1 us -> 14.9 us  [the longest x4 8.62 us: noise_of(): kernel_call(functools.partial(noise_kernel, 'tm', 'space', blocks, len(af...]
  transfers between devices with their start and end apart: 15 -> 16, of which waited for: 6 -> 7; matrix products, arithmetic and copies ran while one was open for 0% -> 0% of each run, Pallas kernels for 23% -> 23%
where the time goes in v2:
time: 52.5 us; the launch traced here: 52.3 us
  waiting for transfers between devices  19.2 us (37%)
  starting transfers between devices  18 us (34%)
  Pallas kernels  14.9 us (28%)
    ppermute x16, waiting for transfers between devices, swap(): return lax.ppermute(x, axis, [(i, i ^ offset) for i in range(count)])  19.2 us
    ppermute x16, starting transfers between devices, swap(): return lax.ppermute(x, axis, [(i, i ^ offset) for i in range(count)])  18 us
    pallas_call x4, Pallas kernels, noise_of(): kernel_call(functools.partial(noise_kernel, 'tm', 'space', blocks, len(af...  8.62 us
    pallas_call x3, Pallas kernels, local(): kernel_call(functools.partial(block_kernel, 'tm', last), out_shape=result...  3.56 us
    pallas_call x1, Pallas kernels, local(): kernel_call(functools.partial(pack_kernel, 'tm', 'space'), out_shape=[bf1...  1.22 us
  transfers between devices with their start and end apart: 16, of which 7 were waited for; matrix products, arithmetic and copies ran while one was open for 0% of the time, Pallas kernels for 23%

profile of v2, /device:TPU:0, one launch (start us, length us, event | category | flops | bytes accessed | tf_op | source)
XLA Modules:
  0.0 52.3 jit_solution(1884883681103427507)
XLA Ops:
  0.0 1.2 %shard_map.55 = (bf16[288,512]{1,0:T(8,128)(2,1)S(1)}, bf16[288,512]{1,0:T(8,128)(2,1)S(1)}, bf16[288,512]{1,0:T(8,128)(2,1)S(1)}, f32[8,512]{1,0:T(8,128)S(1)}, f32[1,512]{1,0:T(1,128)S(1)}) custom-call(f32[8,512]{1,0:T(8,128)} %coup.1, f32[1,512]{1,0:T(1,128)} %bitcast.11, bf16[2048,512]{1,0:T(8,128)(2,1)} %basis.3), custom_call_target="tpu_custom_call" | custom-call | tf_op jit(solution)/shard_map/pallas_call | solution.py:332
  1.2 4.0 %collective-permute-start.7 = (bf16[288,512]{1,0:T(8,128)(2,1)S(1)}, bf16[288,512]{1,0:T(8,128)(2,1)S(1)}, u32[]{:S(2)}, u32[]{:S(2)}) collective-permute-start(bf16[288,512]{1,0:T(8,128)(2,1)S(1)} %get-tuple-element.24), channel_id=1, source_target_pairs={{0,3},{1,2},{2,1},{3,0},{4,7},{5,6},{6,5},{7,4},{8,11},{9,10},{10,... | collective-permute-start | bytes 884744 | tf_op jit(solution)/shard_map/ppermute | solution.py:22
  5.9 7.3 %collective-permute-done.7.direct = bf16[288,512]{1,0:T(8,128)(2,1)S(1)} collective-permute-done((bf16[288,512]{1,0:T(8,128)(2,1)S(1)}, bf16[288,512]{1,0:T(8,128)(2,1)S(1)}, u32[]{:S(2)}, u32[]{:S(2)}) %collective-permute-start.7) | collective-permute-done | bytes 294944 | tf_op jit(solution)/shard_map/ppermute | solution.py:22
  13.6 1.1 %collective-permute-done.other.coup_other = f32[8,512]{1,0:T(8,128)S(1)} collective-permute-done((f32[8,512]{1,0:T(8,128)S(1)}, f32[8,512]{1,0:T(8,128)S(1)}, u32[]{:S(2)}, u32[]{:S(2)}) %collective-permute-start) | collective-permute-done | bytes 16416 | tf_op jit(solution)/shard_map/ppermute | solution.py:22
  14.8 2.1 %collective-permute-start.1 = (f32[8,512]{1,0:T(8,128)S(1)}, f32[8,512]{1,0:T(8,128)S(1)}, u32[]{:S(2)}, u32[]{:S(2)}) collective-permute-start(f32[8,512]{1,0:T(8,128)S(1)} %shard_map.56.rest_0_.table), channel_id=1, source_target_pairs={{0,8},{4,12},{8,0},{12,4},{16,24},{20,28},{24,16},{28,20},{1,9},{5... | collective-permute-start | bytes 49160 | tf_op jit(solution)/shard_map/ppermute | solution.py:22
  16.9 1.7 %collective-permute-done.10.direct = bf16[288,512]{1,0:T(8,128)(2,1)S(1)} collective-permute-done((bf16[288,512]{1,0:T(8,128)(2,1)S(1)}, bf16[288,512]{1,0:T(8,128)(2,1)S(1)}, u32[]{:S(2)}, u32[]{:S(2)}) %collective-permute-start.10) | collective-permute-done | bytes 294944 | tf_op jit(solution)/shard_map/ppermute | solution.py:22
  18.6 2.8 %collective-permute-start.2 = (f32[8,512]{1,0:T(8,128)S(1)}, f32[8,512]{1,0:T(8,128)S(1)}, u32[]{:S(2)}, u32[]{:S(2)}) collective-permute-start(f32[8,512]{1,0:T(8,128)S(1)} %shard_map.56.rest_0_.table), channel_id=1, source_target_pairs={{0,16},{4,20},{8,24},{12,28},{16,0},{20,4},{24,8},{28,12},{1,17},{... | collective-permute-start | bytes 49160 | tf_op jit(solution)/shard_map/ppermute | solution.py:22
  21.4 1.3 %collective-permute-start.3 = (f32[8,512]{1,0:T(8,128)S(1)}, f32[8,512]{1,0:T(8,128)S(1)}, u32[]{:S(2)}, u32[]{:S(2)}) collective-permute-start(f32[8,512]{1,0:T(8,128)S(1)} %shard_map.56.rest_0_.table), channel_id=1, source_target_pairs={{0,24},{4,28},{8,16},{12,20},{16,8},{20,12},{24,0},{28,4},{1,25},{... | collective-permute-start | bytes 49160 | tf_op jit(solution)/shard_map/ppermute | solution.py:22
  22.7 3.4 %shard_map.57 = (f32[8,64,512]{2,1,0:T(8,128)S(1)}, f32[8,64,512]{2,1,0:T(8,128)S(1)}) custom-call(s32[1,64]{1,0:T(1,128)S(1)} %bitcast.3, s32[1,64]{1,0:T(1,128)S(1)} %bitcast.7, f32[8,512]{1,0:T(8,128)S(1)} %shard_map.56.rest_0_.table), custom_call_target="tpu_custom_call" | custom-call | flops 31457280 | bytes 2097152 | tf_op jit(solution)/shard_map/pallas_call | solution.py:352
  26.1 0.8 %collective-permute-done.3.rest_2_ = f32[8,512]{1,0:T(8,128)S(1)} collective-permute-done((f32[8,512]{1,0:T(8,128)S(1)}, f32[8,512]{1,0:T(8,128)S(1)}, u32[]{:S(2)}, u32[]{:S(2)}) %collective-permute-start.3) | collective-permute-done | bytes 16416 | tf_op jit(solution)/shard_map/ppermute | solution.py:22
  27.6 2.2 %collective-permute-start.5 = (bf16[64,512]{1,0:T(8,128)(2,1)S(1)}, bf16[64,512]{1,0:T(8,128)(2,1)S(1)}, u32[]{:S(2)}, u32[]{:S(2)}) collective-permute-start(bf16[64,512]{1,0:T(8,128)(2,1)S(1)} %get-tuple-element.23.rest_0_), channel_id=1, source_target_pairs={{0,16},{4,20},{8,24},{12,28},{16,0},{20,4},{24,8},{28,12},{1,17},{... | collective-permute-start | bytes 196616 | tf_op jit(solution)/shard_map/ppermute | solution.py:22
  29.8 3.2 %collective-permute-done.4.rest_0_ = bf16[64,512]{1,0:T(8,128)(2,1)S(1)} collective-permute-done((bf16[64,512]{1,0:T(8,128)(2,1)S(1)}, bf16[64,512]{1,0:T(8,128)(2,1)S(1)}, u32[]{:S(2)}, u32[]{:S(2)}) %collective-permute-start.4) | collective-permute-done | bytes 65568 | tf_op jit(solution)/shard_map/ppermute | solution.py:22
  33.5 1.7 %shard_map.59.rest_0_.noise = f32[8,64,512]{2,1,0:T(8,128)S(1)} custom-call(s32[1,64]{1,0:T(1,128)S(1)} %bitcast.4, s32[1,64]{1,0:T(1,128)S(1)} %bitcast.8, bf16[64,512]{1,0:T(8,128)(2,1)S(1)} %get-tuple-element.23.rest_0_), custom_call_target="tpu_custom_call" | custom-call | flops 15728640 | bytes 1048576 | tf_op jit(solution)/shard_map/pallas_call | solution.py:352
  35.2 1.7 %shard_map.60.rest_3_.noise = f32[8,64,512]{2,1,0:T(8,128)S(1)} custom-call(s32[1,64]{1,0:T(1,128)S(1)} %bitcast.5, s32[1,64]{1,0:T(1,128)S(1)} %bitcast.9, f32[8,64,512]{2,1,0:T(8,128)S(1)} %shard_map.59.rest_0_.noise), custom_call_target="tpu_custom_call" | custom-call | flops 15728640 | bytes 1048576 | tf_op jit(solution)/shard_map/pallas_call | solution.py:352
  37.0 2.0 %collective-permute-done.6.rest_2_ = bf16[64,512]{1,0:T(8,128)(2,1)S(1)} collective-permute-done((bf16[64,512]{1,0:T(8,128)(2,1)S(1)}, bf16[64,512]{1,0:T(8,128)(2,1)S(1)}, u32[]{:S(2)}, u32[]{:S(2)}) %collective-permute-start.6) | collective-permute-done | bytes 65568 | tf_op jit(solution)/shard_map/ppermute | solution.py:22
  39.1 1.8 %collective-permute-start.9 = (bf16[80,512]{1,0:T(8,128)(2,1)S(1)}, bf16[80,512]{1,0:T(8,128)(2,1)S(1)}, u32[]{:S(2)}, u32[]{:S(2)}) collective-permute-start(bf16[80,512]{1,0:T(8,128)(2,1)S(1)} %shard_map.61.message.rest_0_), channel_id=1, source_target_pairs={{0,3},{1,2},{2,1},{3,0},{4,7},{5,6},{6,5},{7,4},{8,11},{9,10},{10,... | collective-permute-start | bytes 245768 | tf_op jit(solution)/shard_map/ppermute | solution.py:22
  40.9 1.2 %collective-permute-start.12 = (bf16[80,512]{1,0:T(8,128)(2,1)S(1)}, bf16[80,512]{1,0:T(8,128)(2,1)S(1)}, u32[]{:S(2)}, u32[]{:S(2)}) collective-permute-start(bf16[80,512]{1,0:T(8,128)(2,1)S(1)} %shard_map.61.message.rest_0_), channel_id=1, source_target_pairs={{0,2},{1,3},{2,0},{3,1},{4,6},{5,7},{6,4},{7,5},{8,10},{9,11},{10,... | collective-permute-start | bytes 245768 | tf_op jit(solution)/shard_map/ppermute | solution.py:22
  42.1 3.2 %collective-permute-done.9.message = bf16[80,512]{1,0:T(8,128)(2,1)S(1)} collective-permute-done((bf16[80,512]{1,0:T(8,128)(2,1)S(1)}, bf16[80,512]{1,0:T(8,128)(2,1)S(1)}, u32[]{:S(2)}, u32[]{:S(2)}) %collective-permute-start.9) | collective-permute-done | bytes 81952 | tf_op jit(solution)/shard_map/ppermute | solution.py:22
  45.3 0.8 %collective-permute-start.15 = (bf16[80,512]{1,0:T(8,128)(2,1)S(1)}, bf16[80,512]{1,0:T(8,128)(2,1)S(1)}, u32[]{:S(2)}, u32[]{:S(2)}) collective-permute-start(bf16[80,512]{1,0:T(8,128)(2,1)S(1)} %shard_map.61.message.rest_0_), channel_id=1, source_target_pairs={{0,1},{1,0},{2,3},{3,2},{4,5},{5,4},{6,7},{7,6},{8,9},{9,8},{10,11... | collective-permute-start | bytes 245768 | tf_op jit(solution)/shard_map/ppermute | solution.py:22
  46.1 1.7 %shard_map.63.noise = f32[8,64,512]{2,1,0:T(8,128)S(1)} custom-call(s32[1,64]{1,0:T(1,128)S(1)} %bitcast.6, s32[1,64]{1,0:T(1,128)S(1)} %bitcast.10, bf16[80,512]{1,0:T(8,128)(2,1)S(1)} %shard_map.61.message.rest_0_), custom_call_target="tpu_custom_call" | custom-call | flops 15728640 | bytes 1048576 | tf_op jit(solution)/shard_map/pallas_call | solution.py:352
  47.8 0.8 %shard_map.62.partial = f32[512,512]{1,0:T(8,128)S(1)} custom-call(f32[8,512]{1,0:T(8,128)S(1)} %get-tuple-element.16.coup, f32[1,512]{1,0:T(1,128)S(1)} %get-tuple-element.17.spec, bf16[2048,512]{1,0:T(8,128)(2,1)S(1)} %copy-done, f32[8,64,512]{2,1,0:T(8,128)S(1)} %get-tuple-element.18.noise_own.noise, bf16[80,512]{1,0:T(8,128)(2,1)S(1)} %shard_map.61.message.rest_0_), custom_call_target="tpu_custom_call" | custom-call | flops 268435456 | bytes 1048576 | tf_op jit(solution)/shard_map/pallas_call | solution.py:392
  48.7 0.8 %shard_map.64.partial = f32[512,512]{1,0:T(8,128)S(1)} custom-call(f32[512,512]{1,0:T(8,128)S(1)} %shard_map.62.partial, bf16[288,512]{1,0:T(8,128)(2,1)S(1)} %collective-permute-done.7.direct, bf16[288,512]{1,0:T(8,128)(2,1)S(1)} %collective-permute-done.8.swapped, f32[8,64,512]{2,1,0:T(8,128)S(1)} %shard_map.63.noise, ...), custom_call_target="tpu_custom_call" | custom-call | flops 268435456 | bytes 1048576 | tf_op jit(solution)/shard_map/pallas_call | solution.py:405
  49.6 0.9 %shard_map.65.partial = f32[512,512]{1,0:T(8,128)S(1)} custom-call(f32[512,512]{1,0:T(8,128)S(1)} %shard_map.64.partial, bf16[288,512]{1,0:T(8,128)(2,1)S(1)} %collective-permute-done.10.direct, bf16[288,512]{1,0:T(8,128)(2,1)S(1)} %collective-permute-done.11.swapped, f32[8,64,512]{2,1,0:T(8,128)S(1)} %shard_map.60.rest_3_.noise, ...), custom_call_target="tpu_custom_call" | custom-call | flops 268435456 | bytes 1048576 | tf_op jit(solution)/shard_map/pallas_call | solution.py:405
  50.5 1.8 %shard_map.66 = f32[512,512]{1,0:T(8,128)} custom-call(f32[512,512]{1,0:T(8,128)S(1)} %shard_map.65.partial, bf16[288,512]{1,0:T(8,128)(2,1)S(1)} %collective-permute-done.13.direct, bf16[288,512]{1,0:T(8,128)(2,1)S(1)} %collective-permute-done.14.swapped, f32[8,64,512]{2,1,0:T(8,128)S(1)} %shard_map.59.rest_0_.noise, ...), custom_call_target="tpu_custom_call" | custom-call | flops 268435456 | bytes 1048576 | tf_op jit(solution)/shard_map/pallas_call | solution.py:405
  (28 shorter events, 2.5 us)
Async XLA Ops:
  0.0 13.1 %copy-start.3 = (f32[8,512]{1,0:T(8,128)S(1)}, f32[8,512]{1,0:T(8,128)}, u32[]{:S(2)}) copy-start(f32[8,512]{1,0:T(8,128)} %coup.1) | copy-start | bytes 49156
  0.0 22.7 %copy-start.1 = (s32[64]{0:T(128)S(1)}, s32[64]{0:T(128)}, u32[]{:S(2)}) copy-start(s32[64]{0:T(128)} %param.8) | copy-start | bytes 772
  0.0 22.7 %copy-start.2 = (s32[64]{0:T(128)S(1)}, s32[64]{0:T(128)}, u32[]{:S(2)}) copy-start(s32[64]{0:T(128)} %param.9) | copy-start | bytes 772
  1.2 11.9 %collective-permute-start.7 = (bf16[288,512]{1,0:T(8,128)(2,1)S(1)}, bf16[288,512]{1,0:T(8,128)(2,1)S(1)}, u32[]{:S(2)}, u32[]{:S(2)}) collective-permute-start(bf16[288,512]{1,0:T(8,128)(2,1)S(1)} %get-tuple-element.24), channel_id=1, source_target_pairs={{0,3},{1,2},{2,1},{3,0},{4,7},{5,6},{6,5},{7,4},{8,11},{9,10},{10,... | collective-permute-start | bytes 884744 | tf_op jit(solution)/shard_map/ppermute | solution.py:22
  5.2 13.3 %collective-permute-start.10 = (bf16[288,512]{1,0:T(8,128)(2,1)S(1)}, bf16[288,512]{1,0:T(8,128)(2,1)S(1)}, u32[]{:S(2)}, u32[]{:S(2)}) collective-permute-start(bf16[288,512]{1,0:T(8,128)(2,1)S(1)} %get-tuple-element.25), channel_id=1, source_target_pairs={{0,2},{1,3},{2,0},{3,1},{4,6},{5,7},{6,4},{7,5},{8,10},{9,11},{10,... | collective-permute-start | bytes 884744 | tf_op jit(solution)/shard_map/ppermute | solution.py:22
  5.7 21.8 %collective-permute-start.13 = (bf16[288,512]{1,0:T(8,128)(2,1)S(1)}, bf16[288,512]{1,0:T(8,128)(2,1)S(1)}, u32[]{:S(2)}, u32[]{:S(2)}) collective-permute-start(bf16[288,512]{1,0:T(8,128)(2,1)S(1)} %get-tuple-element.26), channel_id=1, source_target_pairs={{0,1},{1,0},{2,3},{3,2},{4,5},{5,4},{6,7},{7,6},{8,9},{9,8},{10,11... | collective-permute-start | bytes 884744 | tf_op jit(solution)/shard_map/ppermute | solution.py:22
  13.1 35.6 %collective-permute-start.8 = (bf16[288,512]{1,0:T(8,128)(2,1)S(1)}, bf16[288,512]{1,0:T(8,128)(2,1)S(1)}, u32[]{:S(2)}, u32[]{:S(2)}) collective-permute-start(bf16[288,512]{1,0:T(8,128)(2,1)S(1)} %collective-permute-done.7.direct), channel_id=1, source_target_pairs={{0,4},{4,0},{8,12},{12,8},{16,20},{20,16},{24,28},{28,24},{1,5},{5... | collective-permute-start | bytes 884744 | tf_op jit(solution)/shard_map/ppermute | solution.py:22
  13.1 1.6 %collective-permute-start = (f32[8,512]{1,0:T(8,128)S(1)}, f32[8,512]{1,0:T(8,128)S(1)}, u32[]{:S(2)}, u32[]{:S(2)}) collective-permute-start(f32[8,512]{1,0:T(8,128)S(1)} %copy-done.3), channel_id=1, source_target_pairs={{0,4},{4,0},{8,12},{12,8},{16,20},{20,16},{24,28},{28,24},{1,5},{5... | collective-permute-start | bytes 49160 | tf_op jit(solution)/shard_map/ppermute | solution.py:22
  14.8 6.6 %collective-permute-start.1 = (f32[8,512]{1,0:T(8,128)S(1)}, f32[8,512]{1,0:T(8,128)S(1)}, u32[]{:S(2)}, u32[]{:S(2)}) collective-permute-start(f32[8,512]{1,0:T(8,128)S(1)} %shard_map.56.rest_0_.table), channel_id=1, source_target_pairs={{0,8},{4,12},{8,0},{12,4},{16,24},{20,28},{24,16},{28,20},{1,9},{5... | collective-permute-start | bytes 49160 | tf_op jit(solution)/shard_map/ppermute | solution.py:22
  18.6 31.0 %collective-permute-start.11 = (bf16[288,512]{1,0:T(8,128)(2,1)S(1)}, bf16[288,512]{1,0:T(8,128)(2,1)S(1)}, u32[]{:S(2)}, u32[]{:S(2)}) collective-permute-start(bf16[288,512]{1,0:T(8,128)(2,1)S(1)} %collective-permute-done.10.direct), channel_id=1, source_target_pairs={{0,4},{4,0},{8,12},{12,8},{16,20},{20,16},{24,28},{28,24},{1,5},{5... | collective-permute-start | bytes 884744 | tf_op jit(solution)/shard_map/ppermute | solution.py:22
  18.6 7.5 %collective-permute-start.2 = (f32[8,512]{1,0:T(8,128)S(1)}, f32[8,512]{1,0:T(8,128)S(1)}, u32[]{:S(2)}, u32[]{:S(2)}) collective-permute-start(f32[8,512]{1,0:T(8,128)S(1)} %shard_map.56.rest_0_.table), channel_id=1, source_target_pairs={{0,16},{4,20},{8,24},{12,28},{16,0},{20,4},{24,8},{28,12},{1,17},{... | collective-permute-start | bytes 49160 | tf_op jit(solution)/shard_map/ppermute | solution.py:22
  21.4 5.5 %collective-permute-start.3 = (f32[8,512]{1,0:T(8,128)S(1)}, f32[8,512]{1,0:T(8,128)S(1)}, u32[]{:S(2)}, u32[]{:S(2)}) collective-permute-start(f32[8,512]{1,0:T(8,128)S(1)} %shard_map.56.rest_0_.table), channel_id=1, source_target_pairs={{0,24},{4,28},{8,16},{12,20},{16,8},{20,12},{24,0},{28,4},{1,25},{... | collective-permute-start | bytes 49160 | tf_op jit(solution)/shard_map/ppermute | solution.py:22
  27.4 5.5 %collective-permute-start.4 = (bf16[64,512]{1,0:T(8,128)(2,1)S(1)}, bf16[64,512]{1,0:T(8,128)(2,1)S(1)}, u32[]{:S(2)}, u32[]{:S(2)}) collective-permute-start(bf16[64,512]{1,0:T(8,128)(2,1)S(1)} %get-tuple-element.23.rest_0_), channel_id=1, source_target_pairs={{0,8},{4,12},{8,0},{12,4},{16,24},{20,28},{24,16},{28,20},{1,9},{5... | collective-permute-start | bytes 196616 | tf_op jit(solution)/shard_map/ppermute | solution.py:22
  27.5 22.9 %collective-permute-start.14 = (bf16[288,512]{1,0:T(8,128)(2,1)S(1)}, bf16[288,512]{1,0:T(8,128)(2,1)S(1)}, u32[]{:S(2)}, u32[]{:S(2)}) collective-permute-start(bf16[288,512]{1,0:T(8,128)(2,1)S(1)} %collective-permute-done.13.direct), channel_id=1, source_target_pairs={{0,4},{4,0},{8,12},{12,8},{16,20},{20,16},{24,28},{28,24},{1,5},{5... | collective-permute-start | bytes 884744 | tf_op jit(solution)/shard_map/ppermute | solution.py:22
  27.6 9.4 %collective-permute-start.5 = (bf16[64,512]{1,0:T(8,128)(2,1)S(1)}, bf16[64,512]{1,0:T(8,128)(2,1)S(1)}, u32[]{:S(2)}, u32[]{:S(2)}) collective-permute-start(bf16[64,512]{1,0:T(8,128)(2,1)S(1)} %get-tuple-element.23.rest_0_), channel_id=1, source_target_pairs={{0,16},{4,20},{8,24},{12,28},{16,0},{20,4},{24,8},{28,12},{1,17},{... | collective-permute-start | bytes 196616 | tf_op jit(solution)/shard_map/ppermute | solution.py:22
  33.0 6.1 %collective-permute-start.6 = (bf16[64,512]{1,0:T(8,128)(2,1)S(1)}, bf16[64,512]{1,0:T(8,128)(2,1)S(1)}, u32[]{:S(2)}, u32[]{:S(2)}) collective-permute-start(bf16[64,512]{1,0:T(8,128)(2,1)S(1)} %get-tuple-element.23.rest_0_), channel_id=1, source_target_pairs={{0,24},{4,28},{8,16},{12,20},{16,8},{20,12},{24,0},{28,4},{1,25},{... | collective-permute-start | bytes 196616 | tf_op jit(solution)/shard_map/ppermute | solution.py:22
  35.2 12.6 %copy-start = (bf16[2048,512]{1,0:T(8,128)(2,1)S(1)}, bf16[2048,512]{1,0:T(8,128)(2,1)}, u32[]{:S(2)}) copy-start(bf16[2048,512]{1,0:T(8,128)(2,1)} %basis.3) | copy-start | bytes 6291460
  39.1 6.2 %collective-permute-start.9 = (bf16[80,512]{1,0:T(8,128)(2,1)S(1)}, bf16[80,512]{1,0:T(8,128)(2,1)S(1)}, u32[]{:S(2)}, u32[]{:S(2)}) collective-permute-start(bf16[80,512]{1,0:T(8,128)(2,1)S(1)} %shard_map.61.message.rest_0_), channel_id=1, source_target_pairs={{0,3},{1,2},{2,1},{3,0},{4,7},{5,6},{6,5},{7,4},{8,11},{9,10},{10,... | collective-permute-start | bytes 245768 | tf_op jit(solution)/shard_map/ppermute | solution.py:22
  40.9 8.6 %collective-permute-start.12 = (bf16[80,512]{1,0:T(8,128)(2,1)S(1)}, bf16[80,512]{1,0:T(8,128)(2,1)S(1)}, u32[]{:S(2)}, u32[]{:S(2)}) collective-permute-start(bf16[80,512]{1,0:T(8,128)(2,1)S(1)} %shard_map.61.message.rest_0_), channel_id=1, source_target_pairs={{0,2},{1,3},{2,0},{3,1},{4,6},{5,7},{6,4},{7,5},{8,10},{9,11},{10,... | collective-permute-start | bytes 245768 | tf_op jit(solution)/shard_map/ppermute | solution.py:22
  45.3 5.1 %collective-permute-start.15 = (bf16[80,512]{1,0:T(8,128)(2,1)S(1)}, bf16[80,512]{1,0:T(8,128)(2,1)S(1)}, u32[]{:S(2)}, u32[]{:S(2)}) collective-permute-start(bf16[80,512]{1,0:T(8,128)(2,1)S(1)} %shard_map.61.message.rest_0_), channel_id=1, source_target_pairs={{0,1},{1,0},{2,3},{3,2},{4,5},{5,4},{6,7},{7,6},{8,9},{9,8},{10,11... | collective-permute-start | bytes 245768 | tf_op jit(solution)/shard_map/ppermute | solution.py:22

commit v3 on v2

--- a/solution.py
+++ b/solution.py
@@ -15,6 +15,22 @@
 HBM = pl.BlockSpec(memory_space=pltpu.HBM)
 LIMIT = pltpu.CompilerParams(vmem_limit_bytes=48 << 20)
 SINE = (6.28318516, -41.34165503, 81.60100406, -76.54978208, 39.53670436)
+
+
+def partners(count):
+    pairs = [(i, i + 1) for i in range(1, count - 2, 2)]
+    return pairs, ([count - 1] if count > 1 else [])
+
+
+def exchange(x, move):
+    tm, space = lax.axis_size("tm"), lax.axis_size("space")
+    moves = []
+    for t in range(tm):
+        for s in range(space):
+            to = move(t, s)
+            if to is not None:
+                moves.append((t * space + s, to[0] * space + to[1]))
+    return lax.ppermute(x, ("tm", "space"), moves)
 
 
 def swap(x, axis, offset):
@@ -52,36 +68,33 @@
     return radius * (sine * w)
 
 
-TAIL = 32
-
-
-def pack_kernel(tm_axis, sp_axis, coup, spec, basis, *rest):
+TAIL = 64
+
+
+def pick(core, offsets):
+    return offsets[0] if offsets[0] == offsets[1] else jnp.where(core == 0, offsets[0], offsets[1])
+
+
+def pack_kernel(tm_axis, sp_axis, offsets, coup, spec, basis, *rest):
     *outs, coup_out, spec_out, sems = rest
     me, sp = lax.axis_index(tm_axis), lax.axis_index(sp_axis)
     core = lax.rem(me, 2)
-    rows = outs[0].shape[0] - TAIL
-    small = [
+    copies = [
         pltpu.make_async_copy(coup, coup_out, sems.at[len(outs)]),
         pltpu.make_async_copy(spec, spec_out, sems.at[len(outs) + 1]),
     ]
-    large = []
-    for i, out in enumerate(outs):
-        start = pl.multiple_of(((sp ^ (i + 1)) * 2 + core) * rows, rows)
-        large.append(
+    for i, (out, offset) in enumerate(zip(outs, offsets)):
+        rows = out.shape[0] - TAIL
+        block = sp ^ pick(core, offset)
+        if offset[0] == offset[1]:
+            block = block * 2 + core
+        start = pl.multiple_of(block * rows, rows)
+        copies.append(
             pltpu.make_async_copy(basis.at[pl.ds(start, rows), :], out.at[pl.ds(0, rows), :], sems.at[i])
         )
-    for copy in small + large:
+    for copy in copies:
         copy.start()
-    for copy in small:
-        copy.wait()
-    x = coup_out[...]
-    parts = split3(x)
-    upper = jnp.concatenate(parts[:2], 0).astype(BF16)
-    lower = jnp.concatenate([parts[2], table_rows(x.shape, split3(spec_out[...]))], 0).astype(BF16)
-    for out in outs:
-        out[pl.ds(rows, 16), :] = upper
-        out[pl.ds(rows + 16, 16), :] = lower
-    for copy in large:
+    for copy in copies:
         copy.wait()
 
 
@@ -113,10 +126,23 @@
     return early, late
 
 
-def table_kernel(tm_axis, coup, other, out):
+def table_kernel(tm_axis, count, coup, other, spec, *rest):
+    out, *messages, tail, sems = rest[count:]
     first = lax.rem(lax.axis_index(tm_axis), 2) == 0
+    (x,), (y,) = ordered(first, (coup[...],), (other[...],))
+    parts = split3(x) + split3(y)
+    parts = parts + (table_rows(x.shape, split3(spec[...])), jnp.zeros_like(x))
+    for j in range(4):
+        tail[pl.ds(16 * j, 16), :] = jnp.concatenate(parts[2 * j : 2 * j + 2], 0).astype(BF16)
+    copies = []
+    for i, message in enumerate(messages):
+        rows = message.shape[0] - TAIL
+        copies.append(pltpu.make_async_copy(tail, message.at[pl.ds(rows, TAIL), :], sems.at[i]))
+        copies[-1].start()
     early, late = ordered(first, totals(coup), totals(other))
     out[...] = table_rows(out.shape, (*joined(early, late), *early, *late))
+    for copy in copies:
+        copy.wait()
 
 
 def noise_kernel(tm_axis, sp_axis, blocks, extras, keys, counters, *rest):
@@ -276,23 +302,37 @@
     out[...] = product(lhs[...], rhs[...])
 
 
-def block_kernel(tm_axis, last, partial, direct, swapped, noise, message, out, lhs, rhs, sems, *rest):
+def block_kernel(tm_axis, place, last, partial, direct, swapped, noise, message, out, lhs, rhs, tail, sems, *rest):
     coefs = rest[:3]
     core = lax.rem(lax.axis_index(tm_axis), 2)
-    rows = lhs.shape[0] // 2
-    copies = []
-    for j, source in enumerate((direct, swapped)):
-        place = pl.multiple_of((core if j == 0 else 1 - core) * rows, rows)
-        copies.append(
-            pltpu.make_async_copy(source.at[pl.ds(0, rows), :], lhs.at[pl.ds(place, rows), :], sems.at[j])
-        )
-        copies[-1].start()
-    upper = direct[pl.ds(rows, 16), :].astype(F32)
-    lower = direct[pl.ds(rows + 16, 16), :].astype(F32)
-    c = upper[0:8] + upper[8:16] + lower[0:8]
-    values(noise, message, c, lower[8:9] + lower[9:10] + lower[10:11], coefs, rhs)
-    for copy in copies:
-        copy.wait()
+    rows = direct.shape[0] - TAIL
+    if place is None:
+        head = pltpu.make_async_copy(direct.at[pl.ds(rows, TAIL), :], tail, sems.at[0])
+        head.start()
+        for j, source in enumerate((direct, swapped)):
+            at = pl.multiple_of((core if j == 0 else 1 - core) * rows, rows)
+            pltpu.make_async_copy(source.at[pl.ds(0, rows), :], lhs.at[pl.ds(at, rows), :], sems.at[1 + j]).start()
+        head.wait()
+    else:
+        for j, source in enumerate((direct, swapped)):
+
+            @pl.when((core == place) == (j == 0))
+            def _():
+                pltpu.make_async_copy(source.at[pl.ds(rows, TAIL), :], tail, sems.at[0]).start()
+                pltpu.make_async_copy(source.at[pl.ds(0, rows), :], lhs, sems.at[1]).start()
+
+        pltpu.make_async_copy(direct.at[pl.ds(rows, TAIL), :], tail, sems.at[0]).wait()
+    x = [tail[pl.ds(16 * j, 16), :].astype(F32) for j in range(4)]
+    early = x[0][0:8] + x[0][8:16] + x[1][0:8]
+    late = x[1][8:16] + x[2][0:8] + x[2][8:16]
+    c = jnp.where(core == 0, early, late)
+    values(noise, message, c, x[3][0:1] + x[3][1:2] + x[3][2:3], coefs, rhs)
+    if place is None:
+        for j, source in enumerate((direct, swapped)):
+            at = pl.multiple_of((core if j == 0 else 1 - core) * rows, rows)
+            pltpu.make_async_copy(source.at[pl.ds(0, rows), :], lhs.at[pl.ds(at, rows), :], sems.at[1 + j]).wait()
+    else:
+        pltpu.make_async_copy(direct.at[pl.ds(0, rows), :], lhs, sems.at[1]).wait()
     if not last:
         out[...] = partial[...] + product(lhs[...], rhs[...])
         return
@@ -302,7 +342,7 @@
     for i in range(result.shape[0]):
         at = pl.ds(i * width, width)
         result[i] = partial[:, at] + product(lhs[...], rhs[at, :])
-        copies.append(pltpu.make_async_copy(result.at[i], out.at[:, at], sems.at[2 + i]))
+        copies.append(pltpu.make_async_copy(result.at[i], out.at[:, at], sems.at[3 + i]))
         copies[-1].start()
     for copy in copies:
         copy.wait()
@@ -328,24 +368,29 @@
         for x in (coupling, spectrum.reshape(1, modes), spatial_basis)
     ]
 
+    pairs, single = partners(space)
+    routes = [(d, d) for d in single] + pairs
+    sizes = [half + TAIL] * len(single) + [nodes_here + TAIL] * len(pairs)
     other = swap(coupling, "tm", 1)
     *messages, coup, spec = kernel_call(
-        functools.partial(pack_kernel, "tm", "space"),
-        out_shape=[bf16(half + TAIL, modes)] * (space - 1) + [f32(steps, modes), f32(1, modes)],
+        functools.partial(pack_kernel, "tm", "space", routes),
+        out_shape=[bf16(n, modes) for n in sizes] + [f32(steps, modes), f32(1, modes)],
         in_specs=[HBM] * 3,
-        out_specs=[VMEM] * (space + 1),
-        scratch_shapes=[pltpu.SemaphoreType.DMA((space + 1,))],
+        out_specs=[VMEM] * (len(sizes) + 2),
+        scratch_shapes=[pltpu.SemaphoreType.DMA((len(sizes) + 2,))],
         **fast,
     )(*in_hbm)
-    table = kernel_call(
-        functools.partial(table_kernel, "tm"),
-        out_shape=f32(8, modes),
-        in_specs=[VMEM] * 2,
-        out_specs=VMEM,
+    table, *messages = kernel_call(
+        functools.partial(table_kernel, "tm", len(sizes)),
+        out_shape=[f32(8, modes)] + [bf16(n, modes) for n in sizes],
+        in_specs=[VMEM] * 3 + [ANY] * len(sizes),
+        out_specs=[VMEM] + [ANY] * len(sizes),
+        scratch_shapes=[pltpu.VMEM((TAIL, modes), BF16), pltpu.SemaphoreType.DMA((len(sizes),))],
+        input_output_aliases={3 + i: 1 + i for i in range(len(sizes))},
         **fast,
-    )(coup, other)
+    )(coup, other, spec, *messages)
     tables = [swap(table, "tm", 2 * e) for e in range(1, chips)]
-    direct = [swap(m, "space", d + 1) for d, m in enumerate(messages)]
+    direct = [exchange(m, lambda t, s, r=r: (t, s ^ r[t % 2])) for m, r in zip(messages, routes)]
 
     def noise_of(blocks, after):
         count = len(blocks) * steps * vecs * modes
@@ -400,19 +445,26 @@
     )(coup, spec, spatial_basis, own, carry)
     width = 128
     chunks = steps * vecs // width
-    for d in range(space - 2, -1, -1):
-        last = d == 0
+    order = [(d, 0, None) for d in single]
+    order += [(d, len(single) + j, place) for j, pair in enumerate(pairs) for place, d in enumerate(pair)]
+    for n, (d, i, place) in enumerate(order):
+        last = n == len(order) - 1
         out = kernel_call(
-            functools.partial(block_kernel, "tm", last),
+            functools.partial(block_kernel, "tm", place, last),
             out_shape=result,
-            in_specs=[VMEM] * 5,
+            in_specs=[VMEM, ANY, ANY, VMEM, VMEM],
             out_specs=HBM if last else VMEM,
-            scratch_shapes=[lhs, rhs, pltpu.SemaphoreType.DMA((2 + chunks if last else 2,))]
+            scratch_shapes=[
+                lhs,
+                rhs,
+                pltpu.VMEM((TAIL, modes), BF16),
+                pltpu.SemaphoreType.DMA((3 + chunks if last else 3,)),
+            ]
             + coefs
             + ([pltpu.VMEM((chunks, nodes_here, width), F32)] if last else []),
             cost_estimate=cost,
             **fast,
-        )(out, direct[d], swapped[d], noise[d], carries[d])
+        )(out, direct[i], swapped[i], noise[d - 1], carries[d - 1])
     return out
 
 

time: 52.5 us -> 49.9 us (0.950)
  waiting for transfers between devices: 19.2 us -> 17.2 us
  starting transfers between devices: 18 us -> 17.1 us
    ppermute x16 -> x12, waiting for transfers between devices: 19.2 us -> 2.36 us  [swap(): return lax.ppermute(x, axis, [(i, i ^ offset) for i in range(count)])]
    ppermute x0 -> x2, waiting for transfers between devices: none -> 14.9 us  [exchange(): return lax.ppermute(x, ('tm', 'space'), moves)]
    ppermute x16 -> x12, starting transfers between devices: 18 us -> 12.9 us  [swap(): return lax.ppermute(x, axis, [(i, i ^ offset) for i in range(count)])]
    ppermute x0 -> x2, starting transfers between devices: none -> 4.21 us  [exchange(): return lax.ppermute(x, ('tm', 'space'), moves)]
  transfers between devices with their start and end apart: 16 -> 14, of which waited for: 7 -> 4; matrix products, arithmetic and copies ran while one was open for 0% -> 0% of each run, Pallas kernels for 23% -> 26%
where the time goes in v3:
time: 49.9 us; the launch traced here: 49.7 us
  waiting for transfers between devices  17.2 us (34%)
  starting transfers between devices  17.1 us (34%)
  Pallas kernels  15.2 us (30%)
    ppermute x2, waiting for transfers between devices, exchange(): return lax.ppermute(x, ('tm', 'space'), moves)  14.9 us
    ppermute x12, starting transfers between devices, swap(): return lax.ppermute(x, axis, [(i, i ^ offset) for i in range(count)])  12.9 us
    pallas_call x4, Pallas kernels, noise_of(): kernel_call(functools.partial(noise_kernel, 'tm', 'space', blocks, len(af...  8.62 us
    ppermute x2, starting transfers between devices, exchange(): return lax.ppermute(x, ('tm', 'space'), moves)  4.21 us
    pallas_call x3, Pallas kernels, local(): kernel_call(functools.partial(block_kernel, 'tm', place, last), out_shape...  3.78 us
    ppermute x12, waiting for transfers between devices, swap(): return lax.ppermute(x, axis, [(i, i ^ offset) for i in range(count)])  2.36 us
    pallas_call x1, Pallas kernels, local(): kernel_call(functools.partial(pack_kernel, 'tm', 'space', routes), out_sh...  1.19 us
  transfers between devices with their start and end apart: 14, of which 4 were waited for; matrix products, arithmetic and copies ran while one was open for 0% of the time, Pallas kernels for 26%

profile of v3, /device:TPU:0, one launch (start us, length us, event | category | flops | bytes accessed | tf_op | source)
XLA Modules:
  0.0 49.7 jit_solution(18259413060171535154)
XLA Ops:
  0.0 0.5 collective-permute-start
  0.5 1.2 %shard_map.55 = (bf16[320,512]{1,0:T(8,128)(2,1)S(1)}, bf16[576,512]{1,0:T(8,128)(2,1)S(1)}, f32[8,512]{1,0:T(8,128)S(1)}, f32[1,512]{1,0:T(1,128)S(1)}) custom-call(f32[8,512]{1,0:T(8,128)} %coup.1, f32[1,512]{1,0:T(1,128)} %bitcast.11, bf16[2048,512]{1,0:T(8,128)(2,1)} %basis.3), custom_call_target="tpu_custom_call" | custom-call | tf_op jit(solution)/shard_map/pallas_call | solution.py:375
  2.0 2.7 %collective-permute-start.10 = (bf16[576,512]{1,0:T(8,128)(2,1)S(1)}, bf16[576,512]{1,0:T(8,128)(2,1)S(1)}, u32[]{:S(2)}, u32[]{:S(2)}) collective-permute-start(bf16[576,512]{1,0:T(8,128)(2,1)S(1)} %get-tuple-element.30), channel_id=1, source_target_pairs={{0,1},{1,0},{2,3},{3,2},{4,6},{5,7},{6,4},{7,5},{8,9},{9,8},{10,11... | collective-permute-start | bytes 1769480 | tf_op jit(solution)/shard_map/ppermute | solution.py:33
  4.7 1.5 %collective-permute-start.7 = (bf16[320,512]{1,0:T(8,128)(2,1)S(1)}, bf16[320,512]{1,0:T(8,128)(2,1)S(1)}, u32[]{:S(2)}, u32[]{:S(2)}) collective-permute-start(bf16[320,512]{1,0:T(8,128)(2,1)S(1)} %get-tuple-element.29), channel_id=1, source_target_pairs={{0,3},{1,2},{2,1},{3,0},{4,7},{5,6},{6,5},{7,4},{8,11},{9,10},{10,... | collective-permute-start | bytes 983048 | tf_op jit(solution)/shard_map/ppermute | solution.py:33
  6.2 9.9 %collective-permute-done.10.direct = bf16[576,512]{1,0:T(8,128)(2,1)S(1)} collective-permute-done((bf16[576,512]{1,0:T(8,128)(2,1)S(1)}, bf16[576,512]{1,0:T(8,128)(2,1)S(1)}, u32[]{:S(2)}, u32[]{:S(2)}) %collective-permute-start.10) | collective-permute-done | bytes 589856 | tf_op jit(solution)/shard_map/ppermute | solution.py:33
  16.1 5.0 %collective-permute-done.7.direct = bf16[320,512]{1,0:T(8,128)(2,1)S(1)} collective-permute-done((bf16[320,512]{1,0:T(8,128)(2,1)S(1)}, bf16[320,512]{1,0:T(8,128)(2,1)S(1)}, u32[]{:S(2)}, u32[]{:S(2)}) %collective-permute-start.7) | collective-permute-done | bytes 327712 | tf_op jit(solution)/shard_map/ppermute | solution.py:33
  21.0 1.6 %collective-permute-start.1 = (f32[8,512]{1,0:T(8,128)S(1)}, f32[8,512]{1,0:T(8,128)S(1)}, u32[]{:S(2)}, u32[]{:S(2)}) collective-permute-start(f32[8,512]{1,0:T(8,128)S(1)} %get-tuple-element.22.rest_0_.table), channel_id=1, source_target_pairs={{0,8},{4,12},{8,0},{12,4},{16,24},{20,28},{24,16},{28,20},{1,9},{5... | collective-permute-start | bytes 49160 | tf_op jit(solution)/shard_map/ppermute | solution.py:38
  22.6 2.6 %collective-permute-start.2 = (f32[8,512]{1,0:T(8,128)S(1)}, f32[8,512]{1,0:T(8,128)S(1)}, u32[]{:S(2)}, u32[]{:S(2)}) collective-permute-start(f32[8,512]{1,0:T(8,128)S(1)} %get-tuple-element.22.rest_0_.table), channel_id=1, source_target_pairs={{0,16},{4,20},{8,24},{12,28},{16,0},{20,4},{24,8},{28,12},{1,17},{... | collective-permute-start | bytes 49160 | tf_op jit(solution)/shard_map/ppermute | solution.py:38
  25.4 3.4 %shard_map.57 = (f32[8,64,512]{2,1,0:T(8,128)S(1)}, f32[8,64,512]{2,1,0:T(8,128)S(1)}) custom-call(s32[1,64]{1,0:T(1,128)S(1)} %bitcast.3, s32[1,64]{1,0:T(1,128)S(1)} %bitcast.7, f32[8,512]{1,0:T(8,128)S(1)} %get-tuple-element.22.rest_0_.table), custom_call_target="tpu_custom_call" | custom-call | flops 31457280 | bytes 2097152 | tf_op jit(solution)/shard_map/pallas_call | solution.py:397
  28.9 1.9 %collective-permute-done.3.rest_2_ = f32[8,512]{1,0:T(8,128)S(1)} collective-permute-done((f32[8,512]{1,0:T(8,128)S(1)}, f32[8,512]{1,0:T(8,128)S(1)}, u32[]{:S(2)}, u32[]{:S(2)}) %collective-permute-start.3) | collective-permute-done | bytes 16416 | tf_op jit(solution)/shard_map/ppermute | solution.py:38
  30.8 0.5 shard_map.58
  31.3 2.3 %collective-permute-start.5 = (bf16[64,512]{1,0:T(8,128)(2,1)S(1)}, bf16[64,512]{1,0:T(8,128)(2,1)S(1)}, u32[]{:S(2)}, u32[]{:S(2)}) collective-permute-start(bf16[64,512]{1,0:T(8,128)(2,1)S(1)} %get-tuple-element.28.rest_0_), channel_id=1, source_target_pairs={{0,16},{4,20},{8,24},{12,28},{16,0},{20,4},{24,8},{28,12},{1,17},{... | collective-permute-start | bytes 196616 | tf_op jit(solution)/shard_map/ppermute | solution.py:38
  33.6 2.1 %collective-permute-start.6 = (bf16[64,512]{1,0:T(8,128)(2,1)S(1)}, bf16[64,512]{1,0:T(8,128)(2,1)S(1)}, u32[]{:S(2)}, u32[]{:S(2)}) collective-permute-start(bf16[64,512]{1,0:T(8,128)(2,1)S(1)} %get-tuple-element.28.rest_0_), channel_id=1, source_target_pairs={{0,24},{4,28},{8,16},{12,20},{16,8},{20,12},{24,0},{28,4},{1,25},{... | collective-permute-start | bytes 196616 | tf_op jit(solution)/shard_map/ppermute | solution.py:38
  35.7 1.7 %shard_map.59.rest_0_.noise = f32[8,64,512]{2,1,0:T(8,128)S(1)} custom-call(s32[1,64]{1,0:T(1,128)S(1)} %bitcast.4, s32[1,64]{1,0:T(1,128)S(1)} %bitcast.8, bf16[64,512]{1,0:T(8,128)(2,1)S(1)} %get-tuple-element.28.rest_0_), custom_call_target="tpu_custom_call" | custom-call | flops 15728640 | bytes 1048576 | tf_op jit(solution)/shard_map/pallas_call | solution.py:397
  37.5 1.7 %shard_map.60.rest_3_.noise = f32[8,64,512]{2,1,0:T(8,128)S(1)} custom-call(s32[1,64]{1,0:T(1,128)S(1)} %bitcast.5, s32[1,64]{1,0:T(1,128)S(1)} %bitcast.9, f32[8,64,512]{2,1,0:T(8,128)S(1)} %shard_map.59.rest_0_.noise), custom_call_target="tpu_custom_call" | custom-call | flops 15728640 | bytes 1048576 | tf_op jit(solution)/shard_map/pallas_call | solution.py:397
  39.2 0.4 collective-permute-done.6.rest_2_
  39.8 1.5 %collective-permute-start.9 = (bf16[80,512]{1,0:T(8,128)(2,1)S(1)}, bf16[80,512]{1,0:T(8,128)(2,1)S(1)}, u32[]{:S(2)}, u32[]{:S(2)}) collective-permute-start(bf16[80,512]{1,0:T(8,128)(2,1)S(1)} %shard_map.61.message.rest_0_), channel_id=1, source_target_pairs={{0,3},{1,2},{2,1},{3,0},{4,7},{5,6},{6,5},{7,4},{8,11},{9,10},{10,... | collective-permute-start | bytes 245768 | tf_op jit(solution)/shard_map/ppermute | solution.py:38
  41.3 0.5 %collective-permute-start.12 = (bf16[80,512]{1,0:T(8,128)(2,1)S(1)}, bf16[80,512]{1,0:T(8,128)(2,1)S(1)}, u32[]{:S(2)}, u32[]{:S(2)}) collective-permute-start(bf16[80,512]{1,0:T(8,128)(2,1)S(1)} %shard_map.61.message.rest_0_), channel_id=1, source_target_pairs={{0,1},{1,0},{2,3},{3,2},{4,5},{5,4},{6,7},{7,6},{8,9},{9,8},{10,11... | collective-permute-start | bytes 245768 | tf_op jit(solution)/shard_map/ppermute | solution.py:38
  41.8 1.5 %collective-permute-start.13 = (bf16[80,512]{1,0:T(8,128)(2,1)S(1)}, bf16[80,512]{1,0:T(8,128)(2,1)S(1)}, u32[]{:S(2)}, u32[]{:S(2)}) collective-permute-start(bf16[80,512]{1,0:T(8,128)(2,1)S(1)} %shard_map.61.message.rest_0_), channel_id=1, source_target_pairs={{0,2},{1,3},{2,0},{3,1},{4,6},{5,7},{6,4},{7,5},{8,10},{9,11},{10,... | collective-permute-start | bytes 245768 | tf_op jit(solution)/shard_map/ppermute | solution.py:38
  43.3 1.7 %shard_map.63.noise = f32[8,64,512]{2,1,0:T(8,128)S(1)} custom-call(s32[1,64]{1,0:T(1,128)S(1)} %bitcast.6, s32[1,64]{1,0:T(1,128)S(1)} %bitcast.10, bf16[80,512]{1,0:T(8,128)(2,1)S(1)} %shard_map.61.message.rest_0_), custom_call_target="tpu_custom_call" | custom-call | flops 15728640 | bytes 1048576 | tf_op jit(solution)/shard_map/pallas_call | solution.py:397
  45.1 0.8 %shard_map.62.partial = f32[512,512]{1,0:T(8,128)S(1)} custom-call(f32[8,512]{1,0:T(8,128)S(1)} %get-tuple-element.18.coup, f32[1,512]{1,0:T(1,128)S(1)} %get-tuple-element.19.spec, bf16[2048,512]{1,0:T(8,128)(2,1)S(1)} %copy-done, f32[8,64,512]{2,1,0:T(8,128)S(1)} %get-tuple-element.23.noise_own.noise, bf16[80,512]{1,0:T(8,128)(2,1)S(1)} %shard_map.61.message.rest_0_), custom_call_target="tpu_custom_call" | custom-call | flops 268435456 | bytes 1048576 | tf_op jit(solution)/shard_map/pallas_call | solution.py:437
  45.9 0.9 %shard_map.64.partial = f32[512,512]{1,0:T(8,128)S(1)} custom-call(f32[512,512]{1,0:T(8,128)S(1)} %shard_map.62.partial, bf16[320,512]{1,0:T(8,128)(2,1)S(1)} %collective-permute-done.7.direct, bf16[320,512]{1,0:T(8,128)(2,1)S(1)} %collective-permute-done.8.swapped, f32[8,64,512]{2,1,0:T(8,128)S(1)} %shard_map.63.noise, ...), custom_call_target="tpu_custom_call" | custom-call | flops 268435456 | bytes 1048576 | tf_op jit(solution)/shard_map/pallas_call | solution.py:452
  46.9 0.9 %shard_map.65.partial = f32[512,512]{1,0:T(8,128)S(1)} custom-call(f32[512,512]{1,0:T(8,128)S(1)} %shard_map.64.partial, bf16[576,512]{1,0:T(8,128)(2,1)S(1)} %collective-permute-done.10.direct, bf16[576,512]{1,0:T(8,128)(2,1)S(1)} %collective-permute-done.11.swapped, f32[8,64,512]{2,1,0:T(8,128)S(1)} %shard_map.59.rest_0_.noise, ...), custom_call_target="tpu_custom_call" | custom-call | flops 268435456 | bytes 1048576 | tf_op jit(solution)/shard_map/pallas_call | solution.py:452
  47.8 1.9 %shard_map.66 = f32[512,512]{1,0:T(8,128)} custom-call(f32[512,512]{1,0:T(8,128)S(1)} %shard_map.65.partial, bf16[576,512]{1,0:T(8,128)(2,1)S(1)} %collective-permute-done.10.direct, bf16[576,512]{1,0:T(8,128)(2,1)S(1)} %collective-permute-done.11.swapped, f32[8,64,512]{2,1,0:T(8,128)S(1)} %shard_map.60.rest_3_.noise, ...), custom_call_target="tpu_custom_call" | custom-call | flops 268435456 | bytes 1048576 | tf_op jit(solution)/shard_map/pallas_call | solution.py:452
  (22 shorter events, 0.7 us)
Async XLA Ops:
  0.0 25.4 %copy-start.1 = (s32[64]{0:T(128)S(1)}, s32[64]{0:T(128)}, u32[]{:S(2)}) copy-start(s32[64]{0:T(128)} %param.8) | copy-start | bytes 772
  0.0 25.4 %copy-start.2 = (s32[64]{0:T(128)S(1)}, s32[64]{0:T(128)}, u32[]{:S(2)}) copy-start(s32[64]{0:T(128)} %param.9) | copy-start | bytes 772
  0.0 1.7 %collective-permute-start = (f32[8,512]{1,0:T(8,128)}, f32[8,512]{1,0:T(8,128)S(1)}, u32[]{:S(2)}, u32[]{:S(2)}) collective-permute-start(f32[8,512]{1,0:T(8,128)} %coup.1), channel_id=1, source_target_pairs={{0,4},{4,0},{8,12},{12,8},{16,20},{20,16},{24,28},{28,24},{1,5},{5... | collective-permute-start | bytes 49160 | tf_op jit(solution)/shard_map/ppermute | solution.py:38
  2.0 14.1 %collective-permute-start.10 = (bf16[576,512]{1,0:T(8,128)(2,1)S(1)}, bf16[576,512]{1,0:T(8,128)(2,1)S(1)}, u32[]{:S(2)}, u32[]{:S(2)}) collective-permute-start(bf16[576,512]{1,0:T(8,128)(2,1)S(1)} %get-tuple-element.30), channel_id=1, source_target_pairs={{0,1},{1,0},{2,3},{3,2},{4,6},{5,7},{6,4},{7,5},{8,9},{9,8},{10,11... | collective-permute-start | bytes 1769480 | tf_op jit(solution)/shard_map/ppermute | solution.py:33
  4.7 16.4 %collective-permute-start.7 = (bf16[320,512]{1,0:T(8,128)(2,1)S(1)}, bf16[320,512]{1,0:T(8,128)(2,1)S(1)}, u32[]{:S(2)}, u32[]{:S(2)}) collective-permute-start(bf16[320,512]{1,0:T(8,128)(2,1)S(1)} %get-tuple-element.29), channel_id=1, source_target_pairs={{0,3},{1,2},{2,1},{3,0},{4,7},{5,6},{6,5},{7,4},{8,11},{9,10},{10,... | collective-permute-start | bytes 983048 | tf_op jit(solution)/shard_map/ppermute | solution.py:33
  16.0 30.8 %collective-permute-start.11 = (bf16[576,512]{1,0:T(8,128)(2,1)S(1)}, bf16[576,512]{1,0:T(8,128)(2,1)S(1)}, u32[]{:S(2)}, u32[]{:S(2)}) collective-permute-start(bf16[576,512]{1,0:T(8,128)(2,1)S(1)} %collective-permute-done.10.direct), channel_id=1, source_target_pairs={{0,4},{4,0},{8,12},{12,8},{16,20},{20,16},{24,28},{28,24},{1,5},{5... | collective-permute-start | bytes 1769480 | tf_op jit(solution)/shard_map/ppermute | solution.py:38
  21.0 24.9 %collective-permute-start.8 = (bf16[320,512]{1,0:T(8,128)(2,1)S(1)}, bf16[320,512]{1,0:T(8,128)(2,1)S(1)}, u32[]{:S(2)}, u32[]{:S(2)}) collective-permute-start(bf16[320,512]{1,0:T(8,128)(2,1)S(1)} %collective-permute-done.7.direct), channel_id=1, source_target_pairs={{0,4},{4,0},{8,12},{12,8},{16,20},{20,16},{24,28},{28,24},{1,5},{5... | collective-permute-start | bytes 983048 | tf_op jit(solution)/shard_map/ppermute | solution.py:38
  21.0 7.8 %collective-permute-start.1 = (f32[8,512]{1,0:T(8,128)S(1)}, f32[8,512]{1,0:T(8,128)S(1)}, u32[]{:S(2)}, u32[]{:S(2)}) collective-permute-start(f32[8,512]{1,0:T(8,128)S(1)} %get-tuple-element.22.rest_0_.table), channel_id=1, source_target_pairs={{0,8},{4,12},{8,0},{12,4},{16,24},{20,28},{24,16},{28,20},{1,9},{5... | collective-permute-start | bytes 49160 | tf_op jit(solution)/shard_map/ppermute | solution.py:38
  22.6 6.2 %collective-permute-start.2 = (f32[8,512]{1,0:T(8,128)S(1)}, f32[8,512]{1,0:T(8,128)S(1)}, u32[]{:S(2)}, u32[]{:S(2)}) collective-permute-start(f32[8,512]{1,0:T(8,128)S(1)} %get-tuple-element.22.rest_0_.table), channel_id=1, source_target_pairs={{0,16},{4,20},{8,24},{12,28},{16,0},{20,4},{24,8},{28,12},{1,17},{... | collective-permute-start | bytes 49160 | tf_op jit(solution)/shard_map/ppermute | solution.py:38
  25.2 5.5 %collective-permute-start.3 = (f32[8,512]{1,0:T(8,128)S(1)}, f32[8,512]{1,0:T(8,128)S(1)}, u32[]{:S(2)}, u32[]{:S(2)}) collective-permute-start(f32[8,512]{1,0:T(8,128)S(1)} %get-tuple-element.22.rest_0_.table), channel_id=1, source_target_pairs={{0,24},{4,28},{8,16},{12,20},{16,8},{20,12},{24,0},{28,4},{1,25},{... | collective-permute-start | bytes 49160 | tf_op jit(solution)/shard_map/ppermute | solution.py:38
  31.3 8.0 %collective-permute-start.4 = (bf16[64,512]{1,0:T(8,128)(2,1)S(1)}, bf16[64,512]{1,0:T(8,128)(2,1)S(1)}, u32[]{:S(2)}, u32[]{:S(2)}) collective-permute-start(bf16[64,512]{1,0:T(8,128)(2,1)S(1)} %get-tuple-element.28.rest_0_), channel_id=1, source_target_pairs={{0,8},{4,12},{8,0},{12,4},{16,24},{20,28},{24,16},{28,20},{1,9},{5... | collective-permute-start | bytes 196616 | tf_op jit(solution)/shard_map/ppermute | solution.py:38
  31.3 7.9 %collective-permute-start.5 = (bf16[64,512]{1,0:T(8,128)(2,1)S(1)}, bf16[64,512]{1,0:T(8,128)(2,1)S(1)}, u32[]{:S(2)}, u32[]{:S(2)}) collective-permute-start(bf16[64,512]{1,0:T(8,128)(2,1)S(1)} %get-tuple-element.28.rest_0_), channel_id=1, source_target_pairs={{0,16},{4,20},{8,24},{12,28},{16,0},{20,4},{24,8},{28,12},{1,17},{... | collective-permute-start | bytes 196616 | tf_op jit(solution)/shard_map/ppermute | solution.py:38
  33.6 6.1 %collective-permute-start.6 = (bf16[64,512]{1,0:T(8,128)(2,1)S(1)}, bf16[64,512]{1,0:T(8,128)(2,1)S(1)}, u32[]{:S(2)}, u32[]{:S(2)}) collective-permute-start(bf16[64,512]{1,0:T(8,128)(2,1)S(1)} %get-tuple-element.28.rest_0_), channel_id=1, source_target_pairs={{0,24},{4,28},{8,16},{12,20},{16,8},{20,12},{24,0},{28,4},{1,25},{... | collective-permute-start | bytes 196616 | tf_op jit(solution)/shard_map/ppermute | solution.py:38
  37.5 7.6 %copy-start = (bf16[2048,512]{1,0:T(8,128)(2,1)S(1)}, bf16[2048,512]{1,0:T(8,128)(2,1)}, u32[]{:S(2)}) copy-start(bf16[2048,512]{1,0:T(8,128)(2,1)} %basis.3) | copy-start | bytes 6291460
  39.8 6.1 %collective-permute-start.9 = (bf16[80,512]{1,0:T(8,128)(2,1)S(1)}, bf16[80,512]{1,0:T(8,128)(2,1)S(1)}, u32[]{:S(2)}, u32[]{:S(2)}) collective-permute-start(bf16[80,512]{1,0:T(8,128)(2,1)S(1)} %shard_map.61.message.rest_0_), channel_id=1, source_target_pairs={{0,3},{1,2},{2,1},{3,0},{4,7},{5,6},{6,5},{7,4},{8,11},{9,10},{10,... | collective-permute-start | bytes 245768 | tf_op jit(solution)/shard_map/ppermute | solution.py:38
  41.3 5.6 %collective-permute-start.12 = (bf16[80,512]{1,0:T(8,128)(2,1)S(1)}, bf16[80,512]{1,0:T(8,128)(2,1)S(1)}, u32[]{:S(2)}, u32[]{:S(2)}) collective-permute-start(bf16[80,512]{1,0:T(8,128)(2,1)S(1)} %shard_map.61.message.rest_0_), channel_id=1, source_target_pairs={{0,1},{1,0},{2,3},{3,2},{4,5},{5,4},{6,7},{7,6},{8,9},{9,8},{10,11... | collective-permute-start | bytes 245768 | tf_op jit(solution)/shard_map/ppermute | solution.py:38
  41.8 6.0 %collective-permute-start.13 = (bf16[80,512]{1,0:T(8,128)(2,1)S(1)}, bf16[80,512]{1,0:T(8,128)(2,1)S(1)}, u32[]{:S(2)}, u32[]{:S(2)}) collective-permute-start(bf16[80,512]{1,0:T(8,128)(2,1)S(1)} %shard_map.61.message.rest_0_), channel_id=1, source_target_pairs={{0,2},{1,3},{2,0},{3,1},{4,6},{5,7},{6,4},{7,5},{8,10},{9,11},{10,... | collective-permute-start | bytes 245768 | tf_op jit(solution)/shard_map/ppermute | solution.py:38

commit v4 on v3

--- a/solution.py
+++ b/solution.py
@@ -140,9 +140,30 @@
         copies.append(pltpu.make_async_copy(tail, message.at[pl.ds(rows, TAIL), :], sems.at[i]))
         copies[-1].start()
     early, late = ordered(first, totals(coup), totals(other))
-    out[...] = table_rows(out.shape, (*joined(early, late), *early, *late))
+    total = joined(early, late)
+    out[...] = table_rows(out.shape, (*total, *early, *late, 1.0 + total[1], total[0] * total[0]))
     for copy in copies:
         copy.wait()
+
+
+def sums_kernel(tm_axis, table, *rest):
+    *received, out = rest
+    start = start_of(tm_axis, received, out.shape[1])
+    total = table[pl.ds(0, 1), :], table[pl.ds(1, 1), :]
+    out[...] = table_rows(out.shape, (one_row(out), ) * 6 + after(start, total))
+
+
+def one_row(ref):
+    return jnp.ones((1, ref.shape[1]), F32)
+
+
+def start_of(tm_axis, received, modes):
+    chip = lax.axis_index(tm_axis) // 2
+    one = jnp.ones((1, modes), F32)
+    start = (one, one)
+    for r, ref in enumerate(received):
+        start = select(chip == r + 1, (ref[pl.ds(6, 1), :], ref[pl.ds(7, 1), :]), start)
+    return start
 
 
 def noise_kernel(tm_axis, sp_axis, blocks, extras, keys, counters, *rest):
@@ -204,24 +225,11 @@
 
 
 def offset_kernel(tm_axis, noise_own, noise_other, coup, coup_other, spec, table, *rest):
-    received, rest = rest[:-10], rest[-10:]
-    o_ref, late_ref, wts, df, tables, *coefs, tmp = rest
+    received, rest = rest[:-8], rest[-8:]
+    o_ref, late_ref, df, *coefs, tmp = rest
     steps, vecs, modes = noise_own.shape
-    me = lax.axis_index(tm_axis)
-    chip = me // 2
-    first = lax.rem(me, 2) == 0
-    one = jnp.ones((1, modes), F32)
-    tables[chip] = table[...]
-    for e, ref in enumerate(received):
-        tables[chip ^ (e + 1)] = ref[...]
-    now, start, weight = (one, one), (one, one), jnp.zeros((1, modes), F32)
-    for b in range(tables.shape[0]):
-        wts[b] = jnp.broadcast_to(weight, (8, modes))
-        total = tables[b, pl.ds(0, 1), :], tables[b, pl.ds(1, 1), :]
-        here = chip == b
-        start = select(here, now, start)
-        weight = jnp.where(here, 1.0, weight * gain_of(now, total))
-        now = after(now, total)
+    first = lax.rem(lax.axis_index(tm_axis), 2) == 0
+    start = start_of(tm_axis, received, modes)
     early = table[pl.ds(2, 1), :], table[pl.ds(3, 1), :]
     late = table[pl.ds(4, 1), :], table[pl.ds(5, 1), :]
     second = after(start, early)
@@ -250,16 +258,17 @@
         return 0
 
     lax.fori_loop(0, vecs // 16, tile, 0)
-
-
-def carry_kernel(tm_axis, late, wts, df, *rest):
+    o_ref[pl.ds(vecs, 16), :] = table_rows((16, modes), split3(gain_early * gain_late)).astype(BF16)
+
+
+def carry_kernel(tm_axis, late, df, *rest):
     *received, _, out = rest
     vecs, modes = late.shape
-    me = lax.axis_index(tm_axis)
-    first = lax.rem(me, 2) == 0
+    first = lax.rem(lax.axis_index(tm_axis), 2) == 0
     carry = jnp.zeros(late.shape, F32)
-    for e, ref in enumerate(received):
-        carry = carry + wts[(me // 2) ^ (e + 1)][0:1, :] * ref[...].astype(F32)
+    for ref in received[::-1]:
+        gain = ref[pl.ds(vecs, 16), :].astype(F32)
+        carry = ref[pl.ds(0, vecs), :].astype(F32) + (gain[0:1] + gain[1:2] + gain[2:3]) * carry
     out[pl.ds(0, vecs), :] = jnp.where(first, late[...] + df[pl.ds(4, 1), :] * carry, carry).astype(BF16)
     own = select(first, (df[pl.ds(0, 1), :], df[pl.ds(1, 1), :]), (df[pl.ds(2, 1), :], df[pl.ds(3, 1), :]))
     out[pl.ds(vecs, 16), :] = table_rows((16, modes), split3(own[0]) + split3(own[1])).astype(BF16)
@@ -389,7 +398,6 @@
         input_output_aliases={3 + i: 1 + i for i in range(len(sizes))},
         **fast,
     )(coup, other, spec, *messages)
-    tables = [swap(table, "tm", 2 * e) for e in range(1, chips)]
     direct = [exchange(m, lambda t, s, r=r: (t, s ^ r[t % 2])) for m, r in zip(messages, routes)]
 
     def noise_of(blocks, after):
@@ -404,30 +412,45 @@
             **fast,
         )(keys, counters, *after)
 
-    own, paired = noise_of(((0, 0), (1, 0)), (table,))
-    total, late, weights, sums = kernel_call(
+    received, chip_noise, message = [], [], table
+    for r in range(chips - 1):
+        received.append(exchange(message, lambda t, s: (t + 2, s) if t // 2 == r else None))
+        if 1 <= r <= 2:
+            chip_noise += noise_of([(r - 1, 0)], (message,))
+        if r < chips - 2:
+            message = kernel_call(
+                functools.partial(sums_kernel, "tm"),
+                out_shape=f32(8, modes),
+                in_specs=[VMEM] * (1 + len(received)),
+                out_specs=VMEM,
+                **fast,
+            )(table, *received)
+    for r in range(len(chip_noise), 2):
+        chip_noise += noise_of([(r, 0)], (message,))
+    own, paired = chip_noise
+    total, late, sums = kernel_call(
         functools.partial(offset_kernel, "tm"),
-        out_shape=[bf16(vecs, modes), f32(vecs, modes), f32(chips, 8, modes), f32(8, modes)],
-        in_specs=[VMEM] * (6 + len(tables)),
-        out_specs=[VMEM] * 4,
-        scratch_shapes=[pltpu.VMEM((chips, 8, modes), F32)] + [pltpu.VMEM((steps, modes), F32)] * 5,
+        out_shape=[bf16(vecs + 16, modes), f32(vecs, modes), f32(8, modes)],
+        in_specs=[VMEM] * (6 + len(received)),
+        out_specs=[VMEM] * 3,
+        scratch_shapes=[pltpu.VMEM((steps, modes), F32)] * 5,
         **fast,
-    )(own, paired, coup, other, spec, table, *tables)
-    later = [swap(total, "tm", 2 * e) for e in range(1, chips)]
+    )(own, paired, coup, other, spec, table, *received)
+    later = [exchange(total, lambda t, s: (t - 2 * e, s) if t >= 2 * e else None) for e in range(1, chips)]
     third = max(1, (space - 1) // 3)
     parts = [range(1, 1 + third), range(1 + third, 1 + 2 * third), range(1 + 2 * third, space)]
     noise = list(noise_of([(0, d) for d in parts[0]], (total,)))
     noise += noise_of([(0, d) for d in parts[1]], (noise[-1],))
+    noise += noise_of([(0, d) for d in parts[2]], (noise[-1],))
     carry = kernel_call(
         functools.partial(carry_kernel, "tm"),
         out_shape=bf16(vecs + 16, modes),
-        in_specs=[VMEM] * (3 + len(later)) + [ANY],
+        in_specs=[VMEM] * (2 + len(later)) + [ANY],
         out_specs=VMEM,
         **fast,
-    )(late, weights, sums, *later, noise[-1])
+    )(late, sums, *later, noise[-1])
     carries = [swap(carry, "space", d) for d in range(1, space)]
     swapped = [swap(m, "tm", 1) for m in direct]
-    noise += noise_of([(0, d) for d in parts[2]], (carry,))
 
     flops = 2 * nodes_here * modes * steps * vecs
     lhs, rhs = pltpu.VMEM((nodes_here, modes), BF16), pltpu.VMEM((steps * vecs, modes), BF16)

time: 49.9 us -> 56.5 us (1.13)
  waiting for transfers between devices: 17.2 us -> 23.6 us
    ppermute x12 -> x6, starting transfers between devices: 12.9 us -> 4.05 us  [swap(): return lax.ppermute(x, axis, [(i, i ^ offset) for i in range(count)])]
    ppermute x2 -> x8, starting transfers between devices: 4.21 us -> 12.9 us  [exchange(): return lax.ppermute(x, ('tm', 'space'), moves)]
    ppermute x2 -> x8, waiting for transfers between devices: 14.9 us -> 22.5 us  [exchange(): return lax.ppermute(x, ('tm', 'space'), moves)]
    ppermute x12 -> x6, waiting for transfers between devices: 2.36 us -> 1.02 us  [swap(): return lax.ppermute(x, axis, [(i, i ^ offset) for i in range(count)])]
    pallas_call x4 -> x5, Pallas kernels: 8.62 us -> 8.72 us  [noise_of(): kernel_call(functools.partial(noise_kernel, 'tm', 'space', blocks, len(af...]
  transfers between devices with their start and end apart: 14 -> 14, of which waited for: 4 -> 5; matrix products, arithmetic and copies ran while one was open for 0% -> 0% of each run, Pallas kernels for 26% -> 24%
where the time goes in v4:
time: 56.5 us; the launch traced here: 56.2 us
  waiting for transfers between devices  23.6 us (42%)
  starting transfers between devices  16.9 us (30%)
  Pallas kernels  15.5 us (27%)
    ppermute x8, waiting for transfers between devices, exchange(): return lax.ppermute(x, ('tm', 'space'), moves)  22.5 us
    ppermute x8, starting transfers between devices, exchange(): return lax.ppermute(x, ('tm', 'space'), moves)  12.9 us
    pallas_call x5, Pallas kernels, noise_of(): kernel_call(functools.partial(noise_kernel, 'tm', 'space', blocks, len(af...  8.72 us
    ppermute x6, starting transfers between devices, swap(): return lax.ppermute(x, axis, [(i, i ^ offset) for i in range(count)])  4.05 us
    pallas_call x3, Pallas kernels, local(): kernel_call(functools.partial(block_kernel, 'tm', place, last), out_shape...  3.86 us
    pallas_call x1, Pallas kernels, local(): kernel_call(functools.partial(pack_kernel, 'tm', 'space', routes), out_sh...  1.19 us
  transfers between devices with their start and end apart: 14, of which 5 were waited for; matrix products, arithmetic and copies ran while one was open for 0% of the time, Pallas kernels for 24%

profile of v4, /device:TPU:0, one launch (start us, length us, event | category | flops | bytes accessed | tf_op | source)
XLA Modules:
  0.0 56.2 jit_solution(8690170894520057056)
XLA Ops:
  0.5 1.2 %shard_map.55 = (bf16[320,512]{1,0:T(8,128)(2,1)S(1)}, bf16[576,512]{1,0:T(8,128)(2,1)S(1)}, f32[8,512]{1,0:T(8,128)S(1)}, f32[1,512]{1,0:T(1,128)S(1)}) custom-call(f32[8,512]{1,0:T(8,128)} %coup.1, f32[1,512]{1,0:T(1,128)} %bitcast.13, bf16[2048,512]{1,0:T(8,128)(2,1)} %basis.3), custom_call_target="tpu_custom_call" | custom-call | tf_op jit(solution)/shard_map/pallas_call | solution.py:384
  2.0 2.7 %collective-permute-start.10 = (bf16[576,512]{1,0:T(8,128)(2,1)S(1)}, bf16[576,512]{1,0:T(8,128)(2,1)S(1)}, u32[]{:S(2)}, u32[]{:S(2)}) collective-permute-start(bf16[576,512]{1,0:T(8,128)(2,1)S(1)} %get-tuple-element.24), channel_id=1, source_target_pairs={{0,1},{1,0},{2,3},{3,2},{4,6},{5,7},{6,4},{7,5},{8,9},{9,8},{10,11... | collective-permute-start | bytes 1769480 | tf_op jit(solution)/shard_map/ppermute | solution.py:33
  4.7 1.5 %collective-permute-start.7 = (bf16[320,512]{1,0:T(8,128)(2,1)S(1)}, bf16[320,512]{1,0:T(8,128)(2,1)S(1)}, u32[]{:S(2)}, u32[]{:S(2)}) collective-permute-start(bf16[320,512]{1,0:T(8,128)(2,1)S(1)} %get-tuple-element.23), channel_id=1, source_target_pairs={{0,3},{1,2},{2,1},{3,0},{4,7},{5,6},{6,5},{7,4},{8,11},{9,10},{10,... | collective-permute-start | bytes 983048 | tf_op jit(solution)/shard_map/ppermute | solution.py:33
  6.2 9.9 %collective-permute-done.10.direct = bf16[576,512]{1,0:T(8,128)(2,1)S(1)} collective-permute-done((bf16[576,512]{1,0:T(8,128)(2,1)S(1)}, bf16[576,512]{1,0:T(8,128)(2,1)S(1)}, u32[]{:S(2)}, u32[]{:S(2)}) %collective-permute-start.10) | collective-permute-done | bytes 589856 | tf_op jit(solution)/shard_map/ppermute | solution.py:33
  16.1 5.0 %collective-permute-done.7.direct = bf16[320,512]{1,0:T(8,128)(2,1)S(1)} collective-permute-done((bf16[320,512]{1,0:T(8,128)(2,1)S(1)}, bf16[320,512]{1,0:T(8,128)(2,1)S(1)}, u32[]{:S(2)}, u32[]{:S(2)}) %collective-permute-start.7) | collective-permute-done | bytes 327712 | tf_op jit(solution)/shard_map/ppermute | solution.py:33
  21.1 3.5 %collective-permute-start.1 = (f32[8,512]{1,0:T(8,128)S(1)}, f32[8,512]{1,0:T(8,128)S(1)}, u32[]{:S(2)}, u32[]{:S(2)}) collective-permute-start(f32[8,512]{1,0:T(8,128)S(1)} %get-tuple-element.19.table), channel_id=1, source_target_pairs={{0,8},{1,9},{2,10},{3,11},{4,12},{5,13},{6,14},{7,15}} | collective-permute-start | bytes 49160 | tf_op jit(solution)/shard_map/ppermute | solution.py:33
  24.5 1.4 %collective-permute-done.1.rest_0_ = f32[8,512]{1,0:T(8,128)S(1)} collective-permute-done((f32[8,512]{1,0:T(8,128)S(1)}, f32[8,512]{1,0:T(8,128)S(1)}, u32[]{:S(2)}, u32[]{:S(2)}) %collective-permute-start.1) | collective-permute-done | bytes 16416 | tf_op jit(solution)/shard_map/ppermute | solution.py:33
  26.7 0.7 %collective-permute-start.3 = (f32[8,512]{1,0:T(8,128)S(1)}, f32[8,512]{1,0:T(8,128)S(1)}, u32[]{:S(2)}, u32[]{:S(2)}) collective-permute-start(f32[8,512]{1,0:T(8,128)S(1)} %shard_map.59.rest_0_), channel_id=1, source_target_pairs={{16,24},{17,25},{18,26},{19,27},{20,28},{21,29},{22,30},{23,31}} | collective-permute-start | bytes 49160 | tf_op jit(solution)/shard_map/ppermute | solution.py:33
  27.4 1.7 %shard_map.58.noise_own.noise = f32[8,64,512]{2,1,0:T(8,128)S(1)} custom-call(s32[1,64]{1,0:T(1,128)S(1)} %bitcast.3, s32[1,64]{1,0:T(1,128)S(1)} %bitcast.8, f32[8,512]{1,0:T(8,128)S(1)} %shard_map.57.rest_0_), custom_call_target="tpu_custom_call" | custom-call | flops 15728640 | bytes 1048576 | tf_op jit(solution)/shard_map/pallas_call | solution.py:405
  29.1 1.7 %shard_map.60.noise_other = f32[8,64,512]{2,1,0:T(8,128)S(1)} custom-call(s32[1,64]{1,0:T(1,128)S(1)} %bitcast.4, s32[1,64]{1,0:T(1,128)S(1)} %bitcast.9, f32[8,512]{1,0:T(8,128)S(1)} %shard_map.59.rest_0_), custom_call_target="tpu_custom_call" | custom-call | flops 15728640 | bytes 1048576 | tf_op jit(solution)/shard_map/pallas_call | solution.py:405
  31.4 1.3 %collective-permute-start.4 = (bf16[80,512]{1,0:T(8,128)(2,1)S(1)}, bf16[80,512]{1,0:T(8,128)(2,1)S(1)}, u32[]{:S(2)}, u32[]{:S(2)}) collective-permute-start(bf16[80,512]{1,0:T(8,128)(2,1)S(1)} %get-tuple-element.22.rest_0_), channel_id=1, source_target_pairs={{8,0},{9,1},{10,2},{11,3},{12,4},{13,5},{14,6},{15,7},{16,8},{17,9... | collective-permute-start | bytes 245768 | tf_op jit(solution)/shard_map/ppermute | solution.py:33
  32.7 1.3 %collective-permute-start.5 = (bf16[80,512]{1,0:T(8,128)(2,1)S(1)}, bf16[80,512]{1,0:T(8,128)(2,1)S(1)}, u32[]{:S(2)}, u32[]{:S(2)}) collective-permute-start(bf16[80,512]{1,0:T(8,128)(2,1)S(1)} %get-tuple-element.22.rest_0_), channel_id=1, source_target_pairs={{16,0},{17,1},{18,2},{19,3},{20,4},{21,5},{22,6},{23,7},{24,8},{25... | collective-permute-start | bytes 245768 | tf_op jit(solution)/shard_map/ppermute | solution.py:33
  34.0 1.3 %collective-permute-start.6 = (bf16[80,512]{1,0:T(8,128)(2,1)S(1)}, bf16[80,512]{1,0:T(8,128)(2,1)S(1)}, u32[]{:S(2)}, u32[]{:S(2)}) collective-permute-start(bf16[80,512]{1,0:T(8,128)(2,1)S(1)} %get-tuple-element.22.rest_0_), channel_id=1, source_target_pairs={{24,0},{25,1},{26,2},{27,3},{28,4},{29,5},{30,6},{31,7}} | collective-permute-start | bytes 245768 | tf_op jit(solution)/shard_map/ppermute | solution.py:33
  35.3 1.7 %shard_map.62.rest_0_.noise = f32[8,64,512]{2,1,0:T(8,128)S(1)} custom-call(s32[1,64]{1,0:T(1,128)S(1)} %bitcast.5, s32[1,64]{1,0:T(1,128)S(1)} %bitcast.10, bf16[80,512]{1,0:T(8,128)(2,1)S(1)} %get-tuple-element.22.rest_0_), custom_call_target="tpu_custom_call" | custom-call | flops 15728640 | bytes 1048576 | tf_op jit(solution)/shard_map/pallas_call | solution.py:405
  37.1 1.7 %shard_map.63.rest_0_.noise = f32[8,64,512]{2,1,0:T(8,128)S(1)} custom-call(s32[1,64]{1,0:T(1,128)S(1)} %bitcast.6, s32[1,64]{1,0:T(1,128)S(1)} %bitcast.11, f32[8,64,512]{2,1,0:T(8,128)S(1)} %shard_map.62.rest_0_.noise), custom_call_target="tpu_custom_call" | custom-call | flops 15728640 | bytes 1048576 | tf_op jit(solution)/shard_map/pallas_call | solution.py:405
  38.8 1.7 %shard_map.64.rest_3_.noise = f32[8,64,512]{2,1,0:T(8,128)S(1)} custom-call(s32[1,64]{1,0:T(1,128)S(1)} %bitcast.7, s32[1,64]{1,0:T(1,128)S(1)} %bitcast.12, f32[8,64,512]{2,1,0:T(8,128)S(1)} %shard_map.63.rest_0_.noise), custom_call_target="tpu_custom_call" | custom-call | flops 15728640 | bytes 1048576 | tf_op jit(solution)/shard_map/pallas_call | solution.py:405
  40.6 6.2 %collective-permute-done.5.rest_1_ = bf16[80,512]{1,0:T(8,128)(2,1)S(1)} collective-permute-done((bf16[80,512]{1,0:T(8,128)(2,1)S(1)}, bf16[80,512]{1,0:T(8,128)(2,1)S(1)}, u32[]{:S(2)}, u32[]{:S(2)}) %collective-permute-start.5) | collective-permute-done | bytes 81952 | tf_op jit(solution)/shard_map/ppermute | solution.py:33
  46.9 1.5 %collective-permute-start.9 = (bf16[80,512]{1,0:T(8,128)(2,1)S(1)}, bf16[80,512]{1,0:T(8,128)(2,1)S(1)}, u32[]{:S(2)}, u32[]{:S(2)}) collective-permute-start(bf16[80,512]{1,0:T(8,128)(2,1)S(1)} %shard_map.65.message), channel_id=1, source_target_pairs={{0,3},{1,2},{2,1},{3,0},{4,7},{5,6},{6,5},{7,4},{8,11},{9,10},{10,... | collective-permute-start | bytes 245768 | tf_op jit(solution)/shard_map/ppermute | solution.py:38
  48.9 1.5 %collective-permute-start.13 = (bf16[80,512]{1,0:T(8,128)(2,1)S(1)}, bf16[80,512]{1,0:T(8,128)(2,1)S(1)}, u32[]{:S(2)}, u32[]{:S(2)}) collective-permute-start(bf16[80,512]{1,0:T(8,128)(2,1)S(1)} %shard_map.65.message), channel_id=1, source_target_pairs={{0,2},{1,3},{2,0},{3,1},{4,6},{5,7},{6,4},{7,5},{8,10},{9,11},{10,... | collective-permute-start | bytes 245768 | tf_op jit(solution)/shard_map/ppermute | solution.py:38
  50.5 0.8 %shard_map.66.partial = f32[512,512]{1,0:T(8,128)S(1)} custom-call(f32[8,512]{1,0:T(8,128)S(1)} %get-tuple-element.15.coup, f32[1,512]{1,0:T(1,128)S(1)} %get-tuple-element.16.spec, bf16[2048,512]{1,0:T(8,128)(2,1)S(1)} %copy-done, f32[8,64,512]{2,1,0:T(8,128)S(1)} %shard_map.58.noise_own.noise, bf16[80,512]{1,0:T(8,128)(2,1)S(1)} %shard_map.65.message), custom_call_target="tpu_custom_call" | custom-call | flops 268435456 | bytes 1048576 | tf_op jit(solution)/shard_map/pallas_call | solution.py:460
  51.3 1.0 %collective-permute-done.9.message = bf16[80,512]{1,0:T(8,128)(2,1)S(1)} collective-permute-done((bf16[80,512]{1,0:T(8,128)(2,1)S(1)}, bf16[80,512]{1,0:T(8,128)(2,1)S(1)}, u32[]{:S(2)}, u32[]{:S(2)}) %collective-permute-start.9) | collective-permute-done | bytes 81952 | tf_op jit(solution)/shard_map/ppermute | solution.py:38
  52.3 0.9 %shard_map.67.partial = f32[512,512]{1,0:T(8,128)S(1)} custom-call(f32[512,512]{1,0:T(8,128)S(1)} %shard_map.66.partial, bf16[320,512]{1,0:T(8,128)(2,1)S(1)} %collective-permute-done.7.direct, bf16[320,512]{1,0:T(8,128)(2,1)S(1)} %collective-permute-done.8.swapped, f32[8,64,512]{2,1,0:T(8,128)S(1)} %shard_map.64.rest_3_.noise, ...), custom_call_target="tpu_custom_call" | custom-call | flops 268435456 | bytes 1048576 | tf_op jit(solution)/shard_map/pallas_call | solution.py:475
  53.3 1.0 %shard_map.68.partial = f32[512,512]{1,0:T(8,128)S(1)} custom-call(f32[512,512]{1,0:T(8,128)S(1)} %shard_map.67.partial, bf16[576,512]{1,0:T(8,128)(2,1)S(1)} %collective-permute-done.10.direct, bf16[576,512]{1,0:T(8,128)(2,1)S(1)} %collective-permute-done.11.swapped, f32[8,64,512]{2,1,0:T(8,128)S(1)} %shard_map.62.rest_0_.noise, ...), custom_call_target="tpu_custom_call" | custom-call | flops 268435456 | bytes 1048576 | tf_op jit(solution)/shard_map/pallas_call | solution.py:475
  54.3 1.9 %shard_map.69 = f32[512,512]{1,0:T(8,128)} custom-call(f32[512,512]{1,0:T(8,128)S(1)} %shard_map.68.partial, bf16[576,512]{1,0:T(8,128)(2,1)S(1)} %collective-permute-done.10.direct, bf16[576,512]{1,0:T(8,128)(2,1)S(1)} %collective-permute-done.11.swapped, f32[8,64,512]{2,1,0:T(8,128)S(1)} %shard_map.63.rest_0_.noise, ...), custom_call_target="tpu_custom_call" | custom-call | flops 268435456 | bytes 1048576 | tf_op jit(solution)/shard_map/pallas_call | solution.py:475
  (25 shorter events, 2.6 us)
Async XLA Ops:
  0.0 27.4 %copy-start.1 = (s32[64]{0:T(128)S(1)}, s32[64]{0:T(128)}, u32[]{:S(2)}) copy-start(s32[64]{0:T(128)} %param.8) | copy-start | bytes 772
  0.0 27.4 %copy-start.2 = (s32[64]{0:T(128)S(1)}, s32[64]{0:T(128)}, u32[]{:S(2)}) copy-start(s32[64]{0:T(128)} %param.9) | copy-start | bytes 772
  0.0 1.7 %collective-permute-start = (f32[8,512]{1,0:T(8,128)}, f32[8,512]{1,0:T(8,128)S(1)}, u32[]{:S(2)}, u32[]{:S(2)}) collective-permute-start(f32[8,512]{1,0:T(8,128)} %coup.1), channel_id=1, source_target_pairs={{0,4},{4,0},{8,12},{12,8},{16,20},{20,16},{24,28},{28,24},{1,5},{5... | collective-permute-start | bytes 49160 | tf_op jit(solution)/shard_map/ppermute | solution.py:38
  2.0 14.1 %collective-permute-start.10 = (bf16[576,512]{1,0:T(8,128)(2,1)S(1)}, bf16[576,512]{1,0:T(8,128)(2,1)S(1)}, u32[]{:S(2)}, u32[]{:S(2)}) collective-permute-start(bf16[576,512]{1,0:T(8,128)(2,1)S(1)} %get-tuple-element.24), channel_id=1, source_target_pairs={{0,1},{1,0},{2,3},{3,2},{4,6},{5,7},{6,4},{7,5},{8,9},{9,8},{10,11... | collective-permute-start | bytes 1769480 | tf_op jit(solution)/shard_map/ppermute | solution.py:33
  4.7 16.4 %collective-permute-start.7 = (bf16[320,512]{1,0:T(8,128)(2,1)S(1)}, bf16[320,512]{1,0:T(8,128)(2,1)S(1)}, u32[]{:S(2)}, u32[]{:S(2)}) collective-permute-start(bf16[320,512]{1,0:T(8,128)(2,1)S(1)} %get-tuple-element.23), channel_id=1, source_target_pairs={{0,3},{1,2},{2,1},{3,0},{4,7},{5,6},{6,5},{7,4},{8,11},{9,10},{10,... | collective-permute-start | bytes 983048 | tf_op jit(solution)/shard_map/ppermute | solution.py:33
  16.1 37.2 %collective-permute-start.11 = (bf16[576,512]{1,0:T(8,128)(2,1)S(1)}, bf16[576,512]{1,0:T(8,128)(2,1)S(1)}, u32[]{:S(2)}, u32[]{:S(2)}) collective-permute-start(bf16[576,512]{1,0:T(8,128)(2,1)S(1)} %collective-permute-done.10.direct), channel_id=1, source_target_pairs={{0,4},{4,0},{8,12},{12,8},{16,20},{20,16},{24,28},{28,24},{1,5},{5... | collective-permute-start | bytes 1769480 | tf_op jit(solution)/shard_map/ppermute | solution.py:38
  21.0 31.3 %collective-permute-start.8 = (bf16[320,512]{1,0:T(8,128)(2,1)S(1)}, bf16[320,512]{1,0:T(8,128)(2,1)S(1)}, u32[]{:S(2)}, u32[]{:S(2)}) collective-permute-start(bf16[320,512]{1,0:T(8,128)(2,1)S(1)} %collective-permute-done.7.direct), channel_id=1, source_target_pairs={{0,4},{4,0},{8,12},{12,8},{16,20},{20,16},{24,28},{28,24},{1,5},{5... | collective-permute-start | bytes 983048 | tf_op jit(solution)/shard_map/ppermute | solution.py:38
  21.1 4.9 %collective-permute-start.1 = (f32[8,512]{1,0:T(8,128)S(1)}, f32[8,512]{1,0:T(8,128)S(1)}, u32[]{:S(2)}, u32[]{:S(2)}) collective-permute-start(f32[8,512]{1,0:T(8,128)S(1)} %get-tuple-element.19.table), channel_id=1, source_target_pairs={{0,8},{1,9},{2,10},{3,11},{4,12},{5,13},{6,14},{7,15}} | collective-permute-start | bytes 49160 | tf_op jit(solution)/shard_map/ppermute | solution.py:33
  26.0 0.7 %collective-permute-start.2 = (f32[8,512]{1,0:T(8,128)S(1)}, f32[8,512]{1,0:T(8,128)S(1)}, u32[]{:S(2)}, u32[]{:S(2)}) collective-permute-start(f32[8,512]{1,0:T(8,128)S(1)} %shard_map.57.rest_0_), channel_id=1, source_target_pairs={{8,16},{9,17},{10,18},{11,19},{12,20},{13,21},{14,22},{15,23}} | collective-permute-start | bytes 49160 | tf_op jit(solution)/shard_map/ppermute | solution.py:33
  26.7 4.2 %collective-permute-start.3 = (f32[8,512]{1,0:T(8,128)S(1)}, f32[8,512]{1,0:T(8,128)S(1)}, u32[]{:S(2)}, u32[]{:S(2)}) collective-permute-start(f32[8,512]{1,0:T(8,128)S(1)} %shard_map.59.rest_0_), channel_id=1, source_target_pairs={{16,24},{17,25},{18,26},{19,27},{20,28},{21,29},{22,30},{23,31}} | collective-permute-start | bytes 49160 | tf_op jit(solution)/shard_map/ppermute | solution.py:33
  31.4 9.2 %collective-permute-start.4 = (bf16[80,512]{1,0:T(8,128)(2,1)S(1)}, bf16[80,512]{1,0:T(8,128)(2,1)S(1)}, u32[]{:S(2)}, u32[]{:S(2)}) collective-permute-start(bf16[80,512]{1,0:T(8,128)(2,1)S(1)} %get-tuple-element.22.rest_0_), channel_id=1, source_target_pairs={{8,0},{9,1},{10,2},{11,3},{12,4},{13,5},{14,6},{15,7},{16,8},{17,9... | collective-permute-start | bytes 245768 | tf_op jit(solution)/shard_map/ppermute | solution.py:33
  32.7 14.1 %collective-permute-start.5 = (bf16[80,512]{1,0:T(8,128)(2,1)S(1)}, bf16[80,512]{1,0:T(8,128)(2,1)S(1)}, u32[]{:S(2)}, u32[]{:S(2)}) collective-permute-start(bf16[80,512]{1,0:T(8,128)(2,1)S(1)} %get-tuple-element.22.rest_0_), channel_id=1, source_target_pairs={{16,0},{17,1},{18,2},{19,3},{20,4},{21,5},{22,6},{23,7},{24,8},{25... | collective-permute-start | bytes 245768 | tf_op jit(solution)/shard_map/ppermute | solution.py:33
  34.0 12.8 %collective-permute-start.6 = (bf16[80,512]{1,0:T(8,128)(2,1)S(1)}, bf16[80,512]{1,0:T(8,128)(2,1)S(1)}, u32[]{:S(2)}, u32[]{:S(2)}) collective-permute-start(bf16[80,512]{1,0:T(8,128)(2,1)S(1)} %get-tuple-element.22.rest_0_), channel_id=1, source_target_pairs={{24,0},{25,1},{26,2},{27,3},{28,4},{29,5},{30,6},{31,7}} | collective-permute-start | bytes 245768 | tf_op jit(solution)/shard_map/ppermute | solution.py:33
  38.8 11.6 %copy-start = (bf16[2048,512]{1,0:T(8,128)(2,1)S(1)}, bf16[2048,512]{1,0:T(8,128)(2,1)}, u32[]{:S(2)}) copy-start(bf16[2048,512]{1,0:T(8,128)(2,1)} %basis.3) | copy-start | bytes 6291460
  46.9 5.4 %collective-permute-start.9 = (bf16[80,512]{1,0:T(8,128)(2,1)S(1)}, bf16[80,512]{1,0:T(8,128)(2,1)S(1)}, u32[]{:S(2)}, u32[]{:S(2)}) collective-permute-start(bf16[80,512]{1,0:T(8,128)(2,1)S(1)} %shard_map.65.message), channel_id=1, source_target_pairs={{0,3},{1,2},{2,1},{3,0},{4,7},{5,6},{6,5},{7,4},{8,11},{9,10},{10,... | collective-permute-start | bytes 245768 | tf_op jit(solution)/shard_map/ppermute | solution.py:38
  48.4 4.9 %collective-permute-start.12 = (bf16[80,512]{1,0:T(8,128)(2,1)S(1)}, bf16[80,512]{1,0:T(8,128)(2,1)S(1)}, u32[]{:S(2)}, u32[]{:S(2)}) collective-permute-start(bf16[80,512]{1,0:T(8,128)(2,1)S(1)} %shard_map.65.message), channel_id=1, source_target_pairs={{0,1},{1,0},{2,3},{3,2},{4,5},{5,4},{6,7},{7,6},{8,9},{9,8},{10,11... | collective-permute-start | bytes 245768 | tf_op jit(solution)/shard_map/ppermute | solution.py:38
  48.9 5.3 %collective-permute-start.13 = (bf16[80,512]{1,0:T(8,128)(2,1)S(1)}, bf16[80,512]{1,0:T(8,128)(2,1)S(1)}, u32[]{:S(2)}, u32[]{:S(2)}) collective-permute-start(bf16[80,512]{1,0:T(8,128)(2,1)S(1)} %shard_map.65.message), channel_id=1, source_target_pairs={{0,2},{1,3},{2,0},{3,1},{4,6},{5,7},{6,4},{7,5},{8,10},{9,11},{10,... | collective-permute-start | bytes 245768 | tf_op jit(solution)/shard_map/ppermute | solution.py:38

commit v5 on v3

--- a/solution.py
+++ b/solution.py
@@ -13,7 +13,7 @@
 VMEM = pl.BlockSpec(memory_space=pltpu.VMEM)
 ANY = pl.BlockSpec(memory_space=pl.ANY)
 HBM = pl.BlockSpec(memory_space=pltpu.HBM)
-LIMIT = pltpu.CompilerParams(vmem_limit_bytes=48 << 20)
+LIMIT = pltpu.CompilerParams(vmem_limit_bytes=24 << 20)
 SINE = (6.28318516, -41.34165503, 81.60100406, -76.54978208, 39.53670436)
 
 
@@ -162,7 +162,7 @@
     base[...] = jnp.broadcast_to(start, base.shape)
     group = 8
     for out, (block, offset) in zip(outs, blocks):
-        ids = (sp ^ offset) * modes + lax.broadcasted_iota(jnp.int32, (1, modes), 1)
+        ids = (sp ^ pick(lax.rem(me, 2), offset)) * modes + lax.broadcasted_iota(jnp.int32, (1, modes), 1)
         lane = ids * jnp.int32(-1640531535)
         first_step = (me ^ block) * steps
 
@@ -265,86 +265,123 @@
     out[pl.ds(vecs, 16), :] = table_rows((16, modes), split3(own[0]) + split3(own[1])).astype(BF16)
 
 
-def values(noise, message, c, lam, coefs, rhs):
-    steps, vecs, _ = noise.shape
-    df = message[pl.ds(vecs, 16), :].astype(F32)
-    a, ratio = chain(c, lam, df[0:1] + df[1:2] + df[2:3], df[3:4] + df[4:5] + df[5:6])
-    a_ref, ratio_ref, c_ref = coefs
-    a_ref[...] = a
-    ratio_ref[...] = ratio
-    c_ref[...] = c
-
-    def tile(v, _):
-        at = pl.ds(pl.multiple_of(v * 16, 16), 16)
-        carry = message[at, :].astype(F32)
-        for t in range(steps - 1, -1, -1):
-            value = a_ref[pl.ds(t, 1), :] * noise[t, at, :] + ratio_ref[pl.ds(t, 1), :] * carry
+def sums_of(block):
+    return block[0:1] + block[1:2] + block[2:3], block[3:4] + block[4:5] + block[5:6]
+
+
+def set_coefs(coefs, c, lam, sums):
+    a, ratio = chain(c, lam, *sums)
+    coefs[0] = a
+    coefs[1] = ratio
+    coefs[2] = c
+
+
+def values(noise, start, coefs, state, rhs, times):
+    vecs = noise.shape[1]
+    for v in range(0, vecs, 16):
+        at = pl.ds(v, 16)
+        carry = start(at)
+        for n, t in enumerate(times):
+            row = pl.ds(t, 1)
+            value = coefs[0, row, :] * noise[t, at, :] + coefs[1, row, :] * carry
             if t:
-                carry = c_ref[pl.ds(t, 1), :] * value
-            rhs[pl.ds(pl.multiple_of(t * vecs + v * 16, 16), 16), :] = value.astype(BF16)
-        return 0
-
-    lax.fori_loop(0, vecs // 16, tile, 0)
+                carry = coefs[2, row, :] * value
+            rhs[pl.ds((len(times) - 1 - n) * vecs + v, 16), :] = value.astype(BF16)
+        if times[-1]:
+            state[at, :] = carry
 
 
 def product(lhs, rhs):
     return lax.dot_general(lhs, rhs, (((1,), (1,)), ((), ())), preferred_element_type=F32)
 
 
-def own_kernel(sp_axis, coup, spec, basis, noise, message, out, lhs, rhs, *rest):
-    *coefs, sem = rest
+def halves_of(steps):
+    times = list(range(steps - 1, -1, -1))
+    return times[: steps // 2], times[steps // 2 :]
+
+
+def own_kernel(sp_axis, coup, spec, basis, noise, message, out, lhs, rhs, state, coefs, sem):
     rows = lhs.shape[0]
+    steps, vecs, _ = noise.shape
     start = pl.multiple_of(lax.axis_index(sp_axis) * rows, rows)
     copy = pltpu.make_async_copy(basis.at[pl.ds(start, rows), :], lhs, sem)
     copy.start()
-    values(noise, message, coup[...], spec[...], coefs, rhs)
+    set_coefs(coefs, coup[...], spec[...], sums_of(message[pl.ds(vecs, 16), :].astype(F32)))
+    late, early = halves_of(steps)
+    width = vecs * len(late)
+    values(noise, lambda at: message[at, :].astype(F32), coefs, state, rhs.at[0], late)
     copy.wait()
-    out[...] = product(lhs[...], rhs[...])
-
-
-def block_kernel(tm_axis, place, last, partial, direct, swapped, noise, message, out, lhs, rhs, tail, sems, *rest):
-    coefs = rest[:3]
+    values(noise, lambda at: state[at, :], coefs, state, rhs.at[1], early)
+    out[:, pl.ds(width, width)] = product(lhs[...], rhs[0])
+    out[:, pl.ds(0, width)] = product(lhs[...], rhs[1])
+
+
+def final_kernel(tm_axis, pairs, single, partial, *rest):
+    fetched = len(pairs) + len(single)
+    count = 2 * len(pairs) + len(single)
+    direct, rest = rest[:fetched], rest[fetched:]
+    swapped, rest = rest[:fetched], rest[fetched:]
+    noise, rest = rest[:count], rest[count:]
+    messages, rest = rest[:count], rest[count:]
+    out, lhs, rhs, state, coefs, result, sems = rest
+    steps, vecs, _ = noise[0].shape
     core = lax.rem(lax.axis_index(tm_axis), 2)
-    rows = direct.shape[0] - TAIL
-    if place is None:
-        head = pltpu.make_async_copy(direct.at[pl.ds(rows, TAIL), :], tail, sems.at[0])
-        head.start()
-        for j, source in enumerate((direct, swapped)):
+    first = core == 0
+    copies = []
+    for i in range(len(single)):
+        rows = lhs.shape[1] // 2
+        for j, source in enumerate((direct[i], swapped[i])):
             at = pl.multiple_of((core if j == 0 else 1 - core) * rows, rows)
-            pltpu.make_async_copy(source.at[pl.ds(0, rows), :], lhs.at[pl.ds(at, rows), :], sems.at[1 + j]).start()
-        head.wait()
-    else:
-        for j, source in enumerate((direct, swapped)):
-
-            @pl.when((core == place) == (j == 0))
-            def _():
-                pltpu.make_async_copy(source.at[pl.ds(rows, TAIL), :], tail, sems.at[0]).start()
-                pltpu.make_async_copy(source.at[pl.ds(0, rows), :], lhs, sems.at[1]).start()
-
-        pltpu.make_async_copy(direct.at[pl.ds(rows, TAIL), :], tail, sems.at[0]).wait()
-    x = [tail[pl.ds(16 * j, 16), :].astype(F32) for j in range(4)]
-    early = x[0][0:8] + x[0][8:16] + x[1][0:8]
-    late = x[1][8:16] + x[2][0:8] + x[2][8:16]
-    c = jnp.where(core == 0, early, late)
-    values(noise, message, c, x[3][0:1] + x[3][1:2] + x[3][2:3], coefs, rhs)
-    if place is None:
-        for j, source in enumerate((direct, swapped)):
-            at = pl.multiple_of((core if j == 0 else 1 - core) * rows, rows)
-            pltpu.make_async_copy(source.at[pl.ds(0, rows), :], lhs.at[pl.ds(at, rows), :], sems.at[1 + j]).wait()
-    else:
-        pltpu.make_async_copy(direct.at[pl.ds(0, rows), :], lhs, sems.at[1]).wait()
-    if not last:
-        out[...] = partial[...] + product(lhs[...], rhs[...])
-        return
-    result = rest[3]
-    copies = []
-    width = result.shape[2]
-    for i in range(result.shape[0]):
-        at = pl.ds(i * width, width)
-        result[i] = partial[:, at] + product(lhs[...], rhs[at, :])
-        copies.append(pltpu.make_async_copy(result.at[i], out.at[:, at], sems.at[3 + i]))
-        copies[-1].start()
-    for copy in copies:
+            copies.append(
+                pltpu.make_async_copy(
+                    source.at[pl.ds(0, rows), :], lhs.at[i, pl.ds(at, rows), :], sems.at[2 * i + j]
+                )
+            )
+            copies[-1].start()
+
+    def chosen(x, y):
+        return lambda at: jnp.where(first, messages[x][at, :].astype(F32), messages[y][at, :].astype(F32))
+
+    items = []
+    for j, (x, y) in enumerate(pairs):
+        i = len(single) + j
+        rows = direct[i].shape[0] - TAIL
+        near = lambda i=i, rows=rows: direct[i][pl.ds(0, rows), :]
+        far = lambda i=i, rows=rows: swapped[i][pl.ds(0, rows), :]
+        items.append((near, direct[i], noise[len(single) + j], chosen(x - 1, y - 1)))
+        items.append((far, swapped[i], noise[len(single) + len(pairs) + j], chosen(y - 1, x - 1)))
+    for i, d in enumerate(single):
+        items.append((lambda i=i: lhs[i], direct[i], noise[i], chosen(d - 1, d - 1)))
+    for n, (_, source, _, message) in enumerate(items):
+        rows = source.shape[0] - TAIL
+        x = [source[pl.ds(rows + 16 * j, 16), :].astype(F32) for j in range(4)]
+        before = x[0][0:8] + x[0][8:16] + x[1][0:8]
+        behind = x[1][8:16] + x[2][0:8] + x[2][8:16]
+        lam = x[3][0:1] + x[3][1:2] + x[3][2:3]
+        set_coefs(coefs.at[n], jnp.where(first, before, behind), lam, sums_of(message(pl.ds(vecs, 16))))
+    late, early = halves_of(steps)
+    width = vecs * len(late)
+    work = [(h, n) for h in range(2) for n in range(count)]
+
+    def fill(h, n):
+        start = items[n][3] if h == 0 else lambda at: state[n, at, :]
+        values(items[n][2], start, coefs.at[n], state.at[n], rhs.at[h, n], late if h == 0 else early)
+
+    fill(*work[0])
+    outs = []
+    for k, (h, n) in enumerate(work):
+        if k + 1 < len(work):
+            fill(*work[k + 1])
+        if h == 0 and n == count - len(single):
+            for copy in copies:
+                copy.wait()
+        term = product(items[n][0](), rhs[h, n])
+        at = pl.ds((1 - h) * width, width)
+        result[h] = (partial[:, at] if n == 0 else result[h]) + term
+        if n == count - 1:
+            outs.append(pltpu.make_async_copy(result.at[h], out.at[:, at], sems.at[2 * len(single) + h]))
+            outs[-1].start()
+    for copy in outs:
         copy.wait()
 
 
@@ -404,7 +441,7 @@
             **fast,
         )(keys, counters, *after)
 
-    own, paired = noise_of(((0, 0), (1, 0)), (table,))
+    own, paired = noise_of(((0, (0, 0)), (1, (0, 0))), (table,))
     total, late, weights, sums = kernel_call(
         functools.partial(offset_kernel, "tm"),
         out_shape=[bf16(vecs, modes), f32(vecs, modes), f32(chips, 8, modes), f32(8, modes)],
@@ -414,10 +451,8 @@
         **fast,
     )(own, paired, coup, other, spec, table, *tables)
     later = [swap(total, "tm", 2 * e) for e in range(1, chips)]
-    third = max(1, (space - 1) // 3)
-    parts = [range(1, 1 + third), range(1 + third, 1 + 2 * third), range(1 + 2 * third, space)]
-    noise = list(noise_of([(0, d) for d in parts[0]], (total,)))
-    noise += noise_of([(0, d) for d in parts[1]], (noise[-1],))
+    noise = noise_of([(0, (d, d)) for d in single], (total,))
+    noise += noise_of([(0, r) for r in pairs], (noise[-1],))
     carry = kernel_call(
         functools.partial(carry_kernel, "tm"),
         out_shape=bf16(vecs + 16, modes),
@@ -427,45 +462,45 @@
     )(late, weights, sums, *later, noise[-1])
     carries = [swap(carry, "space", d) for d in range(1, space)]
     swapped = [swap(m, "tm", 1) for m in direct]
-    noise += noise_of([(0, d) for d in parts[2]], (carry,))
+    noise += noise_of([(0, r[::-1]) for r in pairs], (carry,))
 
     flops = 2 * nodes_here * modes * steps * vecs
-    lhs, rhs = pltpu.VMEM((nodes_here, modes), BF16), pltpu.VMEM((steps * vecs, modes), BF16)
-    coefs = [pltpu.VMEM((steps, modes), F32)] * 3
+    half_cols = steps // 2 * vecs
     result = f32(nodes_here, steps * vecs)
-    cost = pl.CostEstimate(flops=flops, transcendentals=0, bytes_accessed=4 * steps * vecs * modes)
     out = kernel_call(
         functools.partial(own_kernel, "space"),
         out_shape=result,
         in_specs=[VMEM, VMEM, HBM, VMEM, VMEM],
         out_specs=VMEM,
-        scratch_shapes=[lhs, rhs] + coefs + [pltpu.SemaphoreType.DMA],
-        cost_estimate=cost,
+        scratch_shapes=[
+            pltpu.VMEM((nodes_here, modes), BF16),
+            pltpu.VMEM((2, half_cols, modes), BF16),
+            pltpu.VMEM((vecs, modes), F32),
+            pltpu.VMEM((3, steps, modes), F32),
+            pltpu.SemaphoreType.DMA,
+        ],
+        cost_estimate=pl.CostEstimate(flops=flops, transcendentals=0, bytes_accessed=4 * steps * vecs * modes),
         **fast,
     )(coup, spec, spatial_basis, own, carry)
-    width = 128
-    chunks = steps * vecs // width
-    order = [(d, 0, None) for d in single]
-    order += [(d, len(single) + j, place) for j, pair in enumerate(pairs) for place, d in enumerate(pair)]
-    for n, (d, i, place) in enumerate(order):
-        last = n == len(order) - 1
-        out = kernel_call(
-            functools.partial(block_kernel, "tm", place, last),
-            out_shape=result,
-            in_specs=[VMEM, ANY, ANY, VMEM, VMEM],
-            out_specs=HBM if last else VMEM,
-            scratch_shapes=[
-                lhs,
-                rhs,
-                pltpu.VMEM((TAIL, modes), BF16),
-                pltpu.SemaphoreType.DMA((3 + chunks if last else 3,)),
-            ]
-            + coefs
-            + ([pltpu.VMEM((chunks, nodes_here, width), F32)] if last else []),
-            cost_estimate=cost,
-            **fast,
-        )(out, direct[i], swapped[i], noise[d - 1], carries[d - 1])
-    return out
+    count = space - 1
+    return kernel_call(
+        functools.partial(final_kernel, "tm", pairs, single),
+        out_shape=result,
+        in_specs=[VMEM] * (1 + len(direct) + len(swapped) + len(noise) + len(carries)),
+        out_specs=HBM,
+        scratch_shapes=[
+            pltpu.VMEM((len(single), nodes_here, modes), BF16),
+            pltpu.VMEM((2, count, half_cols, modes), BF16),
+            pltpu.VMEM((count, vecs, modes), F32),
+            pltpu.VMEM((count, 3, steps, modes), F32),
+            pltpu.VMEM((2, nodes_here, half_cols), F32),
+            pltpu.SemaphoreType.DMA((2 * len(single) + 2,)),
+        ],
+        cost_estimate=pl.CostEstimate(
+            flops=flops * count, transcendentals=0, bytes_accessed=4 * steps * vecs * modes * count
+        ),
+        **fast,
+    )(out, *direct, *swapped, *noise, *carries)
 
 
 def solution(mesh):

time: 49.9 us -> 49.1 us (0.984)
  Pallas kernels: 15.2 us -> 14.2 us
    pallas_call x3 -> x1, Pallas kernels: 3.78 us -> 2.79 us  [local(): kernel_call(functools.partial(final_kernel, 'tm', pairs, single), out_sha...]
  transfers between devices with their start and end apart: 14 -> 14, of which waited for: 4 -> 7; matrix products, arithmetic and copies ran while one was open for 0% -> 0% of each run, Pallas kernels for 26% -> 23%
where the time goes in v5:
time: 49.1 us; the launch traced here: 49 us
  waiting for transfers between devices  17.6 us (36%)
  starting transfers between devices  17.1 us (35%)
  Pallas kernels  14.2 us (29%)
    ppermute x2, waiting for transfers between devices, exchange(): return lax.ppermute(x, ('tm', 'space'), moves)  14.9 us
    ppermute x12, starting transfers between devices, swap(): return lax.ppermute(x, axis, [(i, i ^ offset) for i in range(count)])  12.9 us
    pallas_call x4, Pallas kernels, noise_of(): kernel_call(functools.partial(noise_kernel, 'tm', 'space', blocks, len(af...  8.62 us
    ppermute x2, starting transfers between devices, exchange(): return lax.ppermute(x, ('tm', 'space'), moves)  4.21 us
    pallas_call x1, Pallas kernels, local(): kernel_call(functools.partial(final_kernel, 'tm', pairs, single), out_sha...  2.79 us
    ppermute x12, waiting for transfers between devices, swap(): return lax.ppermute(x, axis, [(i, i ^ offset) for i in range(count)])  2.69 us
    pallas_call x1, Pallas kernels, local(): kernel_call(functools.partial(pack_kernel, 'tm', 'space', routes), out_sh...  1.19 us
  transfers between devices with their start and end apart: 14, of which 7 were waited for; matrix products, arithmetic and copies ran while one was open for 0% of the time, Pallas kernels for 23%

profile of v5, /device:TPU:0, one launch (start us, length us, event | category | flops | bytes accessed | tf_op | source)
XLA Modules:
  0.0 49.0 jit_solution(10586697360423488539)
XLA Ops:
  0.0 0.5 %collective-permute-start = (f32[8,512]{1,0:T(8,128)}, f32[8,512]{1,0:T(8,128)S(1)}, u32[]{:S(2)}, u32[]{:S(2)}) collective-permute-start(f32[8,512]{1,0:T(8,128)} %coup.1), channel_id=1, source_target_pairs={{0,4},{4,0},{8,12},{12,8},{16,20},{20,16},{24,28},{28,24},{1,5},{5... | collective-permute-start | bytes 49160 | tf_op jit(solution)/shard_map/ppermute | solution.py:38
  0.5 1.2 %shard_map.55 = (bf16[320,512]{1,0:T(8,128)(2,1)S(1)}, bf16[576,512]{1,0:T(8,128)(2,1)S(1)}, f32[8,512]{1,0:T(8,128)S(1)}, f32[1,512]{1,0:T(1,128)S(1)}) custom-call(f32[8,512]{1,0:T(8,128)} %coup.1, f32[1,512]{1,0:T(1,128)} %bitcast.11, bf16[2048,512]{1,0:T(8,128)(2,1)} %basis.3), custom_call_target="tpu_custom_call" | custom-call | tf_op jit(solution)/shard_map/pallas_call | solution.py:412
  2.0 2.7 %collective-permute-start.8 = (bf16[576,512]{1,0:T(8,128)(2,1)S(1)}, bf16[576,512]{1,0:T(8,128)(2,1)S(1)}, u32[]{:S(2)}, u32[]{:S(2)}) collective-permute-start(bf16[576,512]{1,0:T(8,128)(2,1)S(1)} %get-tuple-element.30), channel_id=1, source_target_pairs={{0,1},{1,0},{2,3},{3,2},{4,6},{5,7},{6,4},{7,5},{8,9},{9,8},{10,11... | collective-permute-start | bytes 1769480 | tf_op jit(solution)/shard_map/ppermute | solution.py:33
  4.7 1.5 %collective-permute-start.7 = (bf16[320,512]{1,0:T(8,128)(2,1)S(1)}, bf16[320,512]{1,0:T(8,128)(2,1)S(1)}, u32[]{:S(2)}, u32[]{:S(2)}) collective-permute-start(bf16[320,512]{1,0:T(8,128)(2,1)S(1)} %get-tuple-element.29), channel_id=1, source_target_pairs={{0,3},{1,2},{2,1},{3,0},{4,7},{5,6},{6,5},{7,4},{8,11},{9,10},{10,... | collective-permute-start | bytes 983048 | tf_op jit(solution)/shard_map/ppermute | solution.py:33
  6.2 9.9 %collective-permute-done.8.rest_1_ = bf16[576,512]{1,0:T(8,128)(2,1)S(1)} collective-permute-done((bf16[576,512]{1,0:T(8,128)(2,1)S(1)}, bf16[576,512]{1,0:T(8,128)(2,1)S(1)}, u32[]{:S(2)}, u32[]{:S(2)}) %collective-permute-start.8) | collective-permute-done | bytes 589856 | tf_op jit(solution)/shard_map/ppermute | solution.py:33
  16.1 5.0 %collective-permute-done.7.rest_0_ = bf16[320,512]{1,0:T(8,128)(2,1)S(1)} collective-permute-done((bf16[320,512]{1,0:T(8,128)(2,1)S(1)}, bf16[320,512]{1,0:T(8,128)(2,1)S(1)}, u32[]{:S(2)}, u32[]{:S(2)}) %collective-permute-start.7) | collective-permute-done | bytes 327712 | tf_op jit(solution)/shard_map/ppermute | solution.py:33
  21.0 3.6 %collective-permute-start.3 = (f32[8,512]{1,0:T(8,128)S(1)}, f32[8,512]{1,0:T(8,128)S(1)}, u32[]{:S(2)}, u32[]{:S(2)}) collective-permute-start(f32[8,512]{1,0:T(8,128)S(1)} %get-tuple-element.22.rest_0_.table), channel_id=1, source_target_pairs={{0,24},{4,28},{8,16},{12,20},{16,8},{20,12},{24,0},{28,4},{1,25},{... | collective-permute-start | bytes 49160 | tf_op jit(solution)/shard_map/ppermute | solution.py:38
  24.7 0.8 %collective-permute-start.1 = (f32[8,512]{1,0:T(8,128)S(1)}, f32[8,512]{1,0:T(8,128)S(1)}, u32[]{:S(2)}, u32[]{:S(2)}) collective-permute-start(f32[8,512]{1,0:T(8,128)S(1)} %get-tuple-element.22.rest_0_.table), channel_id=1, source_target_pairs={{0,8},{4,12},{8,0},{12,4},{16,24},{20,28},{24,16},{28,20},{1,9},{5... | collective-permute-start | bytes 49160 | tf_op jit(solution)/shard_map/ppermute | solution.py:38
  25.4 3.4 %shard_map.57 = (f32[8,64,512]{2,1,0:T(8,128)S(1)}, f32[8,64,512]{2,1,0:T(8,128)S(1)}) custom-call(s32[1,64]{1,0:T(1,128)S(1)} %bitcast.3, s32[1,64]{1,0:T(1,128)S(1)} %bitcast.7, f32[8,512]{1,0:T(8,128)S(1)} %get-tuple-element.22.rest_0_.table), custom_call_target="tpu_custom_call" | custom-call | flops 31457280 | bytes 2097152 | tf_op jit(solution)/shard_map/pallas_call | solution.py:434
  28.8 0.4 collective-permute-done.2.rest_1_
  29.3 0.5 %shard_map.58 = (bf16[64,512]{1,0:T(8,128)(2,1)S(1)}, f32[64,512]{1,0:T(8,128)S(1)}, f32[4,8,512]{2,1,0:T(8,128)S(1)}, f32[8,512]{1,0:T(8,128)S(1)}) custom-call(f32[8,64,512]{2,1,0:T(8,128)S(1)} %get-tuple-element.23.noise_own.noise, f32[8,64,512]{2,1,0:T(8,128)S(1)} %get-tuple-element.24.noise_other, f32[8,512]{1,0:T(8,128)S(1)} %get-tuple-element.18.coup, ...), custom_call_target="tpu_custom_call" | custom-call | tf_op jit(solution)/shard_map/pallas_call | solution.py:445
  29.8 3.2 %collective-permute-start.6 = (bf16[64,512]{1,0:T(8,128)(2,1)S(1)}, bf16[64,512]{1,0:T(8,128)(2,1)S(1)}, u32[]{:S(2)}, u32[]{:S(2)}) collective-permute-start(bf16[64,512]{1,0:T(8,128)(2,1)S(1)} %get-tuple-element.28.rest_0_), channel_id=1, source_target_pairs={{0,24},{4,28},{8,16},{12,20},{16,8},{20,12},{24,0},{28,4},{1,25},{... | collective-permute-start | bytes 196616 | tf_op jit(solution)/shard_map/ppermute | solution.py:38
  33.1 1.2 %collective-permute-start.4 = (bf16[64,512]{1,0:T(8,128)(2,1)S(1)}, bf16[64,512]{1,0:T(8,128)(2,1)S(1)}, u32[]{:S(2)}, u32[]{:S(2)}) collective-permute-start(bf16[64,512]{1,0:T(8,128)(2,1)S(1)} %get-tuple-element.28.rest_0_), channel_id=1, source_target_pairs={{0,8},{4,12},{8,0},{12,4},{16,24},{20,28},{24,16},{28,20},{1,9},{5... | collective-permute-start | bytes 196616 | tf_op jit(solution)/shard_map/ppermute | solution.py:38
  34.3 1.7 %shard_map.59.rest_0_.rest_4_ = f32[8,64,512]{2,1,0:T(8,128)S(1)} custom-call(s32[1,64]{1,0:T(1,128)S(1)} %bitcast.4, s32[1,64]{1,0:T(1,128)S(1)} %bitcast.8, bf16[64,512]{1,0:T(8,128)(2,1)S(1)} %get-tuple-element.28.rest_0_), custom_call_target="tpu_custom_call" | custom-call | flops 15728640 | bytes 1048576 | tf_op jit(solution)/shard_map/pallas_call | solution.py:434
  36.0 1.7 %shard_map.60.rest_3_.rest_5_ = f32[8,64,512]{2,1,0:T(8,128)S(1)} custom-call(s32[1,64]{1,0:T(1,128)S(1)} %bitcast.5, s32[1,64]{1,0:T(1,128)S(1)} %bitcast.9, f32[8,64,512]{2,1,0:T(8,128)S(1)} %shard_map.59.rest_0_.rest_4_), custom_call_target="tpu_custom_call" | custom-call | flops 15728640 | bytes 1048576 | tf_op jit(solution)/shard_map/pallas_call | solution.py:434
  37.8 0.8 %collective-permute-done.5.rest_1_ = bf16[64,512]{1,0:T(8,128)(2,1)S(1)} collective-permute-done((bf16[64,512]{1,0:T(8,128)(2,1)S(1)}, bf16[64,512]{1,0:T(8,128)(2,1)S(1)}, u32[]{:S(2)}, u32[]{:S(2)}) %collective-permute-start.5) | collective-permute-done | bytes 65568 | tf_op jit(solution)/shard_map/ppermute | solution.py:38
  38.7 1.5 %collective-permute-start.13 = (bf16[80,512]{1,0:T(8,128)(2,1)S(1)}, bf16[80,512]{1,0:T(8,128)(2,1)S(1)}, u32[]{:S(2)}, u32[]{:S(2)}) collective-permute-start(bf16[80,512]{1,0:T(8,128)(2,1)S(1)} %shard_map.61.message.rest_0_), channel_id=1, source_target_pairs={{0,3},{1,2},{2,1},{3,0},{4,7},{5,6},{6,5},{7,4},{8,11},{9,10},{10,... | collective-permute-start | bytes 245768 | tf_op jit(solution)/shard_map/ppermute | solution.py:38
  40.2 1.5 %collective-permute-start.12 = (bf16[80,512]{1,0:T(8,128)(2,1)S(1)}, bf16[80,512]{1,0:T(8,128)(2,1)S(1)}, u32[]{:S(2)}, u32[]{:S(2)}) collective-permute-start(bf16[80,512]{1,0:T(8,128)(2,1)S(1)} %shard_map.61.message.rest_0_), channel_id=1, source_target_pairs={{0,2},{1,3},{2,0},{3,1},{4,6},{5,7},{6,4},{7,5},{8,10},{9,11},{10,... | collective-permute-start | bytes 245768 | tf_op jit(solution)/shard_map/ppermute | solution.py:38
  41.8 0.5 %collective-permute-start.11 = (bf16[80,512]{1,0:T(8,128)(2,1)S(1)}, bf16[80,512]{1,0:T(8,128)(2,1)S(1)}, u32[]{:S(2)}, u32[]{:S(2)}) collective-permute-start(bf16[80,512]{1,0:T(8,128)(2,1)S(1)} %shard_map.61.message.rest_0_), channel_id=1, source_target_pairs={{0,1},{1,0},{2,3},{3,2},{4,5},{5,4},{6,7},{7,6},{8,9},{9,8},{10,11... | collective-permute-start | bytes 245768 | tf_op jit(solution)/shard_map/ppermute | solution.py:38
  42.3 1.7 %shard_map.63.rest_6_ = f32[8,64,512]{2,1,0:T(8,128)S(1)} custom-call(s32[1,64]{1,0:T(1,128)S(1)} %bitcast.6, s32[1,64]{1,0:T(1,128)S(1)} %bitcast.10, bf16[80,512]{1,0:T(8,128)(2,1)S(1)} %shard_map.61.message.rest_0_), custom_call_target="tpu_custom_call" | custom-call | flops 15728640 | bytes 1048576 | tf_op jit(solution)/shard_map/pallas_call | solution.py:434
  44.0 0.8 %shard_map.62.partial = f32[512,512]{1,0:T(8,128)S(1)} custom-call(f32[8,512]{1,0:T(8,128)S(1)} %get-tuple-element.18.coup, f32[1,512]{1,0:T(1,128)S(1)} %get-tuple-element.19.spec, bf16[2048,512]{1,0:T(8,128)(2,1)S(1)} %copy-done, f32[8,64,512]{2,1,0:T(8,128)S(1)} %get-tuple-element.23.noise_own.noise, bf16[80,512]{1,0:T(8,128)(2,1)S(1)} %shard_map.61.message.rest_0_), custom_call_target="tpu_custom_call" | custom-call | flops 268435456 | bytes 1048576 | tf_op jit(solution)/shard_map/pallas_call | solution.py:470
  45.0 0.3 collective-permute-done.12.rest_8_
  45.4 0.8 %collective-permute-done.11.rest_7_ = bf16[80,512]{1,0:T(8,128)(2,1)S(1)} collective-permute-done((bf16[80,512]{1,0:T(8,128)(2,1)S(1)}, bf16[80,512]{1,0:T(8,128)(2,1)S(1)}, u32[]{:S(2)}, u32[]{:S(2)}) %collective-permute-start.11) | collective-permute-done | bytes 81952 | tf_op jit(solution)/shard_map/ppermute | solution.py:38
  46.2 2.8 %shard_map.64 = f32[512,512]{1,0:T(8,128)} custom-call(f32[512,512]{1,0:T(8,128)S(1)} %shard_map.62.partial, bf16[320,512]{1,0:T(8,128)(2,1)S(1)} %collective-permute-done.7.rest_0_, bf16[576,512]{1,0:T(8,128)(2,1)S(1)} %collective-permute-done.8.rest_1_, bf16[320,512]{1,0:T(8,128)(2,1)S(1)} %collective-permute-done.9.rest_2_, ...), custom_call_target="tpu_custom_call" | custom-call | flops 805306368 | bytes 3145728 | tf_op jit(solution)/shard_map/pallas_call | solution.py:486
  (20 shorter events, 0.6 us)
Async XLA Ops:
  0.0 25.4 %copy-start.2 = (s32[64]{0:T(128)S(1)}, s32[64]{0:T(128)}, u32[]{:S(2)}) copy-start(s32[64]{0:T(128)} %param.9) | copy-start | bytes 772
  0.0 25.4 %copy-start.1 = (s32[64]{0:T(128)S(1)}, s32[64]{0:T(128)}, u32[]{:S(2)}) copy-start(s32[64]{0:T(128)} %param.8) | copy-start | bytes 772
  0.0 1.7 %collective-permute-start = (f32[8,512]{1,0:T(8,128)}, f32[8,512]{1,0:T(8,128)S(1)}, u32[]{:S(2)}, u32[]{:S(2)}) collective-permute-start(f32[8,512]{1,0:T(8,128)} %coup.1), channel_id=1, source_target_pairs={{0,4},{4,0},{8,12},{12,8},{16,20},{20,16},{24,28},{28,24},{1,5},{5... | collective-permute-start | bytes 49160 | tf_op jit(solution)/shard_map/ppermute | solution.py:38
  2.0 14.1 %collective-permute-start.8 = (bf16[576,512]{1,0:T(8,128)(2,1)S(1)}, bf16[576,512]{1,0:T(8,128)(2,1)S(1)}, u32[]{:S(2)}, u32[]{:S(2)}) collective-permute-start(bf16[576,512]{1,0:T(8,128)(2,1)S(1)} %get-tuple-element.30), channel_id=1, source_target_pairs={{0,1},{1,0},{2,3},{3,2},{4,6},{5,7},{6,4},{7,5},{8,9},{9,8},{10,11... | collective-permute-start | bytes 1769480 | tf_op jit(solution)/shard_map/ppermute | solution.py:33
  4.7 16.4 %collective-permute-start.7 = (bf16[320,512]{1,0:T(8,128)(2,1)S(1)}, bf16[320,512]{1,0:T(8,128)(2,1)S(1)}, u32[]{:S(2)}, u32[]{:S(2)}) collective-permute-start(bf16[320,512]{1,0:T(8,128)(2,1)S(1)} %get-tuple-element.29), channel_id=1, source_target_pairs={{0,3},{1,2},{2,1},{3,0},{4,7},{5,6},{6,5},{7,4},{8,11},{9,10},{10,... | collective-permute-start | bytes 983048 | tf_op jit(solution)/shard_map/ppermute | solution.py:33
  16.0 30.2 %collective-permute-start.10 = (bf16[576,512]{1,0:T(8,128)(2,1)S(1)}, bf16[576,512]{1,0:T(8,128)(2,1)S(1)}, u32[]{:S(2)}, u32[]{:S(2)}) collective-permute-start(bf16[576,512]{1,0:T(8,128)(2,1)S(1)} %collective-permute-done.8.rest_1_), channel_id=1, source_target_pairs={{0,4},{4,0},{8,12},{12,8},{16,20},{20,16},{24,28},{28,24},{1,5},{5... | collective-permute-start | bytes 1769480 | tf_op jit(solution)/shard_map/ppermute | solution.py:38
  21.0 25.2 %collective-permute-start.9 = (bf16[320,512]{1,0:T(8,128)(2,1)S(1)}, bf16[320,512]{1,0:T(8,128)(2,1)S(1)}, u32[]{:S(2)}, u32[]{:S(2)}) collective-permute-start(bf16[320,512]{1,0:T(8,128)(2,1)S(1)} %collective-permute-done.7.rest_0_), channel_id=1, source_target_pairs={{0,4},{4,0},{8,12},{12,8},{16,20},{20,16},{24,28},{28,24},{1,5},{5... | collective-permute-start | bytes 983048 | tf_op jit(solution)/shard_map/ppermute | solution.py:38
  21.0 7.8 %collective-permute-start.3 = (f32[8,512]{1,0:T(8,128)S(1)}, f32[8,512]{1,0:T(8,128)S(1)}, u32[]{:S(2)}, u32[]{:S(2)}) collective-permute-start(f32[8,512]{1,0:T(8,128)S(1)} %get-tuple-element.22.rest_0_.table), channel_id=1, source_target_pairs={{0,24},{4,28},{8,16},{12,20},{16,8},{20,12},{24,0},{28,4},{1,25},{... | collective-permute-start | bytes 49160 | tf_op jit(solution)/shard_map/ppermute | solution.py:38
  24.7 4.6 %collective-permute-start.2 = (f32[8,512]{1,0:T(8,128)S(1)}, f32[8,512]{1,0:T(8,128)S(1)}, u32[]{:S(2)}, u32[]{:S(2)}) collective-permute-start(f32[8,512]{1,0:T(8,128)S(1)} %get-tuple-element.22.rest_0_.table), channel_id=1, source_target_pairs={{0,16},{4,20},{8,24},{12,28},{16,0},{20,4},{24,8},{28,12},{1,17},{... | collective-permute-start | bytes 49160 | tf_op jit(solution)/shard_map/ppermute | solution.py:38
  24.7 4.6 %collective-permute-start.1 = (f32[8,512]{1,0:T(8,128)S(1)}, f32[8,512]{1,0:T(8,128)S(1)}, u32[]{:S(2)}, u32[]{:S(2)}) collective-permute-start(f32[8,512]{1,0:T(8,128)S(1)} %get-tuple-element.22.rest_0_.table), channel_id=1, source_target_pairs={{0,8},{4,12},{8,0},{12,4},{16,24},{20,28},{24,16},{28,20},{1,9},{5... | collective-permute-start | bytes 49160 | tf_op jit(solution)/shard_map/ppermute | solution.py:38
  29.8 8.0 %collective-permute-start.6 = (bf16[64,512]{1,0:T(8,128)(2,1)S(1)}, bf16[64,512]{1,0:T(8,128)(2,1)S(1)}, u32[]{:S(2)}, u32[]{:S(2)}) collective-permute-start(bf16[64,512]{1,0:T(8,128)(2,1)S(1)} %get-tuple-element.28.rest_0_), channel_id=1, source_target_pairs={{0,24},{4,28},{8,16},{12,20},{16,8},{20,12},{24,0},{28,4},{1,25},{... | collective-permute-start | bytes 196616 | tf_op jit(solution)/shard_map/ppermute | solution.py:38
  33.1 5.5 %collective-permute-start.5 = (bf16[64,512]{1,0:T(8,128)(2,1)S(1)}, bf16[64,512]{1,0:T(8,128)(2,1)S(1)}, u32[]{:S(2)}, u32[]{:S(2)}) collective-permute-start(bf16[64,512]{1,0:T(8,128)(2,1)S(1)} %get-tuple-element.28.rest_0_), channel_id=1, source_target_pairs={{0,16},{4,20},{8,24},{12,28},{16,0},{20,4},{24,8},{28,12},{1,17},{... | collective-permute-start | bytes 196616 | tf_op jit(solution)/shard_map/ppermute | solution.py:38
  33.1 5.6 %collective-permute-start.4 = (bf16[64,512]{1,0:T(8,128)(2,1)S(1)}, bf16[64,512]{1,0:T(8,128)(2,1)S(1)}, u32[]{:S(2)}, u32[]{:S(2)}) collective-permute-start(bf16[64,512]{1,0:T(8,128)(2,1)S(1)} %get-tuple-element.28.rest_0_), channel_id=1, source_target_pairs={{0,8},{4,12},{8,0},{12,4},{16,24},{20,28},{24,16},{28,20},{1,9},{5... | collective-permute-start | bytes 196616 | tf_op jit(solution)/shard_map/ppermute | solution.py:38
  36.0 8.0 %copy-start = (bf16[2048,512]{1,0:T(8,128)(2,1)S(1)}, bf16[2048,512]{1,0:T(8,128)(2,1)}, u32[]{:S(2)}) copy-start(bf16[2048,512]{1,0:T(8,128)(2,1)} %basis.3) | copy-start | bytes 6291460
  38.7 6.3 %collective-permute-start.13 = (bf16[80,512]{1,0:T(8,128)(2,1)S(1)}, bf16[80,512]{1,0:T(8,128)(2,1)S(1)}, u32[]{:S(2)}, u32[]{:S(2)}) collective-permute-start(bf16[80,512]{1,0:T(8,128)(2,1)S(1)} %shard_map.61.message.rest_0_), channel_id=1, source_target_pairs={{0,3},{1,2},{2,1},{3,0},{4,7},{5,6},{6,5},{7,4},{8,11},{9,10},{10,... | collective-permute-start | bytes 245768 | tf_op jit(solution)/shard_map/ppermute | solution.py:38
  40.2 5.1 %collective-permute-start.12 = (bf16[80,512]{1,0:T(8,128)(2,1)S(1)}, bf16[80,512]{1,0:T(8,128)(2,1)S(1)}, u32[]{:S(2)}, u32[]{:S(2)}) collective-permute-start(bf16[80,512]{1,0:T(8,128)(2,1)S(1)} %shard_map.61.message.rest_0_), channel_id=1, source_target_pairs={{0,2},{1,3},{2,0},{3,1},{4,6},{5,7},{6,4},{7,5},{8,10},{9,11},{10,... | collective-permute-start | bytes 245768 | tf_op jit(solution)/shard_map/ppermute | solution.py:38
  41.8 4.4 %collective-permute-start.11 = (bf16[80,512]{1,0:T(8,128)(2,1)S(1)}, bf16[80,512]{1,0:T(8,128)(2,1)S(1)}, u32[]{:S(2)}, u32[]{:S(2)}) collective-permute-start(bf16[80,512]{1,0:T(8,128)(2,1)S(1)} %shard_map.61.message.rest_0_), channel_id=1, source_target_pairs={{0,1},{1,0},{2,3},{3,2},{4,5},{5,4},{6,7},{7,6},{8,9},{9,8},{10,11... | collective-permute-start | bytes 245768 | tf_op jit(solution)/shard_map/ppermute | solution.py:38

commit v6 on v5

--- a/solution.py
+++ b/solution.py
@@ -429,17 +429,20 @@
     tables = [swap(table, "tm", 2 * e) for e in range(1, chips)]
     direct = [exchange(m, lambda t, s, r=r: (t, s ^ r[t % 2])) for m, r in zip(messages, routes)]
 
-    def noise_of(blocks, after):
+    def noise_of(blocks, after, through=()):
         count = len(blocks) * steps * vecs * modes
+        extras = len(after) + len(through)
         return kernel_call(
-            functools.partial(noise_kernel, "tm", "space", blocks, len(after)),
-            out_shape=[f32(steps, vecs, modes)] * len(blocks),
-            in_specs=[VMEM] * 2 + [ANY] * len(after),
-            out_specs=[VMEM] * len(blocks),
+            functools.partial(noise_kernel, "tm", "space", blocks, extras),
+            out_shape=[f32(steps, vecs, modes)] * len(blocks)
+            + [jax.ShapeDtypeStruct(x.shape, x.dtype) for x in through],
+            in_specs=[VMEM] * 2 + [ANY] * extras,
+            out_specs=[VMEM] * len(blocks) + [ANY] * len(through),
             scratch_shapes=[pltpu.VMEM((vecs, 128), jnp.int32)],
+            input_output_aliases={2 + len(after) + i: len(blocks) + i for i in range(len(through))},
             cost_estimate=pl.CostEstimate(flops=count * 60, transcendentals=count * 2, bytes_accessed=count * 4),
             **fast,
-        )(keys, counters, *after)
+        )(keys, counters, *after, *through)
 
     own, paired = noise_of(((0, (0, 0)), (1, (0, 0))), (table,))
     total, late, weights, sums = kernel_call(
@@ -451,7 +454,9 @@
         **fast,
     )(own, paired, coup, other, spec, table, *tables)
     later = [swap(total, "tm", 2 * e) for e in range(1, chips)]
-    noise = noise_of([(0, (d, d)) for d in single], (total,))
+    alone = len(single)
+    out = noise_of([(0, (d, d)) for d in single], (total,), direct[alone:])
+    noise, direct = list(out[:alone]), direct[:alone] + list(out[alone:])
     noise += noise_of([(0, r) for r in pairs], (noise[-1],))
     carry = kernel_call(
         functools.partial(carry_kernel, "tm"),

time: 49.1 us -> 41.3 us (0.84)
  waiting for transfers between devices: 17.6 us -> 9.71 us
    ppermute x2, waiting for transfers between devices: 14.9 us -> 4.28 us  [exchange(): return lax.ppermute(x, ('tm', 'space'), moves)]
    ppermute x12, waiting for transfers between devices: 2.69 us -> 5.43 us  [swap(): return lax.ppermute(x, axis, [(i, i ^ offset) for i in range(count)])]
  transfers between devices with their start and end apart: 14 -> 14, of which waited for: 7 -> 8; matrix products, arithmetic and copies ran while one was open for 0% -> 0% of each run, Pallas kernels for 23% -> 27%
where the time goes in v6:
time: 41.3 us; the launch traced here: 41.2 us
  starting transfers between devices  17.1 us (41%)
  Pallas kernels  14.2 us (34%)
  waiting for transfers between devices  9.71 us (24%)
    ppermute x12, starting transfers between devices, swap(): return lax.ppermute(x, axis, [(i, i ^ offset) for i in range(count)])  12.9 us
    pallas_call x4, Pallas kernels, noise_of(): kernel_call(functools.partial(noise_kernel, 'tm', 'space', blocks, extras...  8.62 us
    ppermute x12, waiting for transfers between devices, swap(): return lax.ppermute(x, axis, [(i, i ^ offset) for i in range(count)])  5.43 us
    ppermute x2, waiting for transfers between devices, exchange(): return lax.ppermute(x, ('tm', 'space'), moves)  4.28 us
    ppermute x2, starting transfers between devices, exchange(): return lax.ppermute(x, ('tm', 'space'), moves)  4.21 us
    pallas_call x1, Pallas kernels, local(): kernel_call(functools.partial(final_kernel, 'tm', pairs, single), out_sha...  2.82 us
    pallas_call x1, Pallas kernels, local(): kernel_call(functools.partial(pack_kernel, 'tm', 'space', routes), out_sh...  1.19 us
  transfers between devices with their start and end apart: 14, of which 8 were waited for; matrix products, arithmetic and copies ran while one was open for 0% of the time, Pallas kernels for 27%

profile of v6, /device:TPU:0, one launch (start us, length us, event | category | flops | bytes accessed | tf_op | source)
XLA Modules:
  0.0 41.2 jit_solution(7822896345936041223)
XLA Ops:
  0.0 0.5 %collective-permute-start = (f32[8,512]{1,0:T(8,128)}, f32[8,512]{1,0:T(8,128)S(1)}, u32[]{:S(2)}, u32[]{:S(2)}) collective-permute-start(f32[8,512]{1,0:T(8,128)} %coup.1), channel_id=1, source_target_pairs={{0,4},{4,0},{8,12},{12,8},{16,20},{20,16},{24,28},{28,24},{1,5},{5... | collective-permute-start | bytes 49160 | tf_op jit(solution)/shard_map/ppermute | solution.py:38
  0.5 1.2 %shard_map.55 = (bf16[320,512]{1,0:T(8,128)(2,1)S(1)}, bf16[576,512]{1,0:T(8,128)(2,1)S(1)}, f32[8,512]{1,0:T(8,128)S(1)}, f32[1,512]{1,0:T(1,128)S(1)}) custom-call(f32[8,512]{1,0:T(8,128)} %coup.1, f32[1,512]{1,0:T(1,128)} %bitcast.11, bf16[2048,512]{1,0:T(8,128)(2,1)} %basis.3), custom_call_target="tpu_custom_call" | custom-call | tf_op jit(solution)/shard_map/pallas_call | solution.py:412
  2.0 2.7 %collective-permute-start.7 = (bf16[576,512]{1,0:T(8,128)(2,1)S(1)}, bf16[576,512]{1,0:T(8,128)(2,1)S(1)}, u32[]{:S(2)}, u32[]{:S(2)}) collective-permute-start(bf16[576,512]{1,0:T(8,128)(2,1)S(1)} %get-tuple-element.31), channel_id=1, source_target_pairs={{0,1},{1,0},{2,3},{3,2},{4,6},{5,7},{6,4},{7,5},{8,9},{9,8},{10,11... | collective-permute-start | bytes 1769480 | tf_op jit(solution)/shard_map/ppermute | solution.py:33
  4.7 1.5 %collective-permute-start.8 = (bf16[320,512]{1,0:T(8,128)(2,1)S(1)}, bf16[320,512]{1,0:T(8,128)(2,1)S(1)}, u32[]{:S(2)}, u32[]{:S(2)}) collective-permute-start(bf16[320,512]{1,0:T(8,128)(2,1)S(1)} %get-tuple-element.33), channel_id=1, source_target_pairs={{0,3},{1,2},{2,1},{3,0},{4,7},{5,6},{6,5},{7,4},{8,11},{9,10},{10,... | collective-permute-start | bytes 983048 | tf_op jit(solution)/shard_map/ppermute | solution.py:33
  6.2 3.6 %collective-permute-start.3 = (f32[8,512]{1,0:T(8,128)S(1)}, f32[8,512]{1,0:T(8,128)S(1)}, u32[]{:S(2)}, u32[]{:S(2)}) collective-permute-start(f32[8,512]{1,0:T(8,128)S(1)} %get-tuple-element.24.rest_0_.table), channel_id=1, source_target_pairs={{0,24},{4,28},{8,16},{12,20},{16,8},{20,12},{24,0},{28,4},{1,25},{... | collective-permute-start | bytes 49160 | tf_op jit(solution)/shard_map/ppermute | solution.py:38
  9.8 0.8 %collective-permute-start.1 = (f32[8,512]{1,0:T(8,128)S(1)}, f32[8,512]{1,0:T(8,128)S(1)}, u32[]{:S(2)}, u32[]{:S(2)}) collective-permute-start(f32[8,512]{1,0:T(8,128)S(1)} %get-tuple-element.24.rest_0_.table), channel_id=1, source_target_pairs={{0,8},{4,12},{8,0},{12,4},{16,24},{20,28},{24,16},{28,20},{1,9},{5... | collective-permute-start | bytes 49160 | tf_op jit(solution)/shard_map/ppermute | solution.py:38
  10.6 3.4 %shard_map.57 = (f32[8,64,512]{2,1,0:T(8,128)S(1)}, f32[8,64,512]{2,1,0:T(8,128)S(1)}) custom-call(s32[1,64]{1,0:T(1,128)S(1)} %bitcast.3, s32[1,64]{1,0:T(1,128)S(1)} %bitcast.7, f32[8,512]{1,0:T(8,128)S(1)} %get-tuple-element.24.rest_0_.table), custom_call_target="tpu_custom_call" | custom-call | flops 31457280 | bytes 2097152 | tf_op jit(solution)/shard_map/pallas_call | solution.py:435
  14.0 0.4 %collective-permute-done.2.rest_1_ = f32[8,512]{1,0:T(8,128)S(1)} collective-permute-done((f32[8,512]{1,0:T(8,128)S(1)}, f32[8,512]{1,0:T(8,128)S(1)}, u32[]{:S(2)}, u32[]{:S(2)}) %collective-permute-start.2) | collective-permute-done | bytes 16416 | tf_op jit(solution)/shard_map/ppermute | solution.py:38
  14.4 0.5 %shard_map.58 = (bf16[64,512]{1,0:T(8,128)(2,1)S(1)}, f32[64,512]{1,0:T(8,128)S(1)}, f32[4,8,512]{2,1,0:T(8,128)S(1)}, f32[8,512]{1,0:T(8,128)S(1)}) custom-call(f32[8,64,512]{2,1,0:T(8,128)S(1)} %get-tuple-element.25.noise_own.noise, f32[8,64,512]{2,1,0:T(8,128)S(1)} %get-tuple-element.26.noise_other, f32[8,512]{1,0:T(8,128)S(1)} %get-tuple-element.20.coup, ...), custom_call_target="tpu_custom_call" | custom-call | tf_op jit(solution)/shard_map/pallas_call | solution.py:448
  14.9 1.1 %collective-permute-done.7.rest_1_ = bf16[576,512]{1,0:T(8,128)(2,1)S(1)} collective-permute-done((bf16[576,512]{1,0:T(8,128)(2,1)S(1)}, bf16[576,512]{1,0:T(8,128)(2,1)S(1)}, u32[]{:S(2)}, u32[]{:S(2)}) %collective-permute-start.7) | collective-permute-done | bytes 589856 | tf_op jit(solution)/shard_map/ppermute | solution.py:33
  16.0 1.7 %shard_map.59 = (f32[8,64,512]{2,1,0:T(8,128)S(1)}, bf16[576,512]{1,0:T(8,128)(2,1)S(1)}) custom-call(s32[1,64]{1,0:T(1,128)S(1)} %bitcast.4, s32[1,64]{1,0:T(1,128)S(1)} %bitcast.8, bf16[64,512]{1,0:T(8,128)(2,1)S(1)} %get-tuple-element.30.rest_0_, bf16[576,512]{1,0:T(8,128)(2,1)S(1)} %collective-permute-done.7.rest_1_), custom_call_target="tpu_custom_call", output_to_operand_aliasing={{1}: (3, {})} | custom-call | flops 15728640 | bytes 1048576 | tf_op jit(solution)/shard_map/pallas_call | solution.py:435
  17.9 3.2 %collective-permute-done.8.rest_0_ = bf16[320,512]{1,0:T(8,128)(2,1)S(1)} collective-permute-done((bf16[320,512]{1,0:T(8,128)(2,1)S(1)}, bf16[320,512]{1,0:T(8,128)(2,1)S(1)}, u32[]{:S(2)}, u32[]{:S(2)}) %collective-permute-start.8) | collective-permute-done | bytes 327712 | tf_op jit(solution)/shard_map/ppermute | solution.py:33
  21.0 3.6 %collective-permute-start.6 = (bf16[64,512]{1,0:T(8,128)(2,1)S(1)}, bf16[64,512]{1,0:T(8,128)(2,1)S(1)}, u32[]{:S(2)}, u32[]{:S(2)}) collective-permute-start(bf16[64,512]{1,0:T(8,128)(2,1)S(1)} %get-tuple-element.30.rest_0_), channel_id=1, source_target_pairs={{0,24},{4,28},{8,16},{12,20},{16,8},{20,12},{24,0},{28,4},{1,25},{... | collective-permute-start | bytes 196616 | tf_op jit(solution)/shard_map/ppermute | solution.py:38
  24.7 0.8 %collective-permute-start.4 = (bf16[64,512]{1,0:T(8,128)(2,1)S(1)}, bf16[64,512]{1,0:T(8,128)(2,1)S(1)}, u32[]{:S(2)}, u32[]{:S(2)}) collective-permute-start(bf16[64,512]{1,0:T(8,128)(2,1)S(1)} %get-tuple-element.30.rest_0_), channel_id=1, source_target_pairs={{0,8},{4,12},{8,0},{12,4},{16,24},{20,28},{24,16},{28,20},{1,9},{5... | collective-permute-start | bytes 196616 | tf_op jit(solution)/shard_map/ppermute | solution.py:38
  25.4 1.7 %shard_map.60.rest_3_.rest_5_ = f32[8,64,512]{2,1,0:T(8,128)S(1)} custom-call(s32[1,64]{1,0:T(1,128)S(1)} %bitcast.5, s32[1,64]{1,0:T(1,128)S(1)} %bitcast.9, f32[8,64,512]{2,1,0:T(8,128)S(1)} %get-tuple-element.32.rest_0_.rest_4_), custom_call_target="tpu_custom_call" | custom-call | flops 15728640 | bytes 1048576 | tf_op jit(solution)/shard_map/pallas_call | solution.py:435
  27.6 3.2 %collective-permute-done.5.rest_1_ = bf16[64,512]{1,0:T(8,128)(2,1)S(1)} collective-permute-done((bf16[64,512]{1,0:T(8,128)(2,1)S(1)}, bf16[64,512]{1,0:T(8,128)(2,1)S(1)}, u32[]{:S(2)}, u32[]{:S(2)}) %collective-permute-start.5) | collective-permute-done | bytes 65568 | tf_op jit(solution)/shard_map/ppermute | solution.py:38
  30.9 1.5 %collective-permute-start.13 = (bf16[80,512]{1,0:T(8,128)(2,1)S(1)}, bf16[80,512]{1,0:T(8,128)(2,1)S(1)}, u32[]{:S(2)}, u32[]{:S(2)}) collective-permute-start(bf16[80,512]{1,0:T(8,128)(2,1)S(1)} %shard_map.61.message.rest_0_), channel_id=1, source_target_pairs={{0,3},{1,2},{2,1},{3,0},{4,7},{5,6},{6,5},{7,4},{8,11},{9,10},{10,... | collective-permute-start | bytes 245768 | tf_op jit(solution)/shard_map/ppermute | solution.py:38
  32.4 1.5 %collective-permute-start.12 = (bf16[80,512]{1,0:T(8,128)(2,1)S(1)}, bf16[80,512]{1,0:T(8,128)(2,1)S(1)}, u32[]{:S(2)}, u32[]{:S(2)}) collective-permute-start(bf16[80,512]{1,0:T(8,128)(2,1)S(1)} %shard_map.61.message.rest_0_), channel_id=1, source_target_pairs={{0,2},{1,3},{2,0},{3,1},{4,6},{5,7},{6,4},{7,5},{8,10},{9,11},{10,... | collective-permute-start | bytes 245768 | tf_op jit(solution)/shard_map/ppermute | solution.py:38
  33.9 0.5 %collective-permute-start.11 = (bf16[80,512]{1,0:T(8,128)(2,1)S(1)}, bf16[80,512]{1,0:T(8,128)(2,1)S(1)}, u32[]{:S(2)}, u32[]{:S(2)}) collective-permute-start(bf16[80,512]{1,0:T(8,128)(2,1)S(1)} %shard_map.61.message.rest_0_), channel_id=1, source_target_pairs={{0,1},{1,0},{2,3},{3,2},{4,5},{5,4},{6,7},{7,6},{8,9},{9,8},{10,11... | collective-permute-start | bytes 245768 | tf_op jit(solution)/shard_map/ppermute | solution.py:38
  34.4 1.7 %shard_map.63.rest_6_ = f32[8,64,512]{2,1,0:T(8,128)S(1)} custom-call(s32[1,64]{1,0:T(1,128)S(1)} %bitcast.6, s32[1,64]{1,0:T(1,128)S(1)} %bitcast.10, bf16[80,512]{1,0:T(8,128)(2,1)S(1)} %shard_map.61.message.rest_0_), custom_call_target="tpu_custom_call" | custom-call | flops 15728640 | bytes 1048576 | tf_op jit(solution)/shard_map/pallas_call | solution.py:435
  36.2 0.8 %shard_map.62.partial = f32[512,512]{1,0:T(8,128)S(1)} custom-call(f32[8,512]{1,0:T(8,128)S(1)} %get-tuple-element.20.coup, f32[1,512]{1,0:T(1,128)S(1)} %get-tuple-element.21.spec, bf16[2048,512]{1,0:T(8,128)(2,1)S(1)} %copy-done, f32[8,64,512]{2,1,0:T(8,128)S(1)} %get-tuple-element.25.noise_own.noise, bf16[80,512]{1,0:T(8,128)(2,1)S(1)} %shard_map.61.message.rest_0_), custom_call_target="tpu_custom_call" | custom-call | flops 268435456 | bytes 1048576 | tf_op jit(solution)/shard_map/pallas_call | solution.py:475
  37.0 0.6 %collective-permute-done.12.rest_8_ = bf16[80,512]{1,0:T(8,128)(2,1)S(1)} collective-permute-done((bf16[80,512]{1,0:T(8,128)(2,1)S(1)}, bf16[80,512]{1,0:T(8,128)(2,1)S(1)}, u32[]{:S(2)}, u32[]{:S(2)}) %collective-permute-start.12) | collective-permute-done | bytes 81952 | tf_op jit(solution)/shard_map/ppermute | solution.py:38
  37.6 0.7 %collective-permute-done.11.rest_7_ = bf16[80,512]{1,0:T(8,128)(2,1)S(1)} collective-permute-done((bf16[80,512]{1,0:T(8,128)(2,1)S(1)}, bf16[80,512]{1,0:T(8,128)(2,1)S(1)}, u32[]{:S(2)}, u32[]{:S(2)}) %collective-permute-start.11) | collective-permute-done | bytes 81952 | tf_op jit(solution)/shard_map/ppermute | solution.py:38
  38.3 2.8 %shard_map.64 = f32[512,512]{1,0:T(8,128)} custom-call(f32[512,512]{1,0:T(8,128)S(1)} %shard_map.62.partial, bf16[320,512]{1,0:T(8,128)(2,1)S(1)} %collective-permute-done.8.rest_0_, bf16[576,512]{1,0:T(8,128)(2,1)S(1)} %get-tuple-element.34.rest_1_, bf16[320,512]{1,0:T(8,128)(2,1)S(1)} %collective-permute-done.9.rest_2_, ...), custom_call_target="tpu_custom_call" | custom-call | flops 805306368 | bytes 3145728 | tf_op jit(solution)/shard_map/pallas_call | solution.py:491
  (20 shorter events, 0.9 us)
Async XLA Ops:
  0.0 10.6 %copy-start.2 = (s32[64]{0:T(128)S(1)}, s32[64]{0:T(128)}, u32[]{:S(2)}) copy-start(s32[64]{0:T(128)} %param.9) | copy-start | bytes 772
  0.0 10.6 %copy-start.1 = (s32[64]{0:T(128)S(1)}, s32[64]{0:T(128)}, u32[]{:S(2)}) copy-start(s32[64]{0:T(128)} %param.8) | copy-start | bytes 772
  0.0 1.7 %collective-permute-start = (f32[8,512]{1,0:T(8,128)}, f32[8,512]{1,0:T(8,128)S(1)}, u32[]{:S(2)}, u32[]{:S(2)}) collective-permute-start(f32[8,512]{1,0:T(8,128)} %coup.1), channel_id=1, source_target_pairs={{0,4},{4,0},{8,12},{12,8},{16,20},{20,16},{24,28},{28,24},{1,5},{5... | collective-permute-start | bytes 49160 | tf_op jit(solution)/shard_map/ppermute | solution.py:38
  2.0 14.1 %collective-permute-start.7 = (bf16[576,512]{1,0:T(8,128)(2,1)S(1)}, bf16[576,512]{1,0:T(8,128)(2,1)S(1)}, u32[]{:S(2)}, u32[]{:S(2)}) collective-permute-start(bf16[576,512]{1,0:T(8,128)(2,1)S(1)} %get-tuple-element.31), channel_id=1, source_target_pairs={{0,1},{1,0},{2,3},{3,2},{4,6},{5,7},{6,4},{7,5},{8,9},{9,8},{10,11... | collective-permute-start | bytes 1769480 | tf_op jit(solution)/shard_map/ppermute | solution.py:33
  4.7 16.4 %collective-permute-start.8 = (bf16[320,512]{1,0:T(8,128)(2,1)S(1)}, bf16[320,512]{1,0:T(8,128)(2,1)S(1)}, u32[]{:S(2)}, u32[]{:S(2)}) collective-permute-start(bf16[320,512]{1,0:T(8,128)(2,1)S(1)} %get-tuple-element.33), channel_id=1, source_target_pairs={{0,3},{1,2},{2,1},{3,0},{4,7},{5,6},{6,5},{7,4},{8,11},{9,10},{10,... | collective-permute-start | bytes 983048 | tf_op jit(solution)/shard_map/ppermute | solution.py:33
  6.2 7.8 %collective-permute-start.3 = (f32[8,512]{1,0:T(8,128)S(1)}, f32[8,512]{1,0:T(8,128)S(1)}, u32[]{:S(2)}, u32[]{:S(2)}) collective-permute-start(f32[8,512]{1,0:T(8,128)S(1)} %get-tuple-element.24.rest_0_.table), channel_id=1, source_target_pairs={{0,24},{4,28},{8,16},{12,20},{16,8},{20,12},{24,0},{28,4},{1,25},{... | collective-permute-start | bytes 49160 | tf_op jit(solution)/shard_map/ppermute | solution.py:38
  9.8 4.6 %collective-permute-start.2 = (f32[8,512]{1,0:T(8,128)S(1)}, f32[8,512]{1,0:T(8,128)S(1)}, u32[]{:S(2)}, u32[]{:S(2)}) collective-permute-start(f32[8,512]{1,0:T(8,128)S(1)} %get-tuple-element.24.rest_0_.table), channel_id=1, source_target_pairs={{0,16},{4,20},{8,24},{12,28},{16,0},{20,4},{24,8},{28,12},{1,17},{... | collective-permute-start | bytes 49160 | tf_op jit(solution)/shard_map/ppermute | solution.py:38
  9.8 4.6 %collective-permute-start.1 = (f32[8,512]{1,0:T(8,128)S(1)}, f32[8,512]{1,0:T(8,128)S(1)}, u32[]{:S(2)}, u32[]{:S(2)}) collective-permute-start(f32[8,512]{1,0:T(8,128)S(1)} %get-tuple-element.24.rest_0_.table), channel_id=1, source_target_pairs={{0,8},{4,12},{8,0},{12,4},{16,24},{20,28},{24,16},{28,20},{1,9},{5... | collective-permute-start | bytes 49160 | tf_op jit(solution)/shard_map/ppermute | solution.py:38
  17.8 20.5 %collective-permute-start.10 = (bf16[576,512]{1,0:T(8,128)(2,1)S(1)}, bf16[576,512]{1,0:T(8,128)(2,1)S(1)}, u32[]{:S(2)}, u32[]{:S(2)}) collective-permute-start(bf16[576,512]{1,0:T(8,128)(2,1)S(1)} %get-tuple-element.34.rest_1_), channel_id=1, source_target_pairs={{0,4},{4,0},{8,12},{12,8},{16,20},{20,16},{24,28},{28,24},{1,5},{5... | collective-permute-start | bytes 1769480 | tf_op jit(solution)/shard_map/ppermute | solution.py:38
  21.0 15.9 %collective-permute-start.9 = (bf16[320,512]{1,0:T(8,128)(2,1)S(1)}, bf16[320,512]{1,0:T(8,128)(2,1)S(1)}, u32[]{:S(2)}, u32[]{:S(2)}) collective-permute-start(bf16[320,512]{1,0:T(8,128)(2,1)S(1)} %collective-permute-done.8.rest_0_), channel_id=1, source_target_pairs={{0,4},{4,0},{8,12},{12,8},{16,20},{20,16},{24,28},{28,24},{1,5},{5... | collective-permute-start | bytes 983048 | tf_op jit(solution)/shard_map/ppermute | solution.py:38
  21.0 6.6 %collective-permute-start.6 = (bf16[64,512]{1,0:T(8,128)(2,1)S(1)}, bf16[64,512]{1,0:T(8,128)(2,1)S(1)}, u32[]{:S(2)}, u32[]{:S(2)}) collective-permute-start(bf16[64,512]{1,0:T(8,128)(2,1)S(1)} %get-tuple-element.30.rest_0_), channel_id=1, source_target_pairs={{0,24},{4,28},{8,16},{12,20},{16,8},{20,12},{24,0},{28,4},{1,25},{... | collective-permute-start | bytes 196616 | tf_op jit(solution)/shard_map/ppermute | solution.py:38
  24.7 6.1 %collective-permute-start.5 = (bf16[64,512]{1,0:T(8,128)(2,1)S(1)}, bf16[64,512]{1,0:T(8,128)(2,1)S(1)}, u32[]{:S(2)}, u32[]{:S(2)}) collective-permute-start(bf16[64,512]{1,0:T(8,128)(2,1)S(1)} %get-tuple-element.30.rest_0_), channel_id=1, source_target_pairs={{0,16},{4,20},{8,24},{12,28},{16,0},{20,4},{24,8},{28,12},{1,17},{... | collective-permute-start | bytes 196616 | tf_op jit(solution)/shard_map/ppermute | solution.py:38
  24.7 6.1 %collective-permute-start.4 = (bf16[64,512]{1,0:T(8,128)(2,1)S(1)}, bf16[64,512]{1,0:T(8,128)(2,1)S(1)}, u32[]{:S(2)}, u32[]{:S(2)}) collective-permute-start(bf16[64,512]{1,0:T(8,128)(2,1)S(1)} %get-tuple-element.30.rest_0_), channel_id=1, source_target_pairs={{0,8},{4,12},{8,0},{12,4},{16,24},{20,28},{24,16},{28,20},{1,9},{5... | collective-permute-start | bytes 196616 | tf_op jit(solution)/shard_map/ppermute | solution.py:38
  25.4 10.7 %copy-start = (bf16[2048,512]{1,0:T(8,128)(2,1)S(1)}, bf16[2048,512]{1,0:T(8,128)(2,1)}, u32[]{:S(2)}) copy-start(bf16[2048,512]{1,0:T(8,128)(2,1)} %basis.3) | copy-start | bytes 6291460
  30.9 6.2 %collective-permute-start.13 = (bf16[80,512]{1,0:T(8,128)(2,1)S(1)}, bf16[80,512]{1,0:T(8,128)(2,1)S(1)}, u32[]{:S(2)}, u32[]{:S(2)}) collective-permute-start(bf16[80,512]{1,0:T(8,128)(2,1)S(1)} %shard_map.61.message.rest_0_), channel_id=1, source_target_pairs={{0,3},{1,2},{2,1},{3,0},{4,7},{5,6},{6,5},{7,4},{8,11},{9,10},{10,... | collective-permute-start | bytes 245768 | tf_op jit(solution)/shard_map/ppermute | solution.py:38
  32.4 5.2 %collective-permute-start.12 = (bf16[80,512]{1,0:T(8,128)(2,1)S(1)}, bf16[80,512]{1,0:T(8,128)(2,1)S(1)}, u32[]{:S(2)}, u32[]{:S(2)}) collective-permute-start(bf16[80,512]{1,0:T(8,128)(2,1)S(1)} %shard_map.61.message.rest_0_), channel_id=1, source_target_pairs={{0,2},{1,3},{2,0},{3,1},{4,6},{5,7},{6,4},{7,5},{8,10},{9,11},{10,... | collective-permute-start | bytes 245768 | tf_op jit(solution)/shard_map/ppermute | solution.py:38
  33.9 4.4 %collective-permute-start.11 = (bf16[80,512]{1,0:T(8,128)(2,1)S(1)}, bf16[80,512]{1,0:T(8,128)(2,1)S(1)}, u32[]{:S(2)}, u32[]{:S(2)}) collective-permute-start(bf16[80,512]{1,0:T(8,128)(2,1)S(1)} %shard_map.61.message.rest_0_), channel_id=1, source_target_pairs={{0,1},{1,0},{2,3},{3,2},{4,5},{5,4},{6,7},{7,6},{8,9},{9,8},{10,11... | collective-permute-start | bytes 245768 | tf_op jit(solution)/shard_map/ppermute | solution.py:38
